TPU v7x, 256 devices: a whole 4x4x8 slice. The times are simulated.
256 devices in a mesh: sta: 32 (over z, y), seg: 8 (over x, core).
Axes of the slice: x: 4, y: 4, z: 8, core: 2. Of those that a mesh axis runs over, the one named last changes fastest.
Arguments:
- records: bfloat16 [512, 16384], P('sta', 'seg'), may hold values from -300 to 300, as said below
- owners: int32 [256, 4], P('sta'), may hold values from 0 to 31, all different within a row; in each aligned block of 8 rows (0 to 7, 8 to 15, ...) at most 2 rows name the same one
Outputs:
- whitened: bfloat16 [512, 16384], P('sta', 'seg')
- correlations: bfloat16 [128, 512, 512], P('seg', 'sta')
Inputs may be any that keep to these rules, and one draw needn't show every extreme that they name: Each row names 4 different owners; among the 8 blocks of one index of sta no owner is named more than 2 times, some owner is named exactly 2 times, and every owner is named by some block. Real-valued records.
All inputs are finite; a program needn't handle non-finite values.
Results may differ from a plain program's by a relative error of at most 0.017.
Values may be sent and summed in bfloat16 or wider, within the bound.
No kernel may reach another device: no remote copies, remote signals or barrier semaphores. Data moves between devices by JAX's collectives and lax.ppermute only.
A program may use at most 128 MiB of HBM per device.

v0:
```python
import math

import jax
import jax.numpy as jnp
from jax import lax
from jax.sharding import PartitionSpec as P

LAGS = 512
P_SIZE = 128
BS = 2
DESTS = 4


WATER = 0.5
EPSILON = 1e-06


def padded(block, sides, width):
    for axis, dim in sides:
        count = lax.axis_size(axis)
        forward = [(i, i + 1) for i in range(count - 1)]
        backward = [(target, source) for source, target in forward]
        low = lax.ppermute(
            lax.slice_in_dim(block, block.shape[dim] - width, None, axis=dim), axis, forward
        )
        high = lax.ppermute(lax.slice_in_dim(block, 0, width, axis=dim), axis, backward)
        block = jnp.concatenate([low, block, high], axis=dim)
    return block


def make_table(length):
    sample_ids = jnp.arange(length, dtype=jnp.int32)
    product = sample_ids[:, None] * sample_ids[None, :] % length
    angles = product.astype(jnp.float32) * (2.0 * math.pi / length)
    return jnp.concatenate([jnp.cos(angles), jnp.sin(angles)], axis=1).astype(jnp.bfloat16)


def toeplitz_blocks(extended):
    own_count = extended.shape[0]
    blocks = extended.reshape(own_count, -1, P_SIZE)
    block_pairs = jnp.concatenate([blocks[:, :-1], blocks[:, 1:]], axis=2)
    pair_count = block_pairs.shape[1]
    padded_pairs = jnp.pad(block_pairs, ((0, 0), (0, 0), (0, 1)))
    spread = jnp.broadcast_to(
        padded_pairs[:, :, None, :], (own_count, pair_count, P_SIZE, 2 * P_SIZE + 1)
    )
    spread = spread.reshape(own_count, pair_count, P_SIZE * (2 * P_SIZE + 1))[
        :, :, : P_SIZE * 2 * P_SIZE
    ]
    spread = spread.reshape(own_count, pair_count, P_SIZE, 2 * P_SIZE)
    return spread[:, :, :, P_SIZE:]


def on_device(records, owners):
    own_count, seg_len = records.shape
    seg_count = lax.axis_size("seg")
    window = seg_len * seg_count
    dft_table = make_table(seg_len)
    spectrum = jnp.dot(records, dft_table, preferred_element_type=jnp.float32)
    real_part = spectrum[:, :seg_len]
    imag_part = spectrum[:, seg_len:]
    magnitude = jnp.sqrt(real_part * real_part + imag_part * imag_part)
    amp_total = lax.psum(jnp.sum(magnitude, axis=1), "seg")
    water_level = WATER * amp_total / window + EPSILON
    flattened = (
        spectrum / (jnp.concatenate([magnitude, magnitude], axis=1) + water_level[:, None])
    ).astype(jnp.bfloat16)
    white_trace = lax.dot_general(
        flattened, dft_table, (((1,), (1,)), ((), ())), preferred_element_type=jnp.float32
    ) * (1.0 / seg_len)
    energy = lax.psum(jnp.sum(white_trace * white_trace, axis=1), "seg")
    whitened = (white_trace * lax.rsqrt(energy / window + EPSILON)[:, None]).astype(jnp.bfloat16)
    half_lags = LAGS // 2
    extended = padded(whitened, (("seg", 1),), half_lags)
    lagged = toeplitz_blocks(extended)
    pair_count = lagged.shape[1]
    sources = lax.axis_size("sta")
    block_count = own_count // BS
    slot_count = max(2, 2 * block_count * DESTS // sources)
    slot_ids = jnp.arange(slot_count, dtype=jnp.int32)
    everyone, all_owners = (
        lax.all_gather(whitened, "sta", axis=0, tiled=True),
        lax.all_gather(owners, "sta", axis=0, tiled=True),
    )
    my_index = lax.axis_index("sta")
    wanted = jnp.any(all_owners == my_index, axis=1).reshape(sources, block_count)
    wanted_count = wanted.astype(jnp.int32)
    slot_rank = jnp.cumsum(wanted_count, axis=1) - wanted_count
    selector = (wanted[:, None, :] & (slot_rank[:, None, :] == slot_ids[None, :, None])).astype(
        jnp.bfloat16
    )
    block_data = everyone.reshape(sources, block_count, BS * seg_len)
    received = (
        jnp.einsum("sqj,sjx->sqx", selector, block_data, preferred_element_type=jnp.float32)
        .astype(jnp.bfloat16)
        .reshape(-1, seg_len)
    )
    recv_rows = received.shape[0]
    shift_count = LAGS // P_SIZE
    seg_blocks = received.reshape(recv_rows, seg_len // P_SIZE, P_SIZE)
    padded_rows = jnp.pad(seg_blocks, ((0, 0), (shift_count - 1, shift_count - 1), (0, 0)))
    shifted = jnp.stack(
        [padded_rows[:, offset : offset + pair_count] for offset in range(shift_count)], axis=1
    )
    corr_scale = 1.0 / math.sqrt(window)
    product = jnp.einsum("ajui,bsji->basu", lagged, shifted, preferred_element_type=jnp.float32)
    stacked = lax.psum_scatter(
        (
            product.reshape(recv_rows // seg_count * lax.axis_size("seg"), own_count, LAGS)
            * corr_scale
        ).astype(jnp.bfloat16),
        "seg",
        scatter_dimension=0,
        tiled=True,
    )
    return (whitened, stacked)


def solution(mesh):
    return jax.shard_map(
        on_device,
        mesh=mesh,
        in_specs=(P("sta", "seg"), P("sta", None)),
        out_specs=(P("sta", "seg"), P("seg", "sta", None)),
        check_vma=False,
    )
```

profile of v0, /device:TPU:1, one launch (start us, length us, event | category | flops | bytes accessed | tf_op | source)
XLA Modules:
  0.0 297.4 jit_solution(4871632744596903862)
XLA Ops:
  7.2 66.7 %sine_convert_fusion = (bf16[2048,2048]{1,0:T(8,128)(2,1)S(1)}, bf16[2048,2048]{1,0:T(8,128)(2,1)S(1)}) fusion(), kind=kLoop, calls=%fused_computation.7 | loop fusion | flops 67108864 | bytes 16777216 | tf_op jit(solution)/shard_map/convert.1
  74.0 2.3 fusion.9
  76.3 0.9 copy-done.2
  77.2 2.5 copy-done.3
  79.8 15.0 %psum.14 = f32[16]{0:T(128)S(1)} all-reduce(f32[16]{0:T(128)S(1)} %get-tuple-element.4), channel_id=1, replica_groups=mesh['sta'=32,'seg'=8] {'seg'}, use_global_device_ids=true, to_apply=%region_1.2 | all-reduce | flops 16 | bytes 128 | tf_op jit(solution)/shard_map/psum | solution.py:63
  94.9 8.3 %multiply_reduce_fusion = (f32[16]{0:T(128)S(1)}, f32[16,2048]{1,0:T(8,128)S(1)}) fusion(bf16[2048,2048]{1,0:T(8,128)(2,1)} %copy-done.2, bf16[2048,2048]{1,0:T(8,128)(2,1)} %copy-done.3, f32[16,4096]{1,0:T(8,128)S(1)} %fusion.9, f32[16,2048]{1,0:T(8,128)S(1)} %get-tuple-element.5, f32[16]{0:T(128)S(1)} %multiply_add_fusion), kind=kOutput, calls=%fused_computation.45 | convolution fusion | flops 302350336 | bytes 17301632 | tf_op jit(solution)/shard_map/dot_general | solution.py:68
  103.1 12.9 %psum.15 = f32[16]{0:T(128)S(1)} all-reduce(f32[16]{0:T(128)S(1)} %get-tuple-element.14), channel_id=1, replica_groups=mesh['sta'=32,'seg'=8] {'seg'}, use_global_device_ids=true, to_apply=%region_3.4 | all-reduce | flops 16 | bytes 128 | tf_op jit(solution)/shard_map/psum | solution.py:71
  116.0 0.7 multiply_convert_fusion
  116.8 0.7 fusion.40
  117.5 1.9 collective-permute-start
  119.4 2.4 collective-permute-start.1
  121.9 40.7 %all-gather = s32[32,8,4]{1,2,0:T(4,128)S(1)} all-gather(s32[1,8,4]{1,2,0:T(4,128)S(1)} %bitcast.48), channel_id=1, replica_groups=mesh['sta'=32,'seg'=8] {'sta'}, dimensions={0}, use_global_device_ids=true | all-gather | bytes 4224 | tf_op jit(solution)/shard_map/all_gather | solution.py:83
  162.8 0.8 pad_maximum_fusion.6
  163.9 10.1 %broadcast_in_dim.2 = bf16[16,19,128,257]{3,2,0,1:T(8,128)(2,1)} broadcast(bf16[16,19,257]{2,0,1:T(8,128)(2,1)S(1)} %pad.9.clone), dimensions={0,1,3} | broadcast | bytes 20157024 | tf_op jit(solution)/shard_map/broadcast_in_dim | solution.py:44
  173.9 45.8 %reshape.43 = bf16[16,19,32896]{2,0,1:T(8,128)(2,1)} reshape(bf16[16,19,128,257]{3,2,0,1:T(8,128)(2,1)} %broadcast_in_dim.2) | data formatting | bytes 40001536 | tf_op jit(solution)/shard_map/reshape | solution.py:47
  219.7 6.7 %slice-done = bf16[16,19,32768]{2,0,1:T(8,128)(2,1)S(1)} async-done(((bf16[16,19,32896]{2,0,1:T(8,128)(2,1)}), bf16[16,19,32768]{2,0,1:T(8,128)(2,1)S(1)}, s32[]{:S(2)}) %slice-start) | async-done | bytes 19922968 | tf_op jit(solution)/shard_map/slice | solution.py:47
  226.4 7.2 %copy.19 = bf16[38,8,128,256]{3,2,1,0:T(8,128)(2,1)} copy(bf16[38,8,128,256]{3,1,2,0:T(8,128)(2,1)S(1)} %bitcast.45) | data formatting | bytes 39845888
  233.6 2.7 reshape.41
  236.2 0.7 convolution_convert_fusion
  236.9 0.4 reshape_reshape.3
  237.5 0.6 fusion.18
  238.1 8.3 %fusion.17 = bf16[128,16,4,128]{0,3,1,2:T(8,128)(2,1)S(1)} fusion(bf16[128,1,19,128]{3,0,2,1:T(8,128)(2,1)S(1)} %get-tuple-element.9, bf16[128,1,19,128]{3,0,2,1:T(8,128)(2,1)S(1)} %get-tuple-element.8, bf16[128,1,19,128]{3,0,2,1:T(8,128)(2,1)S(1)} %get-tuple-element.7, bf16[128,1,19,128]{3,0,2,1:T(8,128)(2,1)S(1)} %get-tuple-element.6, ...), kind=kOutput, calls=%fused_computation.27 | convolution fusion | flops 5112332288 | bytes 14548992 | tf_op jit(solution)/shard_map/ajui,bsji->basu/dot_general | solution.py:106
  246.6 3.0 %copy.14 = bf16[128,16,512]{2,1,0:T(8,128)(2,1)} copy(bf16[128,16,512]{0,2,1:T(8,128)(2,1)S(1)} %bitcast.47) | data formatting | bytes 4194304 | tf_op jit(solution)/shard_map/convert_element_type | solution.py:111
  249.7 40.8 %reduce-scatter.2.cloned.1.call-done = bf16[16,16,512]{2,1,0:T(8,128)(2,1)} async-done(((bf16[128,16,512]{2,1,0:T(8,128)(2,1)}), bf16[16,16,512]{2,1,0:T(8,128)(2,1)}) %reduce-scatter.2.cloned.1.call-update) | async-done | bytes 262160 | tf_op jit(solution)/shard_map/reduce_scatter | solution.py:107
  (30 shorter events, 1.0 us)
Async XLA Ops:
  7.2 66.8 %copy-start = (bf16[16,2048]{1,0:T(8,128)(2,1)S(1)}, bf16[16,2048]{1,0:T(8,128)(2,1)}, u32[]{:S(2)}) copy-start(bf16[16,2048]{1,0:T(8,128)(2,1)} %param.2) | copy-start | bytes 196612
  7.2 226.4 %all-gather.3.cloned.1.call-start = ((), (), s32[]{:S(2)}) async-start(), calls=%async_computation.1 | async-start | bytes 2162688 | tf_op jit(solution)/shard_map/all_gather | solution.py:82
  74.0 3.2 %copy-start.2 = (bf16[2048,2048]{1,0:T(8,128)(2,1)}, bf16[2048,2048]{1,0:T(8,128)(2,1)S(1)}, u32[]{:S(2)}) copy-start(bf16[2048,2048]{1,0:T(8,128)(2,1)S(1)} %get-tuple-element.16) | copy-start | bytes 25165828
  74.0 5.7 %copy-start.3 = (bf16[2048,2048]{1,0:T(8,128)(2,1)}, bf16[2048,2048]{1,0:T(8,128)(2,1)S(1)}, u32[]{:S(2)}) copy-start(bf16[2048,2048]{1,0:T(8,128)(2,1)S(1)} %get-tuple-element.17) | copy-start | bytes 25165828
  94.9 27.0 %copy-start.4 = (s32[8,4]{0,1:T(4,128)S(1)}, s32[8,4]{0,1:T(4,128)}, u32[]{:S(2)}) copy-start(s32[8,4]{0,1:T(4,128)} %param.3) | copy-start | bytes 388
  116.7 173.8 %reduce-scatter.2.cloned.1.call-start = ((), (), s32[]{:S(2)}) async-start(), calls=%async_computation.2 | async-start | bytes 2359296 | tf_op jit(solution)/shard_map/reduce_scatter | solution.py:107
  117.5 45.3 %collective-permute-start = (bf16[16,256]{1,0:T(8,128)(2,1)S(1)}, bf16[16,256]{1,0:T(8,128)(2,1)S(1)}, u32[]{:S(2)}, u32[]{:S(2)}) collective-permute-start(bf16[16,256]{1,0:T(8,128)(2,1)S(1)} %get-tuple-element.12), channel_id=1, source_target_pairs={{0,1},{1,2},{2,3},{3,4},{4,5},{5,6},{6,7},{8,9},{9,10},{10,11},{11... | collective-permute-start | bytes 24584 | tf_op jit(solution)/shard_map/ppermute | solution.py:23
  119.4 43.3 %collective-permute-start.1 = (bf16[16,256]{1,0:T(8,128)(2,1)S(1)}, bf16[16,256]{1,0:T(8,128)(2,1)S(1)}, u32[]{:S(2)}, u32[]{:S(2)}) collective-permute-start(bf16[16,256]{1,0:T(8,128)(2,1)S(1)} %get-tuple-element.13), channel_id=1, source_target_pairs={{1,0},{2,1},{3,2},{4,3},{5,4},{6,5},{7,6},{9,8},{10,9},{11,10},{12... | collective-permute-start | bytes 24584 | tf_op jit(solution)/shard_map/ppermute | solution.py:26
  219.7 6.7 %slice-start = ((bf16[16,19,32896]{2,0,1:T(8,128)(2,1)}), bf16[16,19,32768]{2,0,1:T(8,128)(2,1)S(1)}, s32[]{:S(2)}) async-start(bf16[16,19,32896]{2,0,1:T(8,128)(2,1)} %reshape.43), calls=%async_computation.3 | async-start | bytes 39845888 | tf_op jit(solution)/shard_map/slice | solution.py:47
  238.1 52.4 %copy-start.1 = (bf16[16,2048]{1,0:T(8,128)(2,1)S(1)}, bf16[16,2048]{1,0:T(8,128)(2,1)}, u32[]{:S(2)}) copy-start(bf16[16,2048]{1,0:T(8,128)(2,1)} %param.2) | copy-start | bytes 196612
Sparse Core Ops, SparseCore 0:
  116.9 74.5 all-gather.2
  249.8 40.6 reduce-scatter.1
where the time goes:
time: 301 us; the launch traced here: 297 us
  local copies, waits for them, and re-layouts  81 us (27%)
  other arithmetic  68.7 us (23%)
  blocking collectives  68.6 us (23%)
  waiting for transfers between devices  40.9 us (14%)
  matrix products  19.6 us (7%)
  between operations  14.2 us (5%)
  starting transfers between devices  4.39 us (1%)
    another operation x1, other arithmetic  66.7 us
    reshape x1, local copies, waits for them, and re-layouts, toeplitz_blocks(): spread.reshape(own_count, pair_count, P_SIZE * (2 * P_SIZE + 1))  45.8 us
    reduce_scatter x1, waiting for transfers between devices, on_device(): lax.psum_scatter((product.reshape(recv_rows // seg_count * lax.axis_size(...  40.8 us
    all_gather x1, blocking collectives, on_device(): lax.all_gather(owners, 'sta', axis=0, tiled=True)  40.7 us
    psum x1, blocking collectives, on_device(): amp_total = lax.psum(jnp.sum(magnitude, axis=1), 'seg')  15 us
    psum x1, blocking collectives, on_device(): energy = lax.psum(jnp.sum(white_trace * white_trace, axis=1), 'seg')  12.9 us
    unnamed x12, local copies, waits for them, and re-layouts  10.6 us
    broadcast_in_dim x1, local copies, waits for them, and re-layouts, toeplitz_blocks(): jnp.broadcast_to(padded_pairs[:, :, None, :], (own_count, pair_count, P_S...  10.1 us
  transfers between devices with their start and end apart: 4, of which 1 were waited for; matrix products, arithmetic and copies ran while one was open for 22% of the time, Pallas kernels for 0%

commit v1 on v0

v1 whole, which is shorter than its diff:
```python
import math

import jax
import jax.numpy as jnp
from jax import lax
from jax.experimental import pallas as pl
from jax.experimental.pallas import tpu as pltpu
from jax.sharding import PartitionSpec as P

LAGS = 512
BS = 2
SLOTS = 2
WATER = 0.5
EPSILON = 1e-06

PH = 16
STEP = 16
F32 = jnp.float32
BF16 = jnp.bfloat16
MIB = 1 << 20


def dot(a, b):
    return lax.dot_general(a, b, (((1,), (0,)), ((), ())), preferred_element_type=F32)


def dot_t(a, b):
    return lax.dot_general(a, b, (((1,), (1,)), ((), ())), preferred_element_type=F32)


def cos_sin(phase, period):
    phase = phase & (period - 1)
    phase = jnp.where(phase >= period // 2, phase - period, phase)
    theta = phase.astype(F32) * (2.0 * math.pi / period)
    square = theta * theta
    cosine = jnp.full(theta.shape, 1.0 / math.factorial(20), F32)
    sine = jnp.full(theta.shape, 1.0 / math.factorial(21), F32)
    for n in range(9, -1, -1):
        cosine = (1.0 if n % 2 == 0 else -1.0) / math.factorial(2 * n) + square * cosine
        sine = (1.0 if n % 2 == 0 else -1.0) / math.factorial(2 * n + 1) + square * sine
    return cosine, sine * theta


def table_kernel(length, forward_ref, inverse_ref):
    half = length // 2
    per_phase = length // PH
    wide = 256

    def columns(ref, col, freq_in_rows, rows, cos_at, sin_at, transform):
        lane = lax.broadcasted_iota(jnp.int32, (STEP, wide), 1) + col
        row = lax.broadcasted_iota(jnp.int32, (STEP, wide), 0)
        other = transform(lane)
        cosine, sine = cos_sin(row * other, length)
        turn_cos, turn_sin = cos_sin(STEP * other, length)
        if freq_in_rows:
            special = row == 0
            alternate = jnp.where(other & 1 == 0, 1.0, -1.0)
        else:
            special = other == 0
            alternate = jnp.where(row & 1 == 0, 1.0, -1.0)

        def body(k, carry):
            cosine, sine = carry
            at = pl.multiple_of(k * STEP, STEP)
            ref_cos, ref_sin = cos_at(at), sin_at(at)
            patch = special & (k == 0) if freq_in_rows else special
            ref[ref_cos] = cosine.astype(BF16)
            ref[ref_sin] = jnp.where(patch, alternate, sine).astype(BF16)
            return (
                cosine * turn_cos - sine * turn_sin,
                sine * turn_cos + cosine * turn_sin,
            )

        lax.fori_loop(0, rows // STEP, body, (cosine, sine), unroll=4)

    for c in range(half // wide):
        columns(
            forward_ref,
            c * wide,
            False,
            length,
            lambda at, c=c: (pl.ds(at, STEP), pl.ds(c * wide, wide)),
            lambda at, c=c: (pl.ds(at, STEP), pl.ds(half + c * wide, wide)),
            lambda lane: lane,
        )
    for c in range(length // wide):
        columns(
            inverse_ref,
            c * wide,
            True,
            half,
            lambda at, c=c: (pl.ds(at, STEP), pl.ds(c * wide, wide)),
            lambda at, c=c: (pl.ds(pl.multiple_of(half + at, STEP), STEP), pl.ds(c * wide, wide)),
            lambda lane: PH * (lane & (per_phase - 1)) + lane // per_phase,
        )


def make_tables(length):
    shape = jax.ShapeDtypeStruct((length, length), BF16)
    return pl.pallas_call(
        lambda *refs: table_kernel(length, *refs),
        out_shape=(shape, shape),
        in_specs=[],
        out_specs=[pl.BlockSpec(memory_space=pltpu.VMEM)] * 2,
        compiler_params=pltpu.CompilerParams(vmem_limit_bytes=24 * MIB),
        cost_estimate=pl.CostEstimate(
            flops=16 * length * length, bytes_accessed=4 * length * length, transcendentals=0
        ),
        name="tables",
    )()


def slots_kernel(owner_count, records_ref, owners_ref, out_ref):
    stations = records_ref.shape[0]
    blocks, dests = owners_ref.shape
    per_owner = SLOTS * BS
    rows = owner_count * per_owner
    k_of = lax.broadcasted_iota(jnp.int32, (blocks, stations), 0)
    station = lax.broadcasted_iota(jnp.int32, (blocks, stations), 1)
    expand = jnp.where(station // BS == k_of, 1.0, 0.0)
    named = lax.dot_general(
        owners_ref[...].astype(F32), expand, (((0,), (0,)), ((), ())), preferred_element_type=F32
    )
    row = lax.broadcasted_iota(jnp.int32, (rows, stations), 0)
    col = lax.broadcasted_iota(jnp.int32, (rows, stations), 1)
    owner = (row // per_owner).astype(F32)
    wanted = jnp.zeros((rows, stations), F32)
    for d in range(dests):
        wanted = jnp.maximum(wanted, jnp.where(named[d : d + 1, :] == owner, 1.0, 0.0))
    lower = lax.broadcasted_iota(jnp.int32, (stations, stations), 0)
    upper = lax.broadcasted_iota(jnp.int32, (stations, stations), 1)
    earlier = jnp.where((lower // BS < upper // BS) & (lower % BS == 0), 1.0, 0.0)
    rank = dot(wanted.astype(BF16), earlier.astype(BF16))
    slot = (row // BS % SLOTS).astype(F32)
    select = jnp.where((rank == slot) & (row % BS == col % BS), wanted, 0.0).astype(BF16)
    out_ref[...] = dot(select, records_ref[...]).astype(BF16)


def fill_slots(records, owners, owner_count):
    stations, length = records.shape
    rows = owner_count * SLOTS * BS
    return pl.pallas_call(
        lambda *refs: slots_kernel(owner_count, *refs),
        out_shape=jax.ShapeDtypeStruct((rows, length), BF16),
        in_specs=[pl.BlockSpec(memory_space=pltpu.VMEM)] * 2,
        out_specs=pl.BlockSpec(memory_space=pltpu.VMEM),
        compiler_params=pltpu.CompilerParams(vmem_limit_bytes=8 * MIB),
        cost_estimate=pl.CostEstimate(
            flops=2 * rows * stations * length, bytes_accessed=2 * rows * length, transcendentals=0
        ),
        name="slots",
    )(records, owners)


def seg_total(column, segs):
    rows = column.shape[0] // segs
    total = column[:rows]
    for s in range(1, segs):
        total = total + column[s * rows : (s + 1) * rows]
    return jnp.concatenate([total] * segs, axis=0)


def flatten(x_ref, forward_ref, re_ref, im_ref, mag_ref, flat_ref, segs):
    rows, length = x_ref.shape
    half = length // 2
    window = length * segs
    wide = 256
    lane = lax.broadcasted_iota(jnp.int32, (rows, wide), 1)

    total = jnp.zeros((rows, wide), F32)
    for c in range(half // wide):
        cols = pl.ds(c * wide, wide)
        re = dot(x_ref[...], forward_ref[:, c * wide : (c + 1) * wide])
        im = dot(x_ref[...], forward_ref[:, half + c * wide : half + (c + 1) * wide])
        if c == 0:
            mag = jnp.where(lane == 0, jnp.abs(re), jnp.sqrt(re * re + im * im))
            total = total + jnp.where(lane == 0, 0.5 * (jnp.abs(re) + jnp.abs(im)), mag)
        else:
            mag = jnp.sqrt(re * re + im * im)
            total = total + mag
        re_ref[:, cols] = re
        im_ref[:, cols] = im
        mag_ref[:, cols] = mag
    amp = seg_total(2.0 * jnp.sum(total, axis=1, keepdims=True), segs)
    level = WATER * amp / window + EPSILON
    for c in range(half // wide):
        cols = pl.ds(c * wide, wide)
        re, im, mag = re_ref[:, cols], im_ref[:, cols], mag_ref[:, cols]
        flat_re = re / (mag + level)
        if c == 0:
            im_mag = jnp.where(lane == 0, jnp.abs(im), mag)
            flat_im = im / (im_mag + level)
            weight = jnp.where(lane == 0, 1.0, 2.0)
        else:
            flat_im = im / (mag + level)
            weight = 2.0
        flat_ref[:, cols] = (flat_re * weight).astype(BF16)
        flat_ref[:, pl.ds(half + c * wide, wide)] = (flat_im * weight).astype(BF16)


def traces(flat_ref, inverse_ref, trace_ref, segs):
    rows, length = trace_ref.shape
    window = length * segs
    wide = 256
    total = jnp.zeros((rows, wide), F32)
    for c in range(length // wide):
        tr = dot(flat_ref[...], inverse_ref[:, c * wide : (c + 1) * wide]) * (1.0 / length)
        total = total + tr * tr
        trace_ref[:, pl.ds(c * wide, wide)] = tr
    energy = seg_total(jnp.sum(total, axis=1, keepdims=True), segs)
    return lax.rsqrt(energy / window + EPSILON)


def own_kernel(
    segs, x_ref, forward_ref, inverse_ref,
    white_ref, shifted_ref, extra_ref,
    re_ref, im_ref, mag_ref, flat_ref, trace_ref, phase_ref,
):
    rows, length = x_ref.shape
    stations = rows // segs
    per_phase = length // PH
    wide = 256
    flatten(x_ref, forward_ref, re_ref, im_ref, mag_ref, flat_ref, segs)
    scale = traces(flat_ref, inverse_ref, trace_ref, segs)
    mine = pl.multiple_of(lax.axis_index("seg") * stations, stations)
    my_flat = flat_ref[pl.ds(mine, stations), :]
    my_scale = scale[:stations]
    for c in range(length // wide):
        tr = dot_t(my_flat, forward_ref[c * wide : (c + 1) * wide, :]) * (1.0 / length)
        white_ref[:, pl.ds(c * wide, wide)] = (tr * my_scale).astype(BF16)
    for p in range(PH):
        for s in range(segs):
            tile = trace_ref[s * stations : (s + 1) * stations, p * per_phase : (p + 1) * per_phase]
            phase_ref[s, (PH - 1 - p) * stations : (PH - p) * stations, :] = (
                (tile * my_scale).astype(BF16).astype(F32)
            )
    count = LAGS // PH
    total = segs * per_phase
    lane = lax.broadcasted_iota(jnp.int32, (PH, total), 1)

    def body(a, _):
        block = jnp.concatenate(
            [phase_ref[s, pl.ds(a, PH, stride=stations), :] for s in range(segs)], axis=1
        )
        for i in range(-1, count):
            m = i + 1 - count // 2
            moved = pltpu.roll(block, m % total, 1) if m % total else block
            if m > 0:
                moved = jnp.where(lane >= m, moved, 0.0)
            elif m < 0:
                moved = jnp.where(lane < total + m, moved, 0.0)
            moved = moved.astype(BF16)
            if i < 0:
                extra_ref[pl.ds(pl.multiple_of(a * PH, PH), PH), :] = moved
            else:
                shifted_ref[pl.ds(pl.multiple_of(a * LAGS + i * PH, PH), PH), :] = moved
        return 0

    lax.fori_loop(0, stations, body, 0)


def own_part(x, forward, inverse, segs):
    rows, length = x.shape
    stations = rows // segs
    total = segs * length // PH
    half = length // 2
    return pl.pallas_call(
        lambda *refs: own_kernel(segs, *refs),
        out_shape=(
            jax.ShapeDtypeStruct((stations, length), BF16),
            jax.ShapeDtypeStruct((stations * LAGS, total), BF16),
            jax.ShapeDtypeStruct((stations * PH, total), BF16),
        ),
        in_specs=[pl.BlockSpec(memory_space=pltpu.VMEM)] * 3,
        out_specs=[pl.BlockSpec(memory_space=pltpu.VMEM)] * 3,
        scratch_shapes=[
            pltpu.VMEM((rows, half), F32),
            pltpu.VMEM((rows, half), F32),
            pltpu.VMEM((rows, half), F32),
            pltpu.VMEM((rows, length), BF16),
            pltpu.VMEM((rows, length), F32),
            pltpu.VMEM((segs, stations * PH, length // PH), F32),
        ],
        compiler_params=pltpu.CompilerParams(vmem_limit_bytes=48 * MIB),
        cost_estimate=pl.CostEstimate(
            flops=8 * rows * length * length, bytes_accessed=40 * MIB, transcendentals=0
        ),
        name="own",
    )(x, forward, inverse)


def correlate_kernel(
    segs, x_ref, forward_ref, inverse_ref, shifted_ref, extra_ref,
    out_ref,
    re_ref, im_ref, mag_ref, flat_ref, trace_ref, phase_ref, edge_ref, total_ref,
):
    rows, length = x_ref.shape
    received = rows // segs
    stations = shifted_ref.shape[0] // LAGS
    per_phase = length // PH
    flatten(x_ref, forward_ref, re_ref, im_ref, mag_ref, flat_ref, segs)
    scale = traces(flat_ref, inverse_ref, trace_ref, segs)[:received]
    for p in range(PH):
        for s in range(segs):
            tile = trace_ref[s * received : (s + 1) * received, p * per_phase : (p + 1) * per_phase]
            phase_ref[
                p * received : (p + 1) * received, s * per_phase : (s + 1) * per_phase
            ] = (tile * scale).astype(BF16)
    edge = dot_t(phase_ref[...], extra_ref[...])
    width = stations * PH
    lag = lax.broadcasted_iota(jnp.int32, (received, width), 1) % PH
    sums = jnp.zeros((received, width), F32)
    for p in range(PH):
        block = edge[p * received : (p + 1) * received]
        turn = (p + 1 - PH) % width
        if turn:
            block = pltpu.roll(block, turn, 1)
        sums = sums + jnp.where(lag <= p, block, 0.0)
    edge_ref[...] = sums
    lane = lax.broadcasted_iota(jnp.int32, (received, LAGS), 1)
    norm = 1.0 / math.sqrt(segs * length)

    def body(a, _):
        at = pl.multiple_of(a * LAGS, LAGS)
        product = dot_t(phase_ref[...], shifted_ref[pl.ds(at, LAGS), :])
        first = pltpu.roll(edge_ref[...], (stations - a) * PH, 1)
        if width < LAGS:
            first = jnp.concatenate([first, jnp.zeros((received, LAGS - width), F32)], axis=1)
        sums = jnp.where(lane < PH, first, 0.0)
        for p in range(PH):
            block = pltpu.roll(product[p * received : (p + 1) * received], p + 1, 1)
            sums = sums + jnp.where(lane > p, block, 0.0)
        sums = sums * norm
        for c in range(LAGS // 128):
            total_ref[c, pl.ds(a, received, stride=stations), :] = sums[:, c * 128 : (c + 1) * 128]
        return 0

    lax.fori_loop(0, stations, body, 0)
    for c in range(LAGS // 128):
        out_ref[:, c * 128 : (c + 1) * 128] = total_ref[c].astype(BF16)


def correlate(x, forward, inverse, shifted, extra, segs):
    rows, length = x.shape
    received = rows // segs
    stations = shifted.shape[0] // LAGS
    total = segs * length // PH
    half = length // 2
    return pl.pallas_call(
        lambda *refs: correlate_kernel(segs, *refs),
        out_shape=jax.ShapeDtypeStruct((received * stations, LAGS), BF16),
        in_specs=[pl.BlockSpec(memory_space=pltpu.VMEM)] * 5,
        out_specs=pl.BlockSpec(memory_space=pltpu.VMEM),
        scratch_shapes=[
            pltpu.VMEM((rows, half), F32),
            pltpu.VMEM((rows, half), F32),
            pltpu.VMEM((rows, half), F32),
            pltpu.VMEM((rows, length), BF16),
            pltpu.VMEM((rows, length), F32),
            pltpu.VMEM((received * PH, total), BF16),
            pltpu.VMEM((received, stations * PH), F32),
            pltpu.VMEM((LAGS // 128, received * stations, 128), F32),
        ],
        compiler_params=pltpu.CompilerParams(vmem_limit_bytes=48 * MIB),
        cost_estimate=pl.CostEstimate(
            flops=8 * rows * length * length, bytes_accessed=40 * MIB, transcendentals=0
        ),
        name="correlate",
    )(x, forward, inverse, shifted, extra)


def on_device(records, owners):
    stations, length = records.shape
    segs, sources = lax.axis_size("seg"), lax.axis_size("sta")
    rows_of = sources // segs
    route = [
        ((z * rows_of + y) * segs + g, (g * rows_of + y) * segs + z)
        for z in range(segs)
        for y in range(rows_of)
        for g in range(segs)
    ]
    routed = lax.ppermute(records, ("sta", "seg"), route)
    routed_owners = lax.ppermute(owners, ("sta", "seg"), route)
    whole = jnp.broadcast_to(records[None], (segs, stations, length))
    own = lax.all_to_all(whole, "seg", 0, 0, tiled=True).reshape(segs * stations, length)
    forward, inverse = make_tables(length)
    slots = fill_slots(routed, routed_owners, sources)
    slots = slots.reshape(sources, SLOTS * BS, length)
    received = lax.all_to_all(slots, "sta", 0, 0, tiled=True)
    received = received.reshape(segs * rows_of * SLOTS * BS, length)
    whitened, shifted, extra = own_part(own, forward, inverse, segs)
    result = correlate(received, forward, inverse, shifted, extra, segs)
    return whitened, result.reshape(-1, stations, LAGS)


def solution(mesh):
    return jax.shard_map(
        on_device,
        mesh=mesh,
        in_specs=(P("sta", "seg"), P("sta", None)),
        out_specs=(P("sta", "seg"), P("seg", "sta", None)),
        check_vma=False,
    )
```

time: 301 us -> 96.7 us (0.32)
  local copies, waits for them, and re-layouts: 81 us -> 10 us
  other arithmetic: 68.7 us -> 0 us
  blocking collectives: 68.6 us -> 0 us
  Pallas kernels: 0 us -> 53.1 us
  waiting for transfers between devices: 40.9 us -> 2.66 us
  starting transfers between devices: 4.39 us -> 28.4 us
  matrix products: 19.6 us -> 0 us
  between operations: 14.2 us -> 0.69 us
    another operation x2 -> x0, other arithmetic: 66.9 us -> none
    pallas_call x0 -> x4, Pallas kernels: none -> 53.1 us  [the longest x1 24.5 us: correlate(): pl.pallas_call(lambda *refs: correlate_kernel(segs, *refs), out_shape=jax...]
    reshape x3 -> x2, local copies, waits for them, and re-layouts: 48.5 us -> 1.13 us  [the longest x1 1.01 us: on_device(): slots = slots.reshape(sources, SLOTS * BS, length)]
    reduce_scatter x1 -> x0, waiting for transfers between devices: 40.8 us -> none  [on_device(): lax.psum_scatter((product.reshape(recv_rows // seg_count * lax.axis_size(...]
    all_gather x1 -> x0, blocking collectives: 40.7 us -> none  [on_device(): lax.all_gather(owners, 'sta', axis=0, tiled=True)]
    psum x2 -> x0, blocking collectives: 27.9 us -> none  [the longest x1 15 us: on_device(): amp_total = lax.psum(jnp.sum(magnitude, axis=1), 'seg')]
    all_to_all x0 -> x2, starting transfers between devices: none -> 22.9 us  [the longest x1 16.2 us: on_device(): received = lax.all_to_all(slots, 'sta', 0, 0, tiled=True)]
    dot_general x4 -> x0, matrix products: 19.6 us -> none  [the longest x1 8.33 us: on_device(): jnp.einsum('ajui,bsji->basu', lagged, shifted, preferred_element_type=jnp...]
  transfers between devices with their start and end apart: 4 -> 4, of which waited for: 1 -> 1; matrix products, arithmetic and copies ran while one was open for 22% -> 2% of each run, Pallas kernels for 0% -> 30%
where the time goes in v1:
time: 96.7 us; the launch traced here: 94.8 us
  Pallas kernels  53.1 us (55%)
  starting transfers between devices  28.4 us (29%)
  local copies, waits for them, and re-layouts  10 us (10%)
  waiting for transfers between devices  2.66 us (3%)
    pallas_call x1, Pallas kernels, correlate(): pl.pallas_call(lambda *refs: correlate_kernel(segs, *refs), out_shape=jax...  24.5 us
    pallas_call x1, Pallas kernels, own_part(): pl.pallas_call(lambda *refs: own_kernel(segs, *refs), out_shape=(jax.Shap...  22.5 us
    all_to_all x1, starting transfers between devices, on_device(): received = lax.all_to_all(slots, 'sta', 0, 0, tiled=True)  16.2 us
    unnamed x5, local copies, waits for them, and re-layouts  7.21 us
    all_to_all x1, starting transfers between devices, on_device(): lax.all_to_all(whole, 'seg', 0, 0, tiled=True)  6.63 us
    pallas_call x1, Pallas kernels, make_tables(): pl.pallas_call(lambda *refs: table_kernel(length, *refs), out_shape=(shap...  5.52 us
    ppermute x1, starting transfers between devices, on_device(): routed_owners = lax.ppermute(owners, ('sta', 'seg'), route)  2.95 us
    ppermute x1, waiting for transfers between devices, on_device(): routed_owners = lax.ppermute(owners, ('sta', 'seg'), route)  2.65 us
  transfers between devices with their start and end apart: 4, of which 1 were waited for; matrix products, arithmetic and copies ran while one was open for 2% of the time, Pallas kernels for 30%

profile of v1, /device:TPU:1, one launch (start us, length us, event | category | flops | bytes accessed | tf_op | source)
XLA Modules:
  0.0 94.8 jit_solution(4265850430635850566)
XLA Ops:
  0.6 1.7 %broadcast_in_dim.2 = bf16[8,16,2048]{2,1,0:T(8,128)(2,1)} broadcast(bf16[16,2048]{1,0:T(8,128)(2,1)} %param.2), dimensions={1,2} | broadcast | bytes 589824 | tf_op jit(solution)/shard_map/broadcast_in_dim | solution.py:384
  2.3 6.6 %all-to-all-start = ((bf16[8,16,2048]{2,1,0:T(8,128)(2,1)}), bf16[8,16,2048]{2,1,0:T(8,128)(2,1)S(1)}, u32[]{:S(2)}, u32[]{:S(2)}) async-start(bf16[8,16,2048]{2,1,0:T(8,128)(2,1)} %broadcast_in_dim.2), calls=%async_computation | async-start | bytes 1048576 | tf_op jit(solution)/shard_map/all_to_all | solution.py:385
  9.0 2.6 %collective-permute-start = (bf16[16,2048]{1,0:T(8,128)(2,1)}, bf16[16,2048]{1,0:T(8,128)(2,1)S(1)}, u32[]{:S(2)}, u32[]{:S(2)}) collective-permute-start(bf16[16,2048]{1,0:T(8,128)(2,1)} %param.2), channel_id=1, source_target_pairs={{0,0},{1,32},{2,64},{3,96},{4,128},{5,160},{6,192},{7,224},{8,8},{... | collective-permute-start | bytes 196616 | tf_op jit(solution)/shard_map/ppermute | solution.py:382
  11.6 0.8 copy.4
  12.3 2.9 %collective-permute-start.1 = (s32[8,4]{1,0:T(8,128)S(1)}, s32[8,4]{1,0:T(8,128)S(1)}, u32[]{:S(2)}, u32[]{:S(2)}) collective-permute-start(s32[8,4]{1,0:T(8,128)S(1)} %copy.4), channel_id=1, source_target_pairs={{0,0},{1,32},{2,64},{3,96},{4,128},{5,160},{6,192},{7,224},{8,8},{... | collective-permute-start | bytes 392 | tf_op jit(solution)/shard_map/ppermute | solution.py:383
  15.3 2.7 %collective-permute-done.1.refs_1_ = s32[8,4]{1,0:T(8,128)S(1)} collective-permute-done((s32[8,4]{1,0:T(8,128)S(1)}, s32[8,4]{1,0:T(8,128)S(1)}, u32[]{:S(2)}, u32[]{:S(2)}) %collective-permute-start.1) | collective-permute-done | bytes 160 | tf_op jit(solution)/shard_map/ppermute | solution.py:383
  17.9 0.0 collective-permute-done.refs_0_
  17.9 0.6 slots.1
  18.5 1.0 %reshape.18 = bf16[32,4,2048]{2,1,0:T(4,128)(2,1)} reshape(bf16[128,2048]{1,0:T(8,128)(2,1)S(1)} %slots.1) | data formatting | bytes 1048576 | tf_op jit(solution)/shard_map/reshape | solution.py:388
  19.5 0.0 all-to-all-done
  19.5 16.2 %all-to-all-start.1 = ((bf16[32,4,2048]{2,1,0:T(4,128)(2,1)}), bf16[32,4,2048]{2,1,0:T(4,128)(2,1)S(1)}, u32[]{:S(2)}, u32[]{:S(2)}) async-start(bf16[32,4,2048]{2,1,0:T(4,128)(2,1)} %reshape.18), calls=%async_computation.1 | async-start | bytes 1048576 | tf_op jit(solution)/shard_map/all_to_all | solution.py:389
  35.8 5.5 %tables.1 = (bf16[2048,2048]{1,0:T(8,128)(2,1)S(1)}, bf16[2048,2048]{1,0:T(8,128)(2,1)S(1)}) custom-call(), custom_call_target="tpu_custom_call" | custom-call | flops 67108864 | bytes 16777216 | tf_op jit(solution)/shard_map/tables/pallas_call | solution.py:100
  41.3 0.0 copy-start
  41.3 3.2 %copy-done = bf16[2048,2048]{1,0:T(8,128)(2,1)} copy-done((bf16[2048,2048]{1,0:T(8,128)(2,1)}, bf16[2048,2048]{1,0:T(8,128)(2,1)S(1)}, u32[]{:S(2)}) %copy-start) | copy-done | bytes 8388632
  44.5 0.0 copy-start.1
  44.5 3.2 %copy-done.1 = bf16[2048,2048]{1,0:T(8,128)(2,1)} copy-done((bf16[2048,2048]{1,0:T(8,128)(2,1)}, bf16[2048,2048]{1,0:T(8,128)(2,1)S(1)}, u32[]{:S(2)}) %copy-start.1) | copy-done | bytes 8388632
  47.8 22.5 %own.1 = (bf16[16,2048]{1,0:T(8,128)(2,1)}, bf16[8192,1024]{1,0:T(8,128)(2,1)}, bf16[256,1024]{1,0:T(8,128)(2,1)S(1)}) custom-call(bf16[128,2048]{1,0:T(8,128)(2,1)S(1)} %bitcast.2, bf16[2048,2048]{1,0:T(8,128)(2,1)} %copy-done, bf16[2048,2048]{1,0:T(8,128)(2,1)} %copy-done.1), custom_call_target="tpu_custom_call" | custom-call | flops 4294967296 | bytes 41943040 | tf_op jit(solution)/shard_map/own/pallas_call | solution.py:267
  70.2 0.0 all-to-all-done.1
  70.2 0.1 reshape.19.refs_0_
  70.3 24.5 %correlate.1 = bf16[256,512]{1,0:T(8,128)(2,1)} custom-call(bf16[128,2048]{1,0:T(8,128)(2,1)S(1)} %reshape.19.refs_0_, bf16[2048,2048]{1,0:T(8,128)(2,1)} %copy-done, bf16[2048,2048]{1,0:T(8,128)(2,1)} %copy-done.1, bf16[8192,1024]{1,0:T(8,128)(2,1)} %get-tuple-element.10.refs_3_, bf16[256,1024]{1,0:T(8,128)(2,1)S(1)} %get-tuple-element.11.refs_4_), custom_call_target="tpu_custom_call" | custom-call | flops 4294967296 | bytes 41943040 | tf_op jit(solution)/shard_map/correlate/pallas_call | solution.py:349
Async XLA Ops:
  2.3 17.2 %all-to-all-start = ((bf16[8,16,2048]{2,1,0:T(8,128)(2,1)}), bf16[8,16,2048]{2,1,0:T(8,128)(2,1)S(1)}, u32[]{:S(2)}, u32[]{:S(2)}) async-start(bf16[8,16,2048]{2,1,0:T(8,128)(2,1)} %broadcast_in_dim.2), calls=%async_computation | async-start | bytes 1048576 | tf_op jit(solution)/shard_map/all_to_all | solution.py:385
  9.0 9.0 %collective-permute-start = (bf16[16,2048]{1,0:T(8,128)(2,1)}, bf16[16,2048]{1,0:T(8,128)(2,1)S(1)}, u32[]{:S(2)}, u32[]{:S(2)}) collective-permute-start(bf16[16,2048]{1,0:T(8,128)(2,1)} %param.2), channel_id=1, source_target_pairs={{0,0},{1,32},{2,64},{3,96},{4,128},{5,160},{6,192},{7,224},{8,8},{... | collective-permute-start | bytes 196616 | tf_op jit(solution)/shard_map/ppermute | solution.py:382
  12.3 5.6 %collective-permute-start.1 = (s32[8,4]{1,0:T(8,128)S(1)}, s32[8,4]{1,0:T(8,128)S(1)}, u32[]{:S(2)}, u32[]{:S(2)}) collective-permute-start(s32[8,4]{1,0:T(8,128)S(1)} %copy.4), channel_id=1, source_target_pairs={{0,0},{1,32},{2,64},{3,96},{4,128},{5,160},{6,192},{7,224},{8,8},{... | collective-permute-start | bytes 392 | tf_op jit(solution)/shard_map/ppermute | solution.py:383
  19.5 50.7 %all-to-all-start.1 = ((bf16[32,4,2048]{2,1,0:T(4,128)(2,1)}), bf16[32,4,2048]{2,1,0:T(4,128)(2,1)S(1)}, u32[]{:S(2)}, u32[]{:S(2)}) async-start(bf16[32,4,2048]{2,1,0:T(4,128)(2,1)} %reshape.18), calls=%async_computation.1 | async-start | bytes 1048576 | tf_op jit(solution)/shard_map/all_to_all | solution.py:389
  41.3 3.2 %copy-start = (bf16[2048,2048]{1,0:T(8,128)(2,1)}, bf16[2048,2048]{1,0:T(8,128)(2,1)S(1)}, u32[]{:S(2)}) copy-start(bf16[2048,2048]{1,0:T(8,128)(2,1)S(1)} %get-tuple-element.7.refs_1_) | copy-start | bytes 25165828
  44.5 3.2 %copy-start.1 = (bf16[2048,2048]{1,0:T(8,128)(2,1)}, bf16[2048,2048]{1,0:T(8,128)(2,1)S(1)}, u32[]{:S(2)}) copy-start(bf16[2048,2048]{1,0:T(8,128)(2,1)S(1)} %get-tuple-element.8.refs_2_) | copy-start | bytes 25165828

commit v2 on v0

v2 whole, which is shorter than its diff:
```python
import math

import jax
import jax.numpy as jnp
from jax import lax
from jax.experimental import pallas as pl
from jax.experimental.pallas import tpu as pltpu
from jax.sharding import PartitionSpec as P

LAGS = 512
BS = 2
SLOTS = 2
WATER = 0.5
EPSILON = 1e-06

PH = 16
LANES = 128
CORES = 2
GROUP = 4
F32 = jnp.float32
BF16 = jnp.bfloat16
MIB = 1 << 20


def dot(a, b):
    return lax.dot_general(a, b, (((1,), (0,)), ((), ())), preferred_element_type=F32)


def dot_t(a, b):
    return lax.dot_general(a, b, (((1,), (1,)), ((), ())), preferred_element_type=F32)


def iota(shape, axis):
    return lax.broadcasted_iota(jnp.int32, shape, axis)


def cos_sin(phase, period):
    phase = phase & (period - 1)
    phase = jnp.where(phase >= period // 2, phase - period, phase)
    theta = phase.astype(F32) * (2.0 * math.pi / period)
    square = theta * theta
    cosine = jnp.full(theta.shape, 1.0 / math.factorial(20), F32)
    sine = jnp.full(theta.shape, 1.0 / math.factorial(21), F32)
    for n in range(9, -1, -1):
        cosine = (1.0 if n % 2 == 0 else -1.0) / math.factorial(2 * n) + square * cosine
        sine = (1.0 if n % 2 == 0 else -1.0) / math.factorial(2 * n + 1) + square * sine
    return cosine, sine * theta


def spread():
    shape = (LANES, PH * LANES)
    source, target = iota(shape, 0), iota(shape, 1)
    hit = (target // LANES == source % PH) & (target % LANES == source // PH)
    return jnp.where(hit, 1.0, 0.0).astype(BF16)


def prepare_kernel(owner_count, records_ref, owners_ref, phased_ref, slots_ref):
    stations, length = records_ref.shape
    blocks, dests = owners_ref.shape
    per_tile = LANES // PH
    tiles = jnp.concatenate(
        [records_ref[:, t * LANES : (t + 1) * LANES] for t in range(length // LANES)], axis=0
    )
    parts = dot(tiles, spread())
    phases = []
    for p in range(PH):
        total = None
        for t in range(length // LANES):
            part = parts[t * stations : (t + 1) * stations, p * LANES : (p + 1) * LANES]
            part = pltpu.roll(part, per_tile * t, 1) if t else part
            total = part if total is None else total + part
        phases.append(total.astype(BF16))
    for p in range(PH):
        phased_ref[:, p * LANES : (p + 1) * LANES] = phases[p]
    high = PH // GROUP
    stacked = jnp.concatenate(
        [jnp.concatenate(phases[h * GROUP : (h + 1) * GROUP], axis=1) for h in range(high)], axis=0
    )
    rows, width = owner_count * high * SLOTS * BS, high * stations
    k_of, column = iota((blocks, width), 0), iota((blocks, width), 1)
    expand = jnp.where(column % stations // BS == k_of, 1.0, 0.0)
    named = lax.dot_general(
        owners_ref[...].astype(F32), expand, (((0,), (0,)), ((), ())), preferred_element_type=F32
    )
    row, col = iota((rows, width), 0), iota((rows, width), 1)
    owner = (row // (high * SLOTS * BS)).astype(F32)
    wanted = jnp.zeros((rows, width), F32)
    for d in range(dests):
        wanted = jnp.maximum(wanted, jnp.where(named[d : d + 1, :] == owner, 1.0, 0.0))
    first, second = iota((width, width), 0), iota((width, width), 1)
    earlier = (
        (first // stations == second // stations)
        & (first % stations // BS < second % stations // BS)
        & (first % BS == 0)
    )
    rank = dot(wanted.astype(BF16), jnp.where(earlier, 1.0, 0.0).astype(BF16))
    slot = (row // BS % SLOTS).astype(F32)
    right = (
        (rank == slot)
        & (row % BS == col % BS)
        & (row // (SLOTS * BS) % high == col // stations)
    )
    select = jnp.where(right, wanted, 0.0).astype(BF16)
    slots_ref[...] = dot(select, stacked).astype(BF16)


def prepare(records, owners, owner_count):
    stations, length = records.shape
    rows = owner_count * SLOTS * BS * PH // GROUP
    return pl.pallas_call(
        lambda *refs: prepare_kernel(owner_count, *refs),
        out_shape=(
            jax.ShapeDtypeStruct((stations, length), BF16),
            jax.ShapeDtypeStruct((rows, GROUP * LANES), BF16),
        ),
        in_specs=[pl.BlockSpec(memory_space=pltpu.VMEM)] * 2,
        out_specs=[pl.BlockSpec(memory_space=pltpu.VMEM)] * 2,
        compiler_params=pltpu.CompilerParams(vmem_limit_bytes=16 * MIB),
        cost_estimate=pl.CostEstimate(
            flops=100 * MIB, bytes_accessed=2 * MIB, transcendentals=0
        ),
        name="prepare",
    )(records, owners)


def add(a, b):
    return a[0] + b[0], a[1] + b[1]


def sub(a, b):
    return a[0] - b[0], a[1] - b[1]


def times_i(a, sign):
    return (-a[1], a[0]) if sign > 0 else (a[1], -a[0])


def times(a, b):
    return a[0] * b[0] - a[1] * b[1], a[0] * b[1] + a[1] * b[0]


def unit(a, k, sign):
    k %= 16
    if k == 0:
        return a
    if k == 4:
        return times_i(a, sign)
    if k == 8:
        return -a[0], -a[1]
    if k == 12:
        return times_i(a, -sign)
    angle = 2.0 * math.pi * k / 16
    return times(a, (math.cos(angle), sign * math.sin(angle)))


def four(a, sign):
    s, d = add(a[0], a[2]), sub(a[0], a[2])
    t, e = add(a[1], a[3]), times_i(sub(a[1], a[3]), sign)
    return [add(s, t), add(d, e), sub(s, t), sub(d, e)]


def forward_sixteen(v):
    inner = [four([v[4 * p1 + p0] for p1 in range(4)], 1) for p0 in range(4)]
    out = [None] * 8
    for fa in range(4):
        u = [unit(inner[p0][fa], p0 * fa, 1) for p0 in range(4)]
        s, t = add(u[0], u[2]), add(u[1], u[3])
        out[fa] = add(s, t)
        out[fa + 4] = add(sub(u[0], u[2]), times_i(sub(u[1], u[3]), 1))
        if fa == 0:
            last = s[0] - t[0]
    return out, last


def inverse_sixteen(f):
    out = [None] * 16
    for p0 in range(4):
        inner = []
        for fa in range(4):
            turned = unit(f[fa + 4], 4 * p0, -1)
            inner.append(unit(add(f[fa], turned), p0 * fa, -1))
        for p1, value in enumerate(four(inner, -1)):
            out[4 * p1 + p0] = value
    return out


def seg_total(values, segs):
    rows = values.shape[0] // segs
    total = values[:rows]
    for s in range(1, segs):
        total = total + values[s * rows : (s + 1) * rows]
    return total


def whiten(x_ref, y_ref, f_ref, sum_ref, trace_ref, segs):
    rows = x_ref.shape[1]
    length = PH * LANES
    window = length * segs
    half = PH // 2
    n, k = iota((LANES, LANES), 0), iota((LANES, LANES), 1)
    cosine, sine = cos_sin(n * k, LANES)
    table = jnp.concatenate([cosine, sine], axis=1).astype(BF16)
    back = jnp.concatenate([cosine, sine], axis=0).astype(BF16)
    turn_cos, turn_sin = cos_sin(iota((PH, LANES), 0) * iota((PH, LANES), 1), length)
    for p in range(PH):
        y_ref[p] = dot(x_ref[p], table)
    lane = iota((8, LANES), 1)

    def forward(i, _):
        at = pl.ds(pl.multiple_of(i * 8, 8), 8)
        v = []
        for p in range(PH):
            y = y_ref[p, at, :LANES], y_ref[p, at, LANES:]
            v.append(times(y, (turn_cos[p : p + 1], turn_sin[p : p + 1])) if p else y)
        out, last = forward_sixteen(v)
        total = None
        for j, (re, im) in enumerate(out):
            if j == 0:
                mag = jnp.where(lane == 0, jnp.abs(re), jnp.sqrt(re * re + im * im))
                im = jnp.where(lane == 0, last, im)
                total = jnp.where(lane == 0, 0.5 * (jnp.abs(re) + jnp.abs(im)), mag)
            else:
                mag = jnp.sqrt(re * re + im * im)
                total = total + mag
            f_ref[j, at, :] = re
            f_ref[half + j, at, :] = im
            f_ref[2 * half + j, at, :] = mag
        sum_ref[at, :] = total
        return 0

    lax.fori_loop(0, rows // 8, forward, 0)
    amp = 2.0 * jnp.sum(seg_total(sum_ref[...], segs), axis=1, keepdims=True)
    level = WATER * amp / window + EPSILON
    sum_ref[...] = jnp.concatenate(
        [jnp.broadcast_to(level, (rows // segs, LANES))] * segs, axis=0
    )

    def inverse(i, _):
        at = pl.ds(pl.multiple_of(i * 8, 8), 8)
        level = sum_ref[at, :]
        f = []
        for j in range(half):
            re, im, mag = f_ref[j, at, :], f_ref[half + j, at, :], f_ref[2 * half + j, at, :]
            if j == 0:
                edge = im / (jnp.abs(im) + level)
                share = 2.0 / (mag + level)
                f.append(
                    (
                        jnp.where(lane == 0, 0.5, 1.0) * (re * share),
                        jnp.where(lane == 0, 0.0, im * share),
                    )
                )
                edge = jnp.where(lane == 0, edge, 0.0)
            else:
                share = 2.0 / (mag + level)
                f.append((re * share, im * share))
        for p, z in enumerate(inverse_sixteen(f)):
            if p:
                z = times(z, (turn_cos[p : p + 1], -turn_sin[p : p + 1]))
            y_ref[p, at, :LANES] = z[0] - edge if p % 2 else z[0] + edge
            y_ref[p, at, LANES:] = z[1]
        return 0

    lax.fori_loop(0, rows // 8, inverse, 0)
    energy = jnp.zeros((rows, LANES), F32)
    for p in range(PH):
        trace = dot(y_ref[p].astype(BF16), back) * (1.0 / length)
        energy = energy + trace * trace
        trace_ref[p] = trace
    energy = jnp.sum(seg_total(energy, segs), axis=1, keepdims=True)
    return lax.rsqrt(energy / window + EPSILON)


def whiten_scratch(rows):
    return [
        pltpu.VMEM((PH, rows, LANES), BF16),
        pltpu.VMEM((PH, rows, 2 * LANES), F32),
        pltpu.VMEM((3 * PH // 2, rows, LANES), F32),
        pltpu.VMEM((rows, LANES), F32),
        pltpu.VMEM((PH, rows, LANES), F32),
    ]


def own_kernel(
    segs, me_ref, near_ref, far_ref, white_ref, phase_ref, x_ref, y_ref, f_ref, sum_ref, trace_ref
):
    rows, length = x_ref.shape[1], PH * LANES
    stations = rows // segs
    per_tile = LANES // PH
    me, chips = me_ref[0], segs // CORES
    for i in range(chips):
        chip = (me // CORES + chips - i) % chips
        for ref, core in ((near_ref, me % CORES), (far_ref, 1 - me % CORES)):
            at = pl.ds(pl.multiple_of((chip * CORES + core) * stations, stations), stations)
            for p in range(PH):
                x_ref[p, at, :] = ref[
                    i * stations : (i + 1) * stations, p * LANES : (p + 1) * LANES
                ]
    scale = whiten(x_ref, y_ref, f_ref, sum_ref, trace_ref, segs)
    for p in range(PH):
        for s in range(segs):
            tile = trace_ref[p, s * stations : (s + 1) * stations, :]
            phase_ref[s, (PH - 1 - p) * stations : (PH - p) * stations, :] = (
                (tile * scale).astype(BF16).astype(F32)
            )
    mine = pl.ds(pl.multiple_of(me_ref[0] * stations, stations), stations)
    tiles = [trace_ref[p, mine, :] * scale for p in range(PH)]
    moved = []
    for t in range(length // LANES):
        turn = (LANES - per_tile * t) % LANES
        moved.append(
            jnp.concatenate(
                [(pltpu.roll(x, turn, 1) if turn else x).astype(BF16) for x in tiles], axis=1
            )
        )
    natural = dot_t(jnp.concatenate(moved, axis=0), spread()).astype(BF16)
    for t in range(length // LANES):
        white_ref[:, t * LANES : (t + 1) * LANES] = natural[t * stations : (t + 1) * stations]


def own_part(me, near, far, segs):
    rows, length = 2 * near.shape[0], near.shape[1]
    stations = rows // segs
    return pl.pallas_call(
        lambda *refs: own_kernel(segs, *refs),
        out_shape=(
            jax.ShapeDtypeStruct((stations, length), BF16),
            jax.ShapeDtypeStruct((segs, PH * stations, LANES), F32),
        ),
        in_specs=[
            pl.BlockSpec(memory_space=pltpu.SMEM),
            pl.BlockSpec(memory_space=pltpu.VMEM),
            pl.BlockSpec(memory_space=pltpu.VMEM),
        ],
        out_specs=[pl.BlockSpec(memory_space=pltpu.VMEM)] * 2,
        scratch_shapes=whiten_scratch(rows),
        compiler_params=pltpu.CompilerParams(vmem_limit_bytes=32 * MIB),
        cost_estimate=pl.CostEstimate(
            flops=2000 * MIB, bytes_accessed=4 * MIB, transcendentals=0
        ),
        name="own",
    )(me, near, far)


def shift_kernel(segs, stations, phase_ref, shifted_ref, extra_ref):
    count = LAGS // PH
    total = segs * LANES
    lane = iota((PH, total), 1)
    mine = pl.ds(pl.program_id(0), PH, stride=stations)
    block = jnp.concatenate([phase_ref[s, mine, :] for s in range(segs)], axis=1)
    for i in range(-1, count):
        m = i + 1 - count // 2
        moved = pltpu.roll(block, m % total, 1) if m else block
        if m > 0:
            moved = jnp.where(lane >= m, moved, 0.0)
        elif m < 0:
            moved = jnp.where(lane < total + m, moved, 0.0)
        moved = moved.astype(BF16)
        if i < 0:
            extra_ref[...] = moved
        else:
            shifted_ref[i * PH : (i + 1) * PH, :] = moved


def shift(phases, segs):
    stations = phases.shape[1] // PH
    total = segs * LANES
    return pl.pallas_call(
        lambda *refs: shift_kernel(segs, stations, *refs),
        out_shape=(
            jax.ShapeDtypeStruct((stations * LAGS, total), BF16),
            jax.ShapeDtypeStruct((stations * PH, total), BF16),
        ),
        grid=(stations,),
        in_specs=[pl.BlockSpec(phases.shape, lambda a: (0, 0, 0))],
        out_specs=[
            pl.BlockSpec((LAGS, total), lambda a: (a, 0)),
            pl.BlockSpec((PH, total), lambda a: (a, 0)),
        ],
        compiler_params=pltpu.CompilerParams(vmem_limit_bytes=16 * MIB),
        cost_estimate=pl.CostEstimate(
            flops=2000 * MIB, bytes_accessed=18 * MIB, transcendentals=0
        ),
        name="shift",
    )(phases)


def correlate_kernel(
    segs, received_ref, shifted_hbm, extra_hbm,
    out_ref,
    x_ref, y_ref, f_ref, sum_ref, trace_ref, phase_ref, edge_ref, total_ref,
    shifted_ref, extra_ref, sems,
):
    rows = x_ref.shape[1]
    received = rows // segs
    stations = shifted_ref.shape[0]
    copies = [pltpu.make_async_copy(extra_hbm, extra_ref, sems.at[stations])]
    for a in range(stations):
        block = shifted_hbm.at[pl.ds(a * LAGS, LAGS), :]
        copies.append(pltpu.make_async_copy(block, shifted_ref.at[a], sems.at[a]))
    for copy in copies:
        copy.start()
    high, unit_rows = PH // GROUP, SLOTS * BS
    per_seg = high * received
    to, source = iota((per_seg, per_seg), 0), iota((per_seg, per_seg), 1)
    wanted = (
        to % received // unit_rows * (high * unit_rows) + to // received * unit_rows
    ) + to % unit_rows
    order = jnp.where(source == wanted, 1.0, 0.0).astype(BF16)
    for s in range(segs):
        block = dot(order, received_ref[s * per_seg : (s + 1) * per_seg, :]).astype(BF16)
        for p in range(PH):
            x_ref[p, s * received : (s + 1) * received, :] = block[
                p // GROUP * received : (p // GROUP + 1) * received,
                p % GROUP * LANES : (p % GROUP + 1) * LANES,
            ]
    scale = whiten(x_ref, y_ref, f_ref, sum_ref, trace_ref, segs)
    for p in range(PH):
        for s in range(segs):
            tile = trace_ref[p, s * received : (s + 1) * received, :]
            phase_ref[
                p * received : (p + 1) * received, s * LANES : (s + 1) * LANES
            ] = (tile * scale).astype(BF16)
    copies[0].wait()
    edge = dot_t(phase_ref[...], extra_ref[...])
    width = stations * PH
    lag = iota((received, width), 1) % PH
    sums = jnp.zeros((received, width), F32)
    for p in range(PH):
        block = edge[p * received : (p + 1) * received]
        turn = (p + 1 - PH) % width
        block = pltpu.roll(block, turn, 1) if turn else block
        sums = sums + jnp.where(lag <= p, block, 0.0)
    edge_ref[...] = sums
    lane = iota((received, LAGS), 1)
    norm = 1.0 / math.sqrt(segs * PH * LANES)

    def body(a, _):
        block = shifted_hbm.at[pl.ds(pl.multiple_of(a * LAGS, LAGS), LAGS), :]
        pltpu.make_async_copy(block, shifted_ref.at[a], sems.at[a]).wait()
        product = dot_t(phase_ref[...], shifted_ref[a])
        first = pltpu.roll(edge_ref[...], (stations - a) * PH, 1)
        if width < LAGS:
            first = jnp.concatenate([first, jnp.zeros((received, LAGS - width), F32)], axis=1)
        sums = jnp.where(lane < PH, first, 0.0)
        for p in range(PH):
            block = pltpu.roll(product[p * received : (p + 1) * received], p + 1, 1)
            sums = sums + jnp.where(lane > p, block, 0.0)
        sums = sums * norm
        for c in range(LAGS // LANES):
            total_ref[c, pl.ds(a, received, stride=stations), :] = sums[
                :, c * LANES : (c + 1) * LANES
            ]
        return 0

    lax.fori_loop(0, stations, body, 0)
    for c in range(LAGS // LANES):
        out_ref[:, c * LANES : (c + 1) * LANES] = total_ref[c].astype(BF16)


def correlate(received, shifted, extra, segs):
    rows = received.shape[0] // (PH // GROUP)
    count = rows // segs
    stations = shifted.shape[0] // LAGS
    total = segs * LANES
    return pl.pallas_call(
        lambda *refs: correlate_kernel(segs, *refs),
        out_shape=jax.ShapeDtypeStruct((count * stations, LAGS), BF16),
        in_specs=[
            pl.BlockSpec(memory_space=pltpu.VMEM),
            pl.BlockSpec(memory_space=pl.ANY),
            pl.BlockSpec(memory_space=pl.ANY),
        ],
        out_specs=pl.BlockSpec(memory_space=pltpu.VMEM),
        scratch_shapes=[
            *whiten_scratch(rows),
            pltpu.VMEM((count * PH, total), BF16),
            pltpu.VMEM((count, stations * PH), F32),
            pltpu.VMEM((LAGS // LANES, count * stations, LANES), F32),
            pltpu.VMEM((stations, LAGS, total), BF16),
            pltpu.VMEM((stations * PH, total), BF16),
            pltpu.SemaphoreType.DMA((stations + 1,)),
        ],
        compiler_params=pltpu.CompilerParams(vmem_limit_bytes=48 * MIB),
        cost_estimate=pl.CostEstimate(
            flops=6000 * MIB, bytes_accessed=20 * MIB, transcendentals=0
        ),
        name="correlate",
    )(received, shifted, extra)


def on_device(records, owners):
    stations, length = records.shape
    segs, sources = lax.axis_size("seg"), lax.axis_size("sta")
    phased, slots = prepare(records, owners, sources)
    slots = slots.reshape(sources, -1, GROUP * LANES)
    passing = lax.all_to_all(slots, "sta", 0, 0, tiled=True)
    passing = passing.reshape(segs, -1, GROUP * LANES)
    received = lax.all_to_all(passing, "seg", 0, 0, tiled=True).reshape(-1, GROUP * LANES)
    near = [phased]
    for k in range(1, segs // CORES):
        near.append(lax.ppermute(phased, "seg", [(i, (i + k * CORES) % segs) for i in range(segs)]))
    near = jnp.concatenate(near, axis=0)
    far = lax.ppermute(near, "seg", [(i, i ^ 1) for i in range(segs)])
    me = lax.axis_index("seg").reshape(1)
    whitened, phases = own_part(me, near, far, segs)
    shifted, extra = shift(phases, segs)
    result = correlate(received, shifted, extra, segs)
    return whitened, result.reshape(-1, stations, LAGS)


def solution(mesh):
    return jax.shard_map(
        on_device,
        mesh=mesh,
        in_specs=(P("sta", "seg"), P("sta", None)),
        out_specs=(P("sta", "seg"), P("seg", "sta", None)),
        check_vma=False,
    )
```

time: 301 us -> 73.2 us (0.24); the launches traced: 297 us -> 72.9 us
  local copies, waits for them, and re-layouts: 81 us -> 7.35 us
  other arithmetic: 68.7 us -> 0 us
  blocking collectives: 68.6 us -> 0 us
  waiting for transfers between devices: 40.9 us -> 13.2 us
  Pallas kernels: 0 us -> 26.7 us
  starting transfers between devices: 4.39 us -> 24.9 us
  matrix products: 19.6 us -> 0 us
  between operations: 14.2 us -> 0.72 us
    another operation x2 -> x0, other arithmetic: 66.9 us -> none
    reshape x3 -> x0, local copies, waits for them, and re-layouts: 48.5 us -> none  [the longest x1 45.8 us: toeplitz_blocks(): spread.reshape(own_count, pair_count, P_SIZE * (2 * P_SIZE + 1))]
    reduce_scatter x1 -> x0, waiting for transfers between devices: 40.8 us -> none  [on_device(): lax.psum_scatter((product.reshape(recv_rows // seg_count * lax.axis_size(...]
    all_gather x1 -> x0, blocking collectives: 40.7 us -> none  [on_device(): lax.all_gather(owners, 'sta', axis=0, tiled=True)]
    psum x2 -> x0, blocking collectives: 27.9 us -> none  [the longest x1 15 us: on_device(): amp_total = lax.psum(jnp.sum(magnitude, axis=1), 'seg')]
    pallas_call x0 -> x4, Pallas kernels: none -> 26.7 us  [the longest x1 14.5 us: correlate(): pl.pallas_call(lambda *refs: correlate_kernel(segs, *refs), out_shape=jax...]
    dot_general x4 -> x0, matrix products: 19.6 us -> none  [the longest x1 8.33 us: on_device(): jnp.einsum('ajui,bsji->basu', lagged, shifted, preferred_element_type=jnp...]
    all_to_all x0 -> x2, starting transfers between devices: none -> 18.6 us  [the longest x1 11.3 us: on_device(): passing = lax.all_to_all(slots, 'sta', 0, 0, tiled=True)]
  transfers between devices with their start and end apart: 4 -> 6, of which waited for: 1 -> 1; matrix products, arithmetic and copies ran while one was open for 22% -> 0% of each run, Pallas kernels for 0% -> 14%
where the time goes in v2:
time: 73.2 us; the launch traced here: 72.9 us
  Pallas kernels  26.7 us (36%)
  starting transfers between devices  24.9 us (34%)
  waiting for transfers between devices  13.2 us (18%)
  local copies, waits for them, and re-layouts  7.35 us (10%)
    pallas_call x1, Pallas kernels, correlate(): pl.pallas_call(lambda *refs: correlate_kernel(segs, *refs), out_shape=jax...  14.5 us
    all_to_all x1, waiting for transfers between devices, on_device(): passing = lax.all_to_all(slots, 'sta', 0, 0, tiled=True)  13.2 us
    all_to_all x1, starting transfers between devices, on_device(): passing = lax.all_to_all(slots, 'sta', 0, 0, tiled=True)  11.3 us
    unnamed x8, local copies, waits for them, and re-layouts  7.35 us
    all_to_all x1, starting transfers between devices, on_device(): lax.all_to_all(passing, 'seg', 0, 0, tiled=True).reshape(-1, GROUP * LANES)  7.28 us
    pallas_call x1, Pallas kernels, shift(): pl.pallas_call(lambda *refs: shift_kernel(segs, stations, *refs), out_sha...  5.96 us
    ppermute x3, starting transfers between devices, on_device(): lax.ppermute(phased, 'seg', [(i, (i + k * CORES) % segs) for i in range(s...  4.43 us
    pallas_call x1, Pallas kernels, own_part(): pl.pallas_call(lambda *refs: own_kernel(segs, *refs), out_shape=(jax.Shap...  4.35 us
  transfers between devices with their start and end apart: 6, of which 1 were waited for; matrix products, arithmetic and copies ran while one was open for 0% of the time, Pallas kernels for 14%

profile of v2, /device:TPU:1, one launch (start us, length us, event | category | flops | bytes accessed | tf_op | source)
XLA Modules:
  0.0 72.9 jit_solution(5232546655259975216)
XLA Ops:
  0.6 0.8 %copy.4.refs_1_ = s32[8,4]{1,0:T(8,128)S(1)} copy(s32[8,4]{0,1:T(4,128)} %param.3) | data formatting | bytes 256 | tf_op args[1]
  1.4 0.0 copy-start
  1.4 0.8 %copy-done = bf16[16,2048]{1,0:T(8,128)(2,1)S(1)} copy-done((bf16[16,2048]{1,0:T(8,128)(2,1)S(1)}, bf16[16,2048]{1,0:T(8,128)(2,1)}, u32[]{:S(2)}) %copy-start) | copy-done | bytes 65560
  2.2 1.9 %prepare.1 = (bf16[16,2048]{1,0:T(8,128)(2,1)S(1)}, bf16[512,512]{1,0:T(8,128)(2,1)}) custom-call(bf16[16,2048]{1,0:T(8,128)(2,1)S(1)} %copy-done, s32[8,4]{1,0:T(8,128)S(1)} %copy.4.refs_1_), custom_call_target="tpu_custom_call" | custom-call | flops 104857600 | bytes 2097152 | tf_op jit(solution)/shard_map/prepare/pallas_call | solution.py:110
  4.1 3.3 %collective-permute-start.2 = (bf16[16,2048]{1,0:T(8,128)(2,1)S(1)}, bf16[16,2048]{1,0:T(8,128)(2,1)S(1)}, u32[]{:S(2)}, u32[]{:S(2)}) collective-permute-start(bf16[16,2048]{1,0:T(8,128)(2,1)S(1)} %get-tuple-element.8), channel_id=1, source_target_pairs={{0,6},{1,7},{2,0},{3,1},{4,2},{5,3},{6,4},{7,5},{8,14},{9,15},{10,... | collective-permute-start | bytes 196616 | tf_op jit(solution)/shard_map/ppermute | solution.py:502
  7.4 0.5 collective-permute-start.1
  7.9 0.6 collective-permute-start
  8.5 11.3 %all-to-all-start = ((bf16[32,16,512]{2,1,0:T(8,128)(2,1)}), bf16[32,16,512]{2,1,0:T(8,128)(2,1)}, u32[]{:S(2)}, u32[]{:S(2)}) async-start(bf16[32,16,512]{2,1,0:T(8,128)(2,1)} %bitcast.1), calls=%async_computation | async-start | bytes 1048576 | tf_op jit(solution)/shard_map/all_to_all | solution.py:497
  19.9 0.0 collective-permute-done
  19.9 0.0 collective-permute-done.1
  19.9 0.0 collective-permute-done.2
  20.0 1.9 %collective-permute-start.3 = (bf16[64,2048]{1,0:T(8,128)(2,1)S(1)}, bf16[64,2048]{1,0:T(8,128)(2,1)S(1)}, u32[]{:S(2)}, u32[]{:S(2)}) collective-permute-start(bf16[64,2048]{1,0:T(8,128)(2,1)S(1)} %constant_dynamic-update-slice_fusion.refs_1_), channel_id=1, source_target_pairs={{0,1},{1,0},{2,3},{3,2},{4,5},{5,4},{6,7},{7,6},{8,9},{9,8},{10,11... | collective-permute-start | bytes 786440 | tf_op jit(solution)/shard_map/ppermute | solution.py:504
  21.8 13.2 %all-to-all-done = bf16[32,16,512]{2,1,0:T(8,128)(2,1)} async-done(((bf16[32,16,512]{2,1,0:T(8,128)(2,1)}), bf16[32,16,512]{2,1,0:T(8,128)(2,1)}, u32[]{:S(2)}, u32[]{:S(2)}) %all-to-all-start) | async-done | bytes 524320 | tf_op jit(solution)/shard_map/all_to_all | solution.py:497
  35.0 7.3 %all-to-all-start.1 = ((bf16[8,64,512]{2,1,0:T(8,128)(2,1)}), bf16[8,64,512]{2,1,0:T(8,128)(2,1)S(1)}, u32[]{:S(2)}, u32[]{:S(2)}) async-start(bf16[8,64,512]{2,1,0:T(8,128)(2,1)} %bitcast.2), calls=%async_computation.1 | async-start | bytes 1048576 | tf_op jit(solution)/shard_map/all_to_all | solution.py:499
  42.3 0.0 collective-permute-done.3.refs_2_
  42.3 4.4 %own.1 = (bf16[16,2048]{1,0:T(8,128)(2,1)}, f32[8,256,128]{2,1,0:T(8,128)S(1)}) custom-call(s32[1]{0:T(128)} %bitcast.refs_0_, bf16[64,2048]{1,0:T(8,128)(2,1)S(1)} %constant_dynamic-update-slice_fusion.refs_1_, bf16[64,2048]{1,0:T(8,128)(2,1)S(1)} %collective-permute-done.3.refs_2_), custom_call_target="tpu_custom_call" | custom-call | flops 2097152000 | bytes 4194304 | tf_op jit(solution)/shard_map/own/pallas_call | solution.py:324
  46.6 6.0 %shift.1 = (bf16[8192,1024]{1,0:T(8,128)(2,1)S(1)}, bf16[256,1024]{1,0:T(8,128)(2,1)S(1)}) custom-call(f32[8,256,128]{2,1,0:T(8,128)S(1)} %get-tuple-element.11.refs_0_), custom_call_target="tpu_custom_call" | custom-call | flops 2097152000 | bytes 18874368 | tf_op jit(solution)/shard_map/shift/pallas_call | solution.py:368
  52.6 0.0 copy-start.1
  52.6 5.7 %copy-done.1 = bf16[8192,1024]{1,0:T(8,128)(2,1)} copy-done((bf16[8192,1024]{1,0:T(8,128)(2,1)}, bf16[8192,1024]{1,0:T(8,128)(2,1)S(1)}, u32[]{:S(2)}) %copy-start.1) | copy-done | bytes 16777240
  58.4 0.0 all-to-all-done.1
  58.4 14.5 %correlate.1 = bf16[256,512]{1,0:T(8,128)(2,1)} custom-call(bf16[512,512]{1,0:T(8,128)(2,1)S(1)} %bitcast.5, bf16[8192,1024]{1,0:T(8,128)(2,1)} %copy-done.1, bf16[256,1024]{1,0:T(8,128)(2,1)S(1)} %get-tuple-element.13.refs_2_), custom_call_target="tpu_custom_call" | custom-call | flops 6291456000 | bytes 20971520 | tf_op jit(solution)/shard_map/correlate/pallas_call | solution.py:466
  (4 shorter events, 0.0 us)
Async XLA Ops:
  1.4 0.8 %copy-start = (bf16[16,2048]{1,0:T(8,128)(2,1)S(1)}, bf16[16,2048]{1,0:T(8,128)(2,1)}, u32[]{:S(2)}) copy-start(bf16[16,2048]{1,0:T(8,128)(2,1)} %refs_0_.1) | copy-start | bytes 196612
  4.1 15.8 %collective-permute-start.2 = (bf16[16,2048]{1,0:T(8,128)(2,1)S(1)}, bf16[16,2048]{1,0:T(8,128)(2,1)S(1)}, u32[]{:S(2)}, u32[]{:S(2)}) collective-permute-start(bf16[16,2048]{1,0:T(8,128)(2,1)S(1)} %get-tuple-element.8), channel_id=1, source_target_pairs={{0,6},{1,7},{2,0},{3,1},{4,2},{5,3},{6,4},{7,5},{8,14},{9,15},{10,... | collective-permute-start | bytes 196616 | tf_op jit(solution)/shard_map/ppermute | solution.py:502
  7.4 12.5 %collective-permute-start.1 = (bf16[16,2048]{1,0:T(8,128)(2,1)S(1)}, bf16[16,2048]{1,0:T(8,128)(2,1)S(1)}, u32[]{:S(2)}, u32[]{:S(2)}) collective-permute-start(bf16[16,2048]{1,0:T(8,128)(2,1)S(1)} %get-tuple-element.8), channel_id=1, source_target_pairs={{0,4},{1,5},{2,6},{3,7},{4,0},{5,1},{6,2},{7,3},{8,12},{9,13},{10,... | collective-permute-start | bytes 196616 | tf_op jit(solution)/shard_map/ppermute | solution.py:502
  7.9 12.0 %collective-permute-start = (bf16[16,2048]{1,0:T(8,128)(2,1)S(1)}, bf16[16,2048]{1,0:T(8,128)(2,1)S(1)}, u32[]{:S(2)}, u32[]{:S(2)}) collective-permute-start(bf16[16,2048]{1,0:T(8,128)(2,1)S(1)} %get-tuple-element.8), channel_id=1, source_target_pairs={{0,2},{1,3},{2,4},{3,5},{4,6},{5,7},{6,0},{7,1},{8,10},{9,11},{10,... | collective-permute-start | bytes 196616 | tf_op jit(solution)/shard_map/ppermute | solution.py:502
  8.5 26.5 %all-to-all-start = ((bf16[32,16,512]{2,1,0:T(8,128)(2,1)}), bf16[32,16,512]{2,1,0:T(8,128)(2,1)}, u32[]{:S(2)}, u32[]{:S(2)}) async-start(bf16[32,16,512]{2,1,0:T(8,128)(2,1)} %bitcast.1), calls=%async_computation | async-start | bytes 1048576 | tf_op jit(solution)/shard_map/all_to_all | solution.py:497
  20.0 22.3 %collective-permute-start.3 = (bf16[64,2048]{1,0:T(8,128)(2,1)S(1)}, bf16[64,2048]{1,0:T(8,128)(2,1)S(1)}, u32[]{:S(2)}, u32[]{:S(2)}) collective-permute-start(bf16[64,2048]{1,0:T(8,128)(2,1)S(1)} %constant_dynamic-update-slice_fusion.refs_1_), channel_id=1, source_target_pairs={{0,1},{1,0},{2,3},{3,2},{4,5},{5,4},{6,7},{7,6},{8,9},{9,8},{10,11... | collective-permute-start | bytes 786440 | tf_op jit(solution)/shard_map/ppermute | solution.py:504
  35.0 23.4 %all-to-all-start.1 = ((bf16[8,64,512]{2,1,0:T(8,128)(2,1)}), bf16[8,64,512]{2,1,0:T(8,128)(2,1)S(1)}, u32[]{:S(2)}, u32[]{:S(2)}) async-start(bf16[8,64,512]{2,1,0:T(8,128)(2,1)} %bitcast.2), calls=%async_computation.1 | async-start | bytes 1048576 | tf_op jit(solution)/shard_map/all_to_all | solution.py:499
  52.6 5.7 %copy-start.1 = (bf16[8192,1024]{1,0:T(8,128)(2,1)}, bf16[8192,1024]{1,0:T(8,128)(2,1)S(1)}, u32[]{:S(2)}) copy-start(bf16[8192,1024]{1,0:T(8,128)(2,1)S(1)} %get-tuple-element.12.refs_1_) | copy-start | bytes 50331652

commit v3 on v2

--- a/solution.py
+++ b/solution.py
@@ -15,6 +15,7 @@
 
 PH = 16
 LANES = 128
+FINE = 32
 CORES = 2
 GROUP = 4
 F32 = jnp.float32
@@ -54,9 +55,29 @@
     return jnp.where(hit, 1.0, 0.0).astype(BF16)
 
 
+def gather_back():
+    shape = (LANES, PH * LANES)
+    target, source = iota(shape, 0), iota(shape, 1)
+    lane = source % LANES
+    place = FINE // PH * (lane % (LANES // 2)) + lane // (LANES // 2)
+    hit = (source // LANES == target % PH) & (place == target // PH)
+    return jnp.where(hit, 1.0, 0.0).astype(BF16)
+
+
+def fold(trace_ref, scale, segs, put):
+    rows = trace_ref.shape[1] // segs
+    low = iota((rows, LANES), 1) < LANES // 2
+    for p in range(PH):
+        for s in range(segs // 2):
+            first = trace_ref[p, 2 * s * rows : (2 * s + 1) * rows, :] * scale
+            second = trace_ref[p, (2 * s + 1) * rows : (2 * s + 2) * rows, :] * scale
+            put(p, s, jnp.where(low, first, pltpu.roll(second, LANES // 2, 1)).astype(BF16))
+            put(p + PH, s, jnp.where(low, pltpu.roll(first, LANES // 2, 1), second).astype(BF16))
+
+
 def prepare_kernel(owner_count, records_ref, owners_ref, phased_ref, slots_ref):
     stations, length = records_ref.shape
-    blocks, dests = owners_ref.shape
+    dests, blocks = owners_ref.shape
     per_tile = LANES // PH
     tiles = jnp.concatenate(
         [records_ref[:, t * LANES : (t + 1) * LANES] for t in range(length // LANES)], axis=0
@@ -80,7 +101,7 @@
     k_of, column = iota((blocks, width), 0), iota((blocks, width), 1)
     expand = jnp.where(column % stations // BS == k_of, 1.0, 0.0)
     named = lax.dot_general(
-        owners_ref[...].astype(F32), expand, (((0,), (0,)), ((), ())), preferred_element_type=F32
+        owners_ref[...].astype(F32), expand, (((1,), (0,)), ((), ())), preferred_element_type=F32
     )
     row, col = iota((rows, width), 0), iota((rows, width), 1)
     owner = (row // (high * SLOTS * BS)).astype(F32)
@@ -200,7 +221,8 @@
     n, k = iota((LANES, LANES), 0), iota((LANES, LANES), 1)
     cosine, sine = cos_sin(n * k, LANES)
     table = jnp.concatenate([cosine, sine], axis=1).astype(BF16)
-    back = jnp.concatenate([cosine, sine], axis=0).astype(BF16)
+    folded = FINE // PH * (k % (LANES // 2)) + k // (LANES // 2)
+    back = jnp.concatenate(cos_sin(n * folded, LANES), axis=0).astype(BF16)
     turn_cos, turn_sin = cos_sin(iota((PH, LANES), 0) * iota((PH, LANES), 1), length)
     for p in range(PH):
         y_ref[p] = dot(x_ref[p], table)
@@ -297,23 +319,21 @@
                     i * stations : (i + 1) * stations, p * LANES : (p + 1) * LANES
                 ]
     scale = whiten(x_ref, y_ref, f_ref, sum_ref, trace_ref, segs)
-    for p in range(PH):
-        for s in range(segs):
-            tile = trace_ref[p, s * stations : (s + 1) * stations, :]
-            phase_ref[s, (PH - 1 - p) * stations : (PH - p) * stations, :] = (
-                (tile * scale).astype(BF16).astype(F32)
-            )
+    def put(p, s, tile):
+        phase_ref[s, (FINE - 1 - p) * stations : (FINE - p) * stations, :] = tile.astype(F32)
+
+    fold(trace_ref, scale, segs, put)
     mine = pl.ds(pl.multiple_of(me_ref[0] * stations, stations), stations)
     tiles = [trace_ref[p, mine, :] * scale for p in range(PH)]
     moved = []
     for t in range(length // LANES):
-        turn = (LANES - per_tile * t) % LANES
+        turn = (LANES - per_tile // 2 * t) % LANES
         moved.append(
             jnp.concatenate(
                 [(pltpu.roll(x, turn, 1) if turn else x).astype(BF16) for x in tiles], axis=1
             )
         )
-    natural = dot_t(jnp.concatenate(moved, axis=0), spread()).astype(BF16)
+    natural = dot_t(jnp.concatenate(moved, axis=0), gather_back()).astype(BF16)
     for t in range(length // LANES):
         white_ref[:, t * LANES : (t + 1) * LANES] = natural[t * stations : (t + 1) * stations]
 
@@ -325,7 +345,7 @@
         lambda *refs: own_kernel(segs, *refs),
         out_shape=(
             jax.ShapeDtypeStruct((stations, length), BF16),
-            jax.ShapeDtypeStruct((segs, PH * stations, LANES), F32),
+            jax.ShapeDtypeStruct((segs // 2, FINE * stations, LANES), F32),
         ),
         in_specs=[
             pl.BlockSpec(memory_space=pltpu.SMEM),
@@ -342,44 +362,69 @@
     )(me, near, far)
 
 
-def shift_kernel(segs, stations, phase_ref, shifted_ref, extra_ref):
-    count = LAGS // PH
-    total = segs * LANES
-    lane = iota((PH, total), 1)
-    mine = pl.ds(pl.program_id(0), PH, stride=stations)
-    block = jnp.concatenate([phase_ref[s, mine, :] for s in range(segs)], axis=1)
-    for i in range(-1, count):
-        m = i + 1 - count // 2
-        moved = pltpu.roll(block, m % total, 1) if m else block
-        if m > 0:
-            moved = jnp.where(lane >= m, moved, 0.0)
-        elif m < 0:
-            moved = jnp.where(lane < total + m, moved, 0.0)
-        moved = moved.astype(BF16)
-        if i < 0:
-            extra_ref[...] = moved
-        else:
-            shifted_ref[i * PH : (i + 1) * PH, :] = moved
-
-
-def shift(phases, segs):
-    stations = phases.shape[1] // PH
-    total = segs * LANES
+def shift_kernel(stations, phase_ref, shifted_hbm, extra_hbm, shifted_ref, extra_ref, sems):
+    count = LAGS // FINE
+    tiles = phase_ref.shape[0]
+    total = tiles * LANES
+    lane = iota((FINE, total), 1)
+
+    def copies(a):
+        to = shifted_hbm.at[pl.ds(pl.multiple_of(a * LAGS, LAGS), LAGS), :]
+        to_extra = extra_hbm.at[pl.ds(pl.multiple_of(a * FINE, FINE), FINE), :]
+        return (
+            pltpu.make_async_copy(shifted_ref.at[a], to, sems.at[0, a]),
+            pltpu.make_async_copy(extra_ref.at[a], to_extra, sems.at[1, a]),
+        )
+
+    def body(a, _):
+        block = jnp.concatenate(
+            [phase_ref[s, pl.ds(a, FINE, stride=stations), :] for s in range(tiles)], axis=1
+        )
+        for i in range(-1, count):
+            m = i + 1 - count // 2
+            moved = pltpu.roll(block, m % total, 1) if m else block
+            if m > 0:
+                moved = jnp.where(lane >= m, moved, 0.0)
+            elif m < 0:
+                moved = jnp.where(lane < total + m, moved, 0.0)
+            moved = moved.astype(BF16)
+            if i < 0:
+                extra_ref[a] = moved
+            else:
+                shifted_ref[a, i * FINE : (i + 1) * FINE, :] = moved
+        for copy in copies(a):
+            copy.start()
+        return 0
+
+    lax.fori_loop(0, stations, body, 0)
+
+    def finish(a, _):
+        for copy in copies(a):
+            copy.wait()
+        return 0
+
+    lax.fori_loop(0, stations, finish, 0)
+
+
+def shift(phases):
+    stations = phases.shape[1] // FINE
+    total = phases.shape[0] * LANES
     return pl.pallas_call(
-        lambda *refs: shift_kernel(segs, stations, *refs),
+        lambda *refs: shift_kernel(stations, *refs),
         out_shape=(
-            jax.ShapeDtypeStruct((stations * LAGS, total), BF16),
-            jax.ShapeDtypeStruct((stations * PH, total), BF16),
-        ),
-        grid=(stations,),
-        in_specs=[pl.BlockSpec(phases.shape, lambda a: (0, 0, 0))],
-        out_specs=[
-            pl.BlockSpec((LAGS, total), lambda a: (a, 0)),
-            pl.BlockSpec((PH, total), lambda a: (a, 0)),
+            pltpu.HBM((stations * LAGS, total), BF16),
+            pltpu.HBM((stations * FINE, total), BF16),
+        ),
+        in_specs=[pl.BlockSpec(memory_space=pltpu.VMEM)],
+        out_specs=[pl.BlockSpec(memory_space=pltpu.HBM)] * 2,
+        scratch_shapes=[
+            pltpu.VMEM((stations, LAGS, total), BF16),
+            pltpu.VMEM((stations, FINE, total), BF16),
+            pltpu.SemaphoreType.DMA((2, stations)),
         ],
         compiler_params=pltpu.CompilerParams(vmem_limit_bytes=16 * MIB),
         cost_estimate=pl.CostEstimate(
-            flops=2000 * MIB, bytes_accessed=18 * MIB, transcendentals=0
+            flops=2000 * MIB, bytes_accessed=9 * MIB, transcendentals=0
         ),
         name="shift",
     )(phases)
@@ -389,7 +434,7 @@
     segs, received_ref, shifted_hbm, extra_hbm,
     out_ref,
     x_ref, y_ref, f_ref, sum_ref, trace_ref, phase_ref, edge_ref, total_ref,
-    shifted_ref, extra_ref, sems,
+    shifted_ref, extra_ref, even_ref, odd_ref, sems,
 ):
     rows = x_ref.shape[1]
     received = rows // segs
@@ -415,45 +460,55 @@
                 p % GROUP * LANES : (p % GROUP + 1) * LANES,
             ]
     scale = whiten(x_ref, y_ref, f_ref, sum_ref, trace_ref, segs)
-    for p in range(PH):
-        for s in range(segs):
-            tile = trace_ref[p, s * received : (s + 1) * received, :]
-            phase_ref[
-                p * received : (p + 1) * received, s * LANES : (s + 1) * LANES
-            ] = (tile * scale).astype(BF16)
+
+    def put(p, s, tile):
+        phase_ref[p * received : (p + 1) * received, s * LANES : (s + 1) * LANES] = tile
+
+    fold(trace_ref, scale, segs, put)
     copies[0].wait()
     edge = dot_t(phase_ref[...], extra_ref[...])
-    width = stations * PH
-    lag = iota((received, width), 1) % PH
+    width = stations * FINE
+    lag = iota((received, width), 1) % FINE
     sums = jnp.zeros((received, width), F32)
-    for p in range(PH):
+    for p in range(FINE):
         block = edge[p * received : (p + 1) * received]
-        turn = (p + 1 - PH) % width
+        turn = (p + 1 - FINE) % width
         block = pltpu.roll(block, turn, 1) if turn else block
         sums = sums + jnp.where(lag <= p, block, 0.0)
     edge_ref[...] = sums
     lane = iota((received, LAGS), 1)
     norm = 1.0 / math.sqrt(segs * PH * LANES)
 
-    def body(a, _):
+    def multiply(a):
         block = shifted_hbm.at[pl.ds(pl.multiple_of(a * LAGS, LAGS), LAGS), :]
         pltpu.make_async_copy(block, shifted_ref.at[a], sems.at[a]).wait()
-        product = dot_t(phase_ref[...], shifted_ref[a])
-        first = pltpu.roll(edge_ref[...], (stations - a) * PH, 1)
-        if width < LAGS:
-            first = jnp.concatenate([first, jnp.zeros((received, LAGS - width), F32)], axis=1)
-        sums = jnp.where(lane < PH, first, 0.0)
-        for p in range(PH):
-            block = pltpu.roll(product[p * received : (p + 1) * received], p + 1, 1)
+        return dot_t(phase_ref[...], shifted_ref[a])
+
+    def combine(a, product_ref):
+        first = pltpu.roll(edge_ref[...], (stations - a) * FINE, 1)
+        sums = jnp.where(lane < FINE, first[:, :LAGS], 0.0)
+        for p in range(FINE):
+            block = pltpu.roll(product_ref[p * received : (p + 1) * received], p + 1, 1)
             sums = sums + jnp.where(lane > p, block, 0.0)
         sums = sums * norm
         for c in range(LAGS // LANES):
             total_ref[c, pl.ds(a, received, stride=stations), :] = sums[
                 :, c * LANES : (c + 1) * LANES
             ]
+
+    even_ref[...] = multiply(0)
+
+    def body(i, _):
+        odd_ref[...] = multiply(2 * i + 1)
+        combine(2 * i, even_ref)
+        even_ref[...] = multiply(2 * i + 2)
+        combine(2 * i + 1, odd_ref)
         return 0
 
-    lax.fori_loop(0, stations, body, 0)
+    lax.fori_loop(0, stations // 2 - 1, body, 0)
+    odd_ref[...] = multiply(stations - 1)
+    combine(stations - 2, even_ref)
+    combine(stations - 1, odd_ref)
     for c in range(LAGS // LANES):
         out_ref[:, c * LANES : (c + 1) * LANES] = total_ref[c].astype(BF16)
 
@@ -462,23 +517,25 @@
     rows = received.shape[0] // (PH // GROUP)
     count = rows // segs
     stations = shifted.shape[0] // LAGS
-    total = segs * LANES
+    total = shifted.shape[1]
     return pl.pallas_call(
         lambda *refs: correlate_kernel(segs, *refs),
         out_shape=jax.ShapeDtypeStruct((count * stations, LAGS), BF16),
         in_specs=[
             pl.BlockSpec(memory_space=pltpu.VMEM),
-            pl.BlockSpec(memory_space=pl.ANY),
-            pl.BlockSpec(memory_space=pl.ANY),
+            pl.BlockSpec(memory_space=pltpu.HBM),
+            pl.BlockSpec(memory_space=pltpu.HBM),
         ],
         out_specs=pl.BlockSpec(memory_space=pltpu.VMEM),
         scratch_shapes=[
             *whiten_scratch(rows),
-            pltpu.VMEM((count * PH, total), BF16),
-            pltpu.VMEM((count, stations * PH), F32),
+            pltpu.VMEM((count * FINE, total), BF16),
+            pltpu.VMEM((count, stations * FINE), F32),
             pltpu.VMEM((LAGS // LANES, count * stations, LANES), F32),
             pltpu.VMEM((stations, LAGS, total), BF16),
-            pltpu.VMEM((stations * PH, total), BF16),
+            pltpu.VMEM((stations * FINE, total), BF16),
+            pltpu.VMEM((count * FINE, LAGS), F32),
+            pltpu.VMEM((count * FINE, LAGS), F32),
             pltpu.SemaphoreType.DMA((stations + 1,)),
         ],
         compiler_params=pltpu.CompilerParams(vmem_limit_bytes=48 * MIB),
@@ -486,17 +543,20 @@
             flops=6000 * MIB, bytes_accessed=20 * MIB, transcendentals=0
         ),
         name="correlate",
-    )(received, shifted, extra)
+    )(
+        received,
+        pltpu.with_memory_space_constraint(shifted, pltpu.HBM),
+        pltpu.with_memory_space_constraint(extra, pltpu.HBM),
+    )
 
 
 def on_device(records, owners):
     stations, length = records.shape
     segs, sources = lax.axis_size("seg"), lax.axis_size("sta")
-    phased, slots = prepare(records, owners, sources)
+    phased, slots = prepare(records, owners.T, sources)
     slots = slots.reshape(sources, -1, GROUP * LANES)
     passing = lax.all_to_all(slots, "sta", 0, 0, tiled=True)
     passing = passing.reshape(segs, -1, GROUP * LANES)
-    received = lax.all_to_all(passing, "seg", 0, 0, tiled=True).reshape(-1, GROUP * LANES)
     near = [phased]
     for k in range(1, segs // CORES):
         near.append(lax.ppermute(phased, "seg", [(i, (i + k * CORES) % segs) for i in range(segs)]))
@@ -504,7 +564,9 @@
     far = lax.ppermute(near, "seg", [(i, i ^ 1) for i in range(segs)])
     me = lax.axis_index("seg").reshape(1)
     whitened, phases = own_part(me, near, far, segs)
-    shifted, extra = shift(phases, segs)
+    shifted, extra = shift(phases)
+    passing, shifted, extra = lax.optimization_barrier((passing, shifted, extra))
+    received = lax.all_to_all(passing, "seg", 0, 0, tiled=True).reshape(-1, GROUP * LANES)
     result = correlate(received, shifted, extra, segs)
     return whitened, result.reshape(-1, stations, LAGS)
 

time: 73.2 us -> 64.6 us (0.88)
  blocking collectives: 0 us -> 16.4 us
  waiting for transfers between devices: 13.2 us -> 3.75 us
  starting transfers between devices: 24.9 us -> 17.5 us
  local copies, waits for them, and re-layouts: 7.35 us -> 1.54 us
  Pallas kernels: 26.7 us -> 24.4 us
    all_to_all x0 -> x1, blocking collectives: none -> 16.4 us  [on_device(): lax.all_to_all(passing, 'seg', 0, 0, tiled=True).reshape(-1, GROUP * LANES)]
    all_to_all x1, waiting for transfers between devices: 13.2 us -> 2.58 us  [on_device(): passing = lax.all_to_all(slots, 'sta', 0, 0, tiled=True)]
    all_to_all x1 -> x0, starting transfers between devices: 7.28 us -> none  [on_device(): lax.all_to_all(passing, 'seg', 0, 0, tiled=True).reshape(-1, GROUP * LANES)]
    unnamed x8 -> x7, local copies, waits for them, and re-layouts: 7.35 us -> 1.53 us
    pallas_call x1, Pallas kernels: 14.5 us -> 13 us  [correlate(): pl.pallas_call(lambda *refs: correlate_kernel(segs, *refs), out_shape=jax...]
    ppermute x1, waiting for transfers between devices: 0.01 us -> 1.16 us  [on_device(): far = lax.ppermute(near, 'seg', [(i, i ^ 1) for i in range(segs)])]
    pallas_call x1, Pallas kernels: 5.96 us -> 4.92 us  [shift(): pl.pallas_call(lambda *refs: shift_kernel(stations, *refs), out_shape=(pl...]
  transfers between devices with their start and end apart: 6 -> 5, of which waited for: 1 -> 2; matrix products, arithmetic and copies ran while one was open for 0% -> 0% of each run, Pallas kernels for 14% -> 15%
where the time goes in v3:
time: 64.6 us; the launch traced here: 64.3 us
  Pallas kernels  24.4 us (38%)
  starting transfers between devices  17.5 us (27%)
  blocking collectives  16.4 us (25%)
  waiting for transfers between devices  3.75 us (6%)
  local copies, waits for them, and re-layouts  1.54 us (2%)
  between operations  0.71 us (1%)
    all_to_all x1, blocking collectives, on_device(): lax.all_to_all(passing, 'seg', 0, 0, tiled=True).reshape(-1, GROUP * LANES)  16.4 us
    pallas_call x1, Pallas kernels, correlate(): pl.pallas_call(lambda *refs: correlate_kernel(segs, *refs), out_shape=jax...  13 us
    all_to_all x1, starting transfers between devices, on_device(): passing = lax.all_to_all(slots, 'sta', 0, 0, tiled=True)  11.2 us
    pallas_call x1, Pallas kernels, shift(): pl.pallas_call(lambda *refs: shift_kernel(stations, *refs), out_shape=(pl...  4.92 us
    pallas_call x1, Pallas kernels, own_part(): pl.pallas_call(lambda *refs: own_kernel(segs, *refs), out_shape=(jax.Shap...  4.52 us
    ppermute x3, starting transfers between devices, on_device(): lax.ppermute(phased, 'seg', [(i, (i + k * CORES) % segs) for i in range(s...  4.43 us
    all_to_all x1, waiting for transfers between devices, on_device(): passing = lax.all_to_all(slots, 'sta', 0, 0, tiled=True)  2.58 us
    pallas_call x1, Pallas kernels, prepare(): pl.pallas_call(lambda *refs: prepare_kernel(owner_count, *refs), out_shap...  1.89 us
  transfers between devices with their start and end apart: 5, of which 2 were waited for; matrix products, arithmetic and copies ran while one was open for 0% of the time, Pallas kernels for 15%

profile of v3, /device:TPU:1, one launch (start us, length us, event | category | flops | bytes accessed | tf_op | source)
XLA Modules:
  0.0 64.3 jit_solution(17259266031809074778)
XLA Ops:
  0.6 0.0 copy-start
  0.6 0.8 %copy-done = bf16[16,2048]{1,0:T(8,128)(2,1)S(1)} copy-done((bf16[16,2048]{1,0:T(8,128)(2,1)S(1)}, bf16[16,2048]{1,0:T(8,128)(2,1)}, u32[]{:S(2)}) %copy-start) | copy-done | bytes 65560
  1.5 0.0 copy-start.1
  1.5 0.7 %copy-done.1 = s32[8,4]{0,1:T(4,128)S(1)} copy-done((s32[8,4]{0,1:T(4,128)S(1)}, s32[8,4]{0,1:T(4,128)}, u32[]{:S(2)}) %copy-start.1) | copy-done | bytes 152
  2.2 1.9 %prepare.1 = (bf16[16,2048]{1,0:T(8,128)(2,1)S(1)}, bf16[512,512]{1,0:T(8,128)(2,1)}) custom-call(bf16[16,2048]{1,0:T(8,128)(2,1)S(1)} %copy-done, s32[4,8]{1,0:T(4,128)S(1)} %bitcast.7), custom_call_target="tpu_custom_call" | custom-call | flops 104857600 | bytes 2097152 | tf_op jit(solution)/shard_map/prepare/pallas_call | solution.py:131
  4.0 3.3 %collective-permute-start.2 = (bf16[16,2048]{1,0:T(8,128)(2,1)S(1)}, bf16[16,2048]{1,0:T(8,128)(2,1)S(1)}, u32[]{:S(2)}, u32[]{:S(2)}) collective-permute-start(bf16[16,2048]{1,0:T(8,128)(2,1)S(1)} %get-tuple-element.11), channel_id=1, source_target_pairs={{0,6},{1,7},{2,0},{3,1},{4,2},{5,3},{6,4},{7,5},{8,14},{9,15},{10,... | collective-permute-start | bytes 196616 | tf_op jit(solution)/shard_map/ppermute | solution.py:562
  7.3 0.5 collective-permute-start.1
  7.9 0.6 collective-permute-start
  8.5 11.2 %all-to-all-start = ((bf16[32,16,512]{2,1,0:T(8,128)(2,1)}), bf16[32,16,512]{2,1,0:T(8,128)(2,1)S(1)}, u32[]{:S(2)}, u32[]{:S(2)}) async-start(bf16[32,16,512]{2,1,0:T(8,128)(2,1)} %bitcast.2), calls=%async_computation | async-start | bytes 1048576 | tf_op jit(solution)/shard_map/all_to_all | solution.py:558
  19.7 0.0 collective-permute-done
  19.7 0.0 collective-permute-done.1
  19.8 0.0 collective-permute-done.2
  19.8 1.9 %collective-permute-start.3 = (bf16[64,2048]{1,0:T(8,128)(2,1)S(1)}, bf16[64,2048]{1,0:T(8,128)(2,1)S(1)}, u32[]{:S(2)}, u32[]{:S(2)}) collective-permute-start(bf16[64,2048]{1,0:T(8,128)(2,1)S(1)} %constant_dynamic-update-slice_fusion.refs_1_), channel_id=1, source_target_pairs={{0,1},{1,0},{2,3},{3,2},{4,5},{5,4},{6,7},{7,6},{8,9},{9,8},{10,11... | collective-permute-start | bytes 786440 | tf_op jit(solution)/shard_map/ppermute | solution.py:564
  21.7 1.2 %collective-permute-done.3.refs_2_ = bf16[64,2048]{1,0:T(8,128)(2,1)S(1)} collective-permute-done((bf16[64,2048]{1,0:T(8,128)(2,1)S(1)}, bf16[64,2048]{1,0:T(8,128)(2,1)S(1)}, u32[]{:S(2)}, u32[]{:S(2)}) %collective-permute-start.3) | collective-permute-done | bytes 262176 | tf_op jit(solution)/shard_map/ppermute | solution.py:564
  22.8 4.5 %own.1 = (bf16[16,2048]{1,0:T(8,128)(2,1)}, f32[4,512,128]{2,1,0:T(8,128)S(1)}) custom-call(s32[1]{0:T(128)} %bitcast.refs_0_, bf16[64,2048]{1,0:T(8,128)(2,1)S(1)} %constant_dynamic-update-slice_fusion.refs_1_, bf16[64,2048]{1,0:T(8,128)(2,1)S(1)} %collective-permute-done.3.refs_2_), custom_call_target="tpu_custom_call" | custom-call | flops 2097152000 | bytes 4194304 | tf_op jit(solution)/shard_map/own/pallas_call | solution.py:344
  27.3 4.9 %shift.1 = (bf16[8192,512]{1,0:T(8,128)(2,1)}, bf16[512,512]{1,0:T(8,128)(2,1)}) custom-call(f32[4,512,128]{2,1,0:T(8,128)S(1)} %get-tuple-element.14.refs_0_), custom_call_target="tpu_custom_call" | custom-call | flops 2097152000 | bytes 9437184 | tf_op jit(solution)/shard_map/shift/pallas_call | solution.py:412
  32.3 2.6 %all-to-all-done = bf16[32,16,512]{2,1,0:T(8,128)(2,1)S(1)} async-done(((bf16[32,16,512]{2,1,0:T(8,128)(2,1)}), bf16[32,16,512]{2,1,0:T(8,128)(2,1)S(1)}, u32[]{:S(2)}, u32[]{:S(2)}) %all-to-all-start) | async-done | bytes 524320 | tf_op jit(solution)/shard_map/all_to_all | solution.py:558
  34.9 16.4 %all_to_all.10 = bf16[8,64,512]{2,1,0:T(8,128)(2,1)S(1)} all-to-all(bf16[8,64,512]{2,1,0:T(8,128)(2,1)S(1)} %bitcast.8), channel_id=1, replica_groups=mesh['sta'=32,'seg'=8] {'seg'}, dimensions={0} | all-to-all | bytes 1048576 | tf_op jit(solution)/shard_map/all_to_all | solution.py:569
  51.3 13.0 %correlate.1 = bf16[256,512]{1,0:T(8,128)(2,1)} custom-call(bf16[512,512]{1,0:T(8,128)(2,1)S(1)} %bitcast.6, bf16[8192,512]{1,0:T(8,128)(2,1)} %get-tuple-element.18.refs_1_, bf16[512,512]{1,0:T(8,128)(2,1)} %get-tuple-element.19.refs_2_), custom_call_target="tpu_custom_call" | custom-call | flops 6291456000 | bytes 20971520 | tf_op jit(solution)/shard_map/correlate/pallas_call | solution.py:521
  (4 shorter events, 0.0 us)
Async XLA Ops:
  0.6 0.8 %copy-start = (bf16[16,2048]{1,0:T(8,128)(2,1)S(1)}, bf16[16,2048]{1,0:T(8,128)(2,1)}, u32[]{:S(2)}) copy-start(bf16[16,2048]{1,0:T(8,128)(2,1)} %refs_0_.1) | copy-start | bytes 196612
  1.5 0.7 %copy-start.1 = (s32[8,4]{0,1:T(4,128)S(1)}, s32[8,4]{0,1:T(4,128)}, u32[]{:S(2)}) copy-start(s32[8,4]{0,1:T(4,128)} %param.3) | copy-start | bytes 388
  4.0 15.7 %collective-permute-start.2 = (bf16[16,2048]{1,0:T(8,128)(2,1)S(1)}, bf16[16,2048]{1,0:T(8,128)(2,1)S(1)}, u32[]{:S(2)}, u32[]{:S(2)}) collective-permute-start(bf16[16,2048]{1,0:T(8,128)(2,1)S(1)} %get-tuple-element.11), channel_id=1, source_target_pairs={{0,6},{1,7},{2,0},{3,1},{4,2},{5,3},{6,4},{7,5},{8,14},{9,15},{10,... | collective-permute-start | bytes 196616 | tf_op jit(solution)/shard_map/ppermute | solution.py:562
  7.3 12.4 %collective-permute-start.1 = (bf16[16,2048]{1,0:T(8,128)(2,1)S(1)}, bf16[16,2048]{1,0:T(8,128)(2,1)S(1)}, u32[]{:S(2)}, u32[]{:S(2)}) collective-permute-start(bf16[16,2048]{1,0:T(8,128)(2,1)S(1)} %get-tuple-element.11), channel_id=1, source_target_pairs={{0,4},{1,5},{2,6},{3,7},{4,0},{5,1},{6,2},{7,3},{8,12},{9,13},{10,... | collective-permute-start | bytes 196616 | tf_op jit(solution)/shard_map/ppermute | solution.py:562
  7.9 11.8 %collective-permute-start = (bf16[16,2048]{1,0:T(8,128)(2,1)S(1)}, bf16[16,2048]{1,0:T(8,128)(2,1)S(1)}, u32[]{:S(2)}, u32[]{:S(2)}) collective-permute-start(bf16[16,2048]{1,0:T(8,128)(2,1)S(1)} %get-tuple-element.11), channel_id=1, source_target_pairs={{0,2},{1,3},{2,4},{3,5},{4,6},{5,7},{6,0},{7,1},{8,10},{9,11},{10,... | collective-permute-start | bytes 196616 | tf_op jit(solution)/shard_map/ppermute | solution.py:562
  8.5 26.4 %all-to-all-start = ((bf16[32,16,512]{2,1,0:T(8,128)(2,1)}), bf16[32,16,512]{2,1,0:T(8,128)(2,1)S(1)}, u32[]{:S(2)}, u32[]{:S(2)}) async-start(bf16[32,16,512]{2,1,0:T(8,128)(2,1)} %bitcast.2), calls=%async_computation | async-start | bytes 1048576 | tf_op jit(solution)/shard_map/all_to_all | solution.py:558
  19.8 3.0 %collective-permute-start.3 = (bf16[64,2048]{1,0:T(8,128)(2,1)S(1)}, bf16[64,2048]{1,0:T(8,128)(2,1)S(1)}, u32[]{:S(2)}, u32[]{:S(2)}) collective-permute-start(bf16[64,2048]{1,0:T(8,128)(2,1)S(1)} %constant_dynamic-update-slice_fusion.refs_1_), channel_id=1, source_target_pairs={{0,1},{1,0},{2,3},{3,2},{4,5},{5,4},{6,7},{7,6},{8,9},{9,8},{10,11... | collective-permute-start | bytes 786440 | tf_op jit(solution)/shard_map/ppermute | solution.py:564

commit v4 on v3

--- a/solution.py
+++ b/solution.py
@@ -29,6 +29,10 @@
 
 def dot_t(a, b):
     return lax.dot_general(a, b, (((1,), (1,)), ((), ())), preferred_element_type=F32)
+
+
+def in_hbm(x):
+    return pltpu.with_memory_space_constraint(x, pltpu.HBM)
 
 
 def iota(shape, axis):
@@ -75,14 +79,24 @@
             put(p + PH, s, jnp.where(low, pltpu.roll(first, LANES // 2, 1), second).astype(BF16))
 
 
-def prepare_kernel(owner_count, records_ref, owners_ref, phased_ref, slots_ref):
+def prepare_kernel(
+    owner_count, records_hbm, owners_hbm, phased_ref, slots_ref, records_ref, owners_ref, sems
+):
+    loads = [
+        pltpu.make_async_copy(records_hbm, records_ref, sems.at[0]),
+        pltpu.make_async_copy(owners_hbm, owners_ref, sems.at[1]),
+    ]
+    for load in loads:
+        load.start()
     stations, length = records_ref.shape
     dests, blocks = owners_ref.shape
     per_tile = LANES // PH
+    one_hot = spread()
+    loads[0].wait()
     tiles = jnp.concatenate(
         [records_ref[:, t * LANES : (t + 1) * LANES] for t in range(length // LANES)], axis=0
     )
-    parts = dot(tiles, spread())
+    parts = dot(tiles, one_hot)
     phases = []
     for p in range(PH):
         total = None
@@ -100,6 +114,7 @@
     rows, width = owner_count * high * SLOTS * BS, high * stations
     k_of, column = iota((blocks, width), 0), iota((blocks, width), 1)
     expand = jnp.where(column % stations // BS == k_of, 1.0, 0.0)
+    loads[1].wait()
     named = lax.dot_general(
         owners_ref[...].astype(F32), expand, (((1,), (0,)), ((), ())), preferred_element_type=F32
     )
@@ -134,14 +149,19 @@
             jax.ShapeDtypeStruct((stations, length), BF16),
             jax.ShapeDtypeStruct((rows, GROUP * LANES), BF16),
         ),
-        in_specs=[pl.BlockSpec(memory_space=pltpu.VMEM)] * 2,
+        in_specs=[pl.BlockSpec(memory_space=pltpu.HBM)] * 2,
         out_specs=[pl.BlockSpec(memory_space=pltpu.VMEM)] * 2,
+        scratch_shapes=[
+            pltpu.VMEM(records.shape, records.dtype),
+            pltpu.VMEM(owners.shape, owners.dtype),
+            pltpu.SemaphoreType.DMA((2,)),
+        ],
         compiler_params=pltpu.CompilerParams(vmem_limit_bytes=16 * MIB),
         cost_estimate=pl.CostEstimate(
             flops=100 * MIB, bytes_accessed=2 * MIB, transcendentals=0
         ),
         name="prepare",
-    )(records, owners)
+    )(in_hbm(records), in_hbm(owners))
 
 
 def add(a, b):
@@ -250,7 +270,7 @@
         sum_ref[at, :] = total
         return 0
 
-    lax.fori_loop(0, rows // 8, forward, 0)
+    lax.fori_loop(0, rows // 8, forward, 0, unroll=4)
     amp = 2.0 * jnp.sum(seg_total(sum_ref[...], segs), axis=1, keepdims=True)
     level = WATER * amp / window + EPSILON
     sum_ref[...] = jnp.concatenate(
@@ -283,7 +303,7 @@
             y_ref[p, at, LANES:] = z[1]
         return 0
 
-    lax.fori_loop(0, rows // 8, inverse, 0)
+    lax.fori_loop(0, rows // 8, inverse, 0, unroll=4)
     energy = jnp.zeros((rows, LANES), F32)
     for p in range(PH):
         trace = dot(y_ref[p].astype(BF16), back) * (1.0 / length)
@@ -304,19 +324,22 @@
 
 
 def own_kernel(
-    segs, me_ref, near_ref, far_ref, white_ref, phase_ref, x_ref, y_ref, f_ref, sum_ref, trace_ref
+    segs, me_ref, *refs
 ):
+    pairs, refs = refs[: segs // CORES], refs[segs // CORES :]
+    white_ref, phase_ref, x_ref, y_ref, f_ref, sum_ref, trace_ref = refs
     rows, length = x_ref.shape[1], PH * LANES
     stations = rows // segs
     per_tile = LANES // PH
     me, chips = me_ref[0], segs // CORES
-    for i in range(chips):
-        chip = (me // CORES + chips - i) % chips
-        for ref, core in ((near_ref, me % CORES), (far_ref, 1 - me % CORES)):
+    for i, ref in enumerate(pairs):
+        chip = (lax.div(me, CORES) + chips - i) & (chips - 1)
+        for j in range(CORES):
+            core = (me + j) & (CORES - 1)
             at = pl.ds(pl.multiple_of((chip * CORES + core) * stations, stations), stations)
             for p in range(PH):
                 x_ref[p, at, :] = ref[
-                    i * stations : (i + 1) * stations, p * LANES : (p + 1) * LANES
+                    j * stations : (j + 1) * stations, p * LANES : (p + 1) * LANES
                 ]
     scale = whiten(x_ref, y_ref, f_ref, sum_ref, trace_ref, segs)
     def put(p, s, tile):
@@ -338,8 +361,8 @@
         white_ref[:, t * LANES : (t + 1) * LANES] = natural[t * stations : (t + 1) * stations]
 
 
-def own_part(me, near, far, segs):
-    rows, length = 2 * near.shape[0], near.shape[1]
+def own_part(me, pairs, segs):
+    rows, length = len(pairs) * pairs[0].shape[0], pairs[0].shape[1]
     stations = rows // segs
     return pl.pallas_call(
         lambda *refs: own_kernel(segs, *refs),
@@ -349,8 +372,7 @@
         ),
         in_specs=[
             pl.BlockSpec(memory_space=pltpu.SMEM),
-            pl.BlockSpec(memory_space=pltpu.VMEM),
-            pl.BlockSpec(memory_space=pltpu.VMEM),
+            *[pl.BlockSpec(memory_space=pltpu.VMEM)] * len(pairs),
         ],
         out_specs=[pl.BlockSpec(memory_space=pltpu.VMEM)] * 2,
         scratch_shapes=whiten_scratch(rows),
@@ -359,7 +381,7 @@
             flops=2000 * MIB, bytes_accessed=4 * MIB, transcendentals=0
         ),
         name="own",
-    )(me, near, far)
+    )(me, *pairs)
 
 
 def shift_kernel(stations, phase_ref, shifted_hbm, extra_hbm, shifted_ref, extra_ref, sems):
@@ -430,12 +452,15 @@
     )(phases)
 
 
-def correlate_kernel(
-    segs, received_ref, shifted_hbm, extra_hbm,
-    out_ref,
-    x_ref, y_ref, f_ref, sum_ref, trace_ref, phase_ref, edge_ref, total_ref,
-    shifted_ref, extra_ref, even_ref, odd_ref, sems,
-):
+def correlate_kernel(segs, me_ref, *refs):
+    chips = segs // CORES
+    near, (far_ref, shifted_hbm, extra_hbm, out_ref), refs = (
+        refs[:chips],
+        refs[chips : chips + 4],
+        refs[chips + 4 :],
+    )
+    x_ref, y_ref, f_ref, sum_ref, trace_ref, phase_ref, edge_ref, total_ref = refs[:8]
+    shifted_ref, extra_ref, even_ref, odd_ref, sems = refs[8:]
     rows = x_ref.shape[1]
     received = rows // segs
     stations = shifted_ref.shape[0]
@@ -447,15 +472,25 @@
         copy.start()
     high, unit_rows = PH // GROUP, SLOTS * BS
     per_seg = high * received
-    to, source = iota((per_seg, per_seg), 0), iota((per_seg, per_seg), 1)
+    to, at_row = iota((per_seg, per_seg), 0), iota((per_seg, per_seg), 1)
     wanted = (
         to % received // unit_rows * (high * unit_rows) + to // received * unit_rows
     ) + to % unit_rows
-    order = jnp.where(source == wanted, 1.0, 0.0).astype(BF16)
+    order = jnp.where(at_row == wanted, 1.0, 0.0).astype(BF16)
+    me = me_ref[0]
+    mine = me & (CORES - 1)
     for s in range(segs):
-        block = dot(order, received_ref[s * per_seg : (s + 1) * per_seg, :]).astype(BF16)
+        i = s // CORES
+        chip = (lax.div(me, CORES) + chips - i) & (chips - 1)
+        if s % CORES:
+            source, seg = far_ref[i], chip * CORES + 1 - mine
+        else:
+            source = near[i][(chip * CORES if i == 0 else 0) + mine]
+            seg = chip * CORES + mine
+        block = dot(order, source).astype(BF16)
+        at = pl.ds(pl.multiple_of(seg * received, received), received)
         for p in range(PH):
-            x_ref[p, s * received : (s + 1) * received, :] = block[
+            x_ref[p, at, :] = block[
                 p // GROUP * received : (p // GROUP + 1) * received,
                 p % GROUP * LANES : (p % GROUP + 1) * LANES,
             ]
@@ -513,8 +548,8 @@
         out_ref[:, c * LANES : (c + 1) * LANES] = total_ref[c].astype(BF16)
 
 
-def correlate(received, shifted, extra, segs):
-    rows = received.shape[0] // (PH // GROUP)
+def correlate(me, near, far, shifted, extra, segs):
+    rows = segs * far.shape[1] // (PH // GROUP)
     count = rows // segs
     stations = shifted.shape[0] // LAGS
     total = shifted.shape[1]
@@ -522,7 +557,8 @@
         lambda *refs: correlate_kernel(segs, *refs),
         out_shape=jax.ShapeDtypeStruct((count * stations, LAGS), BF16),
         in_specs=[
-            pl.BlockSpec(memory_space=pltpu.VMEM),
+            pl.BlockSpec(memory_space=pltpu.SMEM),
+            *[pl.BlockSpec(memory_space=pltpu.VMEM)] * (len(near) + 1),
             pl.BlockSpec(memory_space=pltpu.HBM),
             pl.BlockSpec(memory_space=pltpu.HBM),
         ],
@@ -544,30 +580,42 @@
         ),
         name="correlate",
     )(
-        received,
-        pltpu.with_memory_space_constraint(shifted, pltpu.HBM),
-        pltpu.with_memory_space_constraint(extra, pltpu.HBM),
+        me,
+        *near,
+        far,
+        in_hbm(shifted),
+        in_hbm(extra),
     )
 
 
 def on_device(records, owners):
     stations, length = records.shape
     segs, sources = lax.axis_size("seg"), lax.axis_size("sta")
+    chips = segs // CORES
+    me = lax.axis_index("seg")
+    chip = lax.div(me, jnp.int32(CORES))
+    along_x = [[(i, (i + k * CORES) % segs) for i in range(segs)] for k in range(chips)]
+    across = [(i, i ^ 1) for i in range(segs)]
     phased, slots = prepare(records, owners.T, sources)
     slots = slots.reshape(sources, -1, GROUP * LANES)
+    other = lax.ppermute(phased, "seg", across)
     passing = lax.all_to_all(slots, "sta", 0, 0, tiled=True)
     passing = passing.reshape(segs, -1, GROUP * LANES)
-    near = [phased]
-    for k in range(1, segs // CORES):
-        near.append(lax.ppermute(phased, "seg", [(i, (i + k * CORES) % segs) for i in range(segs)]))
-    near = jnp.concatenate(near, axis=0)
-    far = lax.ppermute(near, "seg", [(i, i ^ 1) for i in range(segs)])
-    me = lax.axis_index("seg").reshape(1)
-    whitened, phases = own_part(me, near, far, segs)
+    pair = jnp.concatenate([phased, other], axis=0)
+    pairs = [pair] + [lax.ppermute(pair, "seg", along_x[k]) for k in range(1, chips)]
+    whitened, phases = own_part(me.reshape(1), pairs, segs)
     shifted, extra = shift(phases)
     passing, shifted, extra = lax.optimization_barrier((passing, shifted, extra))
-    received = lax.all_to_all(passing, "seg", 0, 0, tiled=True).reshape(-1, GROUP * LANES)
-    result = correlate(received, shifted, extra, segs)
+    near = [passing]
+    for k in range(1, chips):
+        at = ((chip + k) & (chips - 1)) * CORES
+        block = lax.dynamic_slice_in_dim(passing, at, CORES, 0)
+        near.append(lax.ppermute(block, "seg", along_x[k]))
+    other_core = 1 - (me & (CORES - 1))
+    give = [lax.dynamic_slice_in_dim(passing, chip * CORES + other_core, 1, 0)]
+    give += [lax.dynamic_slice_in_dim(block, other_core, 1, 0) for block in near[1:]]
+    far = lax.ppermute(jnp.concatenate(give, axis=0), "seg", across)
+    result = correlate(me.reshape(1), near, far, shifted, extra, segs)
     return whitened, result.reshape(-1, stations, LAGS)
 
 

time: 64.6 us -> 63.3 us (0.980)
  blocking collectives: 16.4 us -> 0 us
  waiting for transfers between devices: 3.75 us -> 14.2 us
  starting transfers between devices: 17.5 us -> 23 us
  local copies, waits for them, and re-layouts: 1.54 us -> 0.07 us
    all_to_all x1 -> x0, blocking collectives: 16.4 us -> none  [on_device(): lax.all_to_all(passing, 'seg', 0, 0, tiled=True).reshape(-1, GROUP * LANES)]
    ppermute x4 -> x8, waiting for transfers between devices: 1.17 us -> 14.2 us  [the longest x3 7.18 us: on_device(): near.append(lax.ppermute(block, 'seg', along_x[k]))]
    ppermute x4 -> x8, starting transfers between devices: 6.31 us -> 11 us  [the longest x3 4.82 us: on_device(): lax.ppermute(pair, 'seg', along_x[k])]
    all_to_all x1, waiting for transfers between devices: 2.58 us -> 0.01 us  [on_device(): passing = lax.all_to_all(slots, 'sta', 0, 0, tiled=True)]
    unnamed x7 -> x1, local copies, waits for them, and re-layouts: 1.53 us -> 0.01 us
    pallas_call x1, Pallas kernels: 1.89 us -> 2.93 us  [prepare(): pl.pallas_call(lambda *refs: prepare_kernel(owner_count, *refs), out_shap...]
    all_to_all x1, starting transfers between devices: 11.2 us -> 12.1 us  [on_device(): passing = lax.all_to_all(slots, 'sta', 0, 0, tiled=True)]
  transfers between devices with their start and end apart: 5 -> 9, of which waited for: 2 -> 7; matrix products, arithmetic and copies ran while one was open for 0% -> 0% of each run, Pallas kernels for 15% -> 14%
where the time goes in v4:
time: 63.3 us; the launch traced here: 63.1 us
  Pallas kernels  24.9 us (39%)
  starting transfers between devices  23 us (36%)
  waiting for transfers between devices  14.2 us (22%)
  between operations  0.85 us (1%)
    pallas_call x1, Pallas kernels, correlate(): pl.pallas_call(lambda *refs: correlate_kernel(segs, *refs), out_shape=jax...  12.9 us
    all_to_all x1, starting transfers between devices, on_device(): passing = lax.all_to_all(slots, 'sta', 0, 0, tiled=True)  12.1 us
    ppermute x3, waiting for transfers between devices, on_device(): near.append(lax.ppermute(block, 'seg', along_x[k]))  7.18 us
    ppermute x3, waiting for transfers between devices, on_device(): lax.ppermute(pair, 'seg', along_x[k])  4.91 us
    pallas_call x1, Pallas kernels, shift(): pl.pallas_call(lambda *refs: shift_kernel(stations, *refs), out_shape=(pl...  4.89 us
    ppermute x3, starting transfers between devices, on_device(): lax.ppermute(pair, 'seg', along_x[k])  4.82 us
    pallas_call x1, Pallas kernels, own_part(): pl.pallas_call(lambda *refs: own_kernel(segs, *refs), out_shape=(jax.Shap...  4.23 us
    ppermute x3, starting transfers between devices, on_device(): near.append(lax.ppermute(block, 'seg', along_x[k]))  3.65 us
  transfers between devices with their start and end apart: 9, of which 7 were waited for; matrix products, arithmetic and copies ran while one was open for 0% of the time, Pallas kernels for 14%

profile of v4, /device:TPU:1, one launch (start us, length us, event | category | flops | bytes accessed | tf_op | source)
XLA Modules:
  0.0 63.1 jit_solution(11508115018354594225)
XLA Ops:
  0.6 2.9 %prepare.1 = (bf16[16,2048]{1,0:T(8,128)(2,1)S(1)}, bf16[512,512]{1,0:T(8,128)(2,1)}) custom-call(bf16[16,2048]{1,0:T(8,128)(2,1)} %refs_0_.1, s32[4,8]{1,0:T(4,128)} %bitcast.8), custom_call_target="tpu_custom_call" | custom-call | flops 104857600 | bytes 2097152 | tf_op jit(solution)/shard_map/prepare/pallas_call | solution.py:146
  3.6 12.1 %all-to-all-start = ((bf16[32,16,512]{2,1,0:T(8,128)(2,1)}), bf16[32,16,512]{2,1,0:T(8,128)(2,1)S(1)}, u32[]{:S(2)}, u32[]{:S(2)}) async-start(bf16[32,16,512]{2,1,0:T(8,128)(2,1)} %bitcast.2), calls=%async_computation | async-start | bytes 1048576 | tf_op jit(solution)/shard_map/all_to_all | solution.py:602
  15.6 1.0 %collective-permute-start = (bf16[16,2048]{1,0:T(8,128)(2,1)S(1)}, bf16[16,2048]{1,0:T(8,128)(2,1)S(1)}, u32[]{:S(2)}, u32[]{:S(2)}) collective-permute-start(bf16[16,2048]{1,0:T(8,128)(2,1)S(1)} %get-tuple-element.11), channel_id=1, source_target_pairs={{0,1},{1,0},{2,3},{3,2},{4,5},{5,4},{6,7},{7,6},{8,9},{9,8},{10,11... | collective-permute-start | bytes 196616 | tf_op jit(solution)/shard_map/ppermute | solution.py:601
  16.7 0.9 %collective-permute-done = bf16[16,2048]{1,0:T(8,128)(2,1)S(1)} collective-permute-done((bf16[16,2048]{1,0:T(8,128)(2,1)S(1)}, bf16[16,2048]{1,0:T(8,128)(2,1)S(1)}, u32[]{:S(2)}, u32[]{:S(2)}) %collective-permute-start) | collective-permute-done | bytes 65568 | tf_op jit(solution)/shard_map/ppermute | solution.py:601
  17.6 1.2 %collective-permute-start.1 = (bf16[32,2048]{1,0:T(8,128)(2,1)S(1)}, bf16[32,2048]{1,0:T(8,128)(2,1)S(1)}, u32[]{:S(2)}, u32[]{:S(2)}) collective-permute-start(bf16[32,2048]{1,0:T(8,128)(2,1)S(1)} %constant_dynamic-update-slice_fusion.refs_1_), channel_id=1, source_target_pairs={{0,2},{1,3},{2,4},{3,5},{4,6},{5,7},{6,0},{7,1},{8,10},{9,11},{10,... | collective-permute-start | bytes 393224 | tf_op jit(solution)/shard_map/ppermute | solution.py:605
  18.8 2.4 %collective-permute-start.2 = (bf16[32,2048]{1,0:T(8,128)(2,1)S(1)}, bf16[32,2048]{1,0:T(8,128)(2,1)S(1)}, u32[]{:S(2)}, u32[]{:S(2)}) collective-permute-start(bf16[32,2048]{1,0:T(8,128)(2,1)S(1)} %constant_dynamic-update-slice_fusion.refs_1_), channel_id=1, source_target_pairs={{0,4},{1,5},{2,6},{3,7},{4,0},{5,1},{6,2},{7,3},{8,12},{9,13},{10,... | collective-permute-start | bytes 393224 | tf_op jit(solution)/shard_map/ppermute | solution.py:605
  21.2 1.2 %collective-permute-start.3 = (bf16[32,2048]{1,0:T(8,128)(2,1)S(1)}, bf16[32,2048]{1,0:T(8,128)(2,1)S(1)}, u32[]{:S(2)}, u32[]{:S(2)}) collective-permute-start(bf16[32,2048]{1,0:T(8,128)(2,1)S(1)} %constant_dynamic-update-slice_fusion.refs_1_), channel_id=1, source_target_pairs={{0,6},{1,7},{2,0},{3,1},{4,2},{5,3},{6,4},{7,5},{8,14},{9,15},{10,... | collective-permute-start | bytes 393224 | tf_op jit(solution)/shard_map/ppermute | solution.py:605
  22.4 1.1 %collective-permute-done.1.refs_2_ = bf16[32,2048]{1,0:T(8,128)(2,1)S(1)} collective-permute-done((bf16[32,2048]{1,0:T(8,128)(2,1)S(1)}, bf16[32,2048]{1,0:T(8,128)(2,1)S(1)}, u32[]{:S(2)}, u32[]{:S(2)}) %collective-permute-start.1) | collective-permute-done | bytes 131104 | tf_op jit(solution)/shard_map/ppermute | solution.py:605
  23.5 3.8 %collective-permute-done.2.refs_3_ = bf16[32,2048]{1,0:T(8,128)(2,1)S(1)} collective-permute-done((bf16[32,2048]{1,0:T(8,128)(2,1)S(1)}, bf16[32,2048]{1,0:T(8,128)(2,1)S(1)}, u32[]{:S(2)}, u32[]{:S(2)}) %collective-permute-start.2) | collective-permute-done | bytes 131104 | tf_op jit(solution)/shard_map/ppermute | solution.py:605
  27.3 0.0 collective-permute-done.3.refs_4_
  27.3 4.2 %own.1 = (bf16[16,2048]{1,0:T(8,128)(2,1)}, f32[4,512,128]{2,1,0:T(8,128)S(1)}) custom-call(s32[1]{0:T(128)} %bitcast.refs_0_, bf16[32,2048]{1,0:T(8,128)(2,1)S(1)} %constant_dynamic-update-slice_fusion.refs_1_, bf16[32,2048]{1,0:T(8,128)(2,1)S(1)} %collective-permute-done.1.refs_2_, bf16[32,2048]{1,0:T(8,128)(2,1)S(1)} %collective-permute-done.2.refs_3_, ...), custom_call_target="tpu_custom_call" | custom-call | flops 2097152000 | bytes 4194304 | tf_op jit(solution)/shard_map/own/pallas_call | solution.py:367
  31.5 4.9 %shift.1 = (bf16[8192,512]{1,0:T(8,128)(2,1)}, bf16[512,512]{1,0:T(8,128)(2,1)}) custom-call(f32[4,512,128]{2,1,0:T(8,128)S(1)} %get-tuple-element.14.refs_0_), custom_call_target="tpu_custom_call" | custom-call | flops 2097152000 | bytes 9437184 | tf_op jit(solution)/shard_map/shift/pallas_call | solution.py:434
  36.4 0.0 all-to-all-done
  36.5 2.1 %collective-permute-start.6 = (bf16[2,64,512]{2,1,0:T(8,128)(2,1)S(1)}, bf16[2,64,512]{2,1,0:T(8,128)(2,1)S(1)}, u32[]{:S(2)}, u32[]{:S(2)}) collective-permute-start(bf16[2,64,512]{2,1,0:T(8,128)(2,1)S(1)} %get-tuple-element.20), channel_id=1, source_target_pairs={{0,6},{1,7},{2,0},{3,1},{4,2},{5,3},{6,4},{7,5},{8,14},{9,15},{10,... | collective-permute-start | bytes 393224 | tf_op jit(solution)/shard_map/ppermute | solution.py:613
  38.6 0.0 collective-permute-start.4
  38.6 1.5 %collective-permute-start.5 = (bf16[2,64,512]{2,1,0:T(8,128)(2,1)S(1)}, bf16[2,64,512]{2,1,0:T(8,128)(2,1)S(1)}, u32[]{:S(2)}, u32[]{:S(2)}) collective-permute-start(bf16[2,64,512]{2,1,0:T(8,128)(2,1)S(1)} %get-tuple-element.21), channel_id=1, source_target_pairs={{0,4},{1,5},{2,6},{3,7},{4,0},{5,1},{6,2},{7,3},{8,12},{9,13},{10,... | collective-permute-start | bytes 393224 | tf_op jit(solution)/shard_map/ppermute | solution.py:613
  40.2 0.4 collective-permute-done.6.refs_4_
  40.6 4.1 %collective-permute-done.5.refs_3_ = bf16[2,64,512]{2,1,0:T(8,128)(2,1)S(1)} collective-permute-done((bf16[2,64,512]{2,1,0:T(8,128)(2,1)S(1)}, bf16[2,64,512]{2,1,0:T(8,128)(2,1)S(1)}, u32[]{:S(2)}, u32[]{:S(2)}) %collective-permute-start.5) | collective-permute-done | bytes 131104 | tf_op jit(solution)/shard_map/ppermute | solution.py:613
  44.6 2.7 %collective-permute-done.4.refs_2_ = bf16[2,64,512]{2,1,0:T(8,128)(2,1)S(1)} collective-permute-done((bf16[2,64,512]{2,1,0:T(8,128)(2,1)S(1)}, bf16[2,64,512]{2,1,0:T(8,128)(2,1)S(1)}, u32[]{:S(2)}, u32[]{:S(2)}) %collective-permute-start.4) | collective-permute-done | bytes 131104 | tf_op jit(solution)/shard_map/ppermute | solution.py:613
  47.4 1.5 %collective-permute-start.7 = (bf16[4,64,512]{2,1,0:T(8,128)(2,1)S(1)}, bf16[4,64,512]{2,1,0:T(8,128)(2,1)S(1)}, u32[]{:S(2)}, u32[]{:S(2)}) collective-permute-start(bf16[4,64,512]{2,1,0:T(8,128)(2,1)S(1)} %pad_maximum_fusion), channel_id=1, source_target_pairs={{0,1},{1,0},{2,3},{3,2},{4,5},{5,4},{6,7},{7,6},{8,9},{9,8},{10,11... | collective-permute-start | bytes 786440 | tf_op jit(solution)/shard_map/ppermute | solution.py:617
  48.8 1.2 %collective-permute-done.7.refs_5_ = bf16[4,64,512]{2,1,0:T(8,128)(2,1)S(1)} collective-permute-done((bf16[4,64,512]{2,1,0:T(8,128)(2,1)S(1)}, bf16[4,64,512]{2,1,0:T(8,128)(2,1)S(1)}, u32[]{:S(2)}, u32[]{:S(2)}) %collective-permute-start.7) | collective-permute-done | bytes 262176 | tf_op jit(solution)/shard_map/ppermute | solution.py:617
  50.0 12.9 %correlate.1 = bf16[256,512]{1,0:T(8,128)(2,1)} custom-call(s32[1]{0:T(128)} %bitcast.refs_0_, bf16[8,64,512]{2,1,0:T(8,128)(2,1)S(1)} %bitcast.7, bf16[2,64,512]{2,1,0:T(8,128)(2,1)S(1)} %collective-permute-done.4.refs_2_, bf16[2,64,512]{2,1,0:T(8,128)(2,1)S(1)} %collective-permute-done.5.refs_3_, bf16[2,64,512]{2,1,0:T(8,128)(2,1)S(1)} %collective-permute-done.6.refs_4_, ...), custom_call_target="tpu_custom_call" | custom-call | flops 6291456000 | bytes 20971520 | tf_op jit(solution)/shard_map/correlate/pallas_call | solution.py:556
  (8 shorter events, 0.1 us)
Async XLA Ops:
  3.6 32.9 %all-to-all-start = ((bf16[32,16,512]{2,1,0:T(8,128)(2,1)}), bf16[32,16,512]{2,1,0:T(8,128)(2,1)S(1)}, u32[]{:S(2)}, u32[]{:S(2)}) async-start(bf16[32,16,512]{2,1,0:T(8,128)(2,1)} %bitcast.2), calls=%async_computation | async-start | bytes 1048576 | tf_op jit(solution)/shard_map/all_to_all | solution.py:602
  15.6 1.9 %collective-permute-start = (bf16[16,2048]{1,0:T(8,128)(2,1)S(1)}, bf16[16,2048]{1,0:T(8,128)(2,1)S(1)}, u32[]{:S(2)}, u32[]{:S(2)}) collective-permute-start(bf16[16,2048]{1,0:T(8,128)(2,1)S(1)} %get-tuple-element.11), channel_id=1, source_target_pairs={{0,1},{1,0},{2,3},{3,2},{4,5},{5,4},{6,7},{7,6},{8,9},{9,8},{10,11... | collective-permute-start | bytes 196616 | tf_op jit(solution)/shard_map/ppermute | solution.py:601
  17.6 5.9 %collective-permute-start.1 = (bf16[32,2048]{1,0:T(8,128)(2,1)S(1)}, bf16[32,2048]{1,0:T(8,128)(2,1)S(1)}, u32[]{:S(2)}, u32[]{:S(2)}) collective-permute-start(bf16[32,2048]{1,0:T(8,128)(2,1)S(1)} %constant_dynamic-update-slice_fusion.refs_1_), channel_id=1, source_target_pairs={{0,2},{1,3},{2,4},{3,5},{4,6},{5,7},{6,0},{7,1},{8,10},{9,11},{10,... | collective-permute-start | bytes 393224 | tf_op jit(solution)/shard_map/ppermute | solution.py:605
  18.8 8.5 %collective-permute-start.2 = (bf16[32,2048]{1,0:T(8,128)(2,1)S(1)}, bf16[32,2048]{1,0:T(8,128)(2,1)S(1)}, u32[]{:S(2)}, u32[]{:S(2)}) collective-permute-start(bf16[32,2048]{1,0:T(8,128)(2,1)S(1)} %constant_dynamic-update-slice_fusion.refs_1_), channel_id=1, source_target_pairs={{0,4},{1,5},{2,6},{3,7},{4,0},{5,1},{6,2},{7,3},{8,12},{9,13},{10,... | collective-permute-start | bytes 393224 | tf_op jit(solution)/shard_map/ppermute | solution.py:605
  21.2 6.1 %collective-permute-start.3 = (bf16[32,2048]{1,0:T(8,128)(2,1)S(1)}, bf16[32,2048]{1,0:T(8,128)(2,1)S(1)}, u32[]{:S(2)}, u32[]{:S(2)}) collective-permute-start(bf16[32,2048]{1,0:T(8,128)(2,1)S(1)} %constant_dynamic-update-slice_fusion.refs_1_), channel_id=1, source_target_pairs={{0,6},{1,7},{2,0},{3,1},{4,2},{5,3},{6,4},{7,5},{8,14},{9,15},{10,... | collective-permute-start | bytes 393224 | tf_op jit(solution)/shard_map/ppermute | solution.py:605
  36.5 4.1 %collective-permute-start.6 = (bf16[2,64,512]{2,1,0:T(8,128)(2,1)S(1)}, bf16[2,64,512]{2,1,0:T(8,128)(2,1)S(1)}, u32[]{:S(2)}, u32[]{:S(2)}) collective-permute-start(bf16[2,64,512]{2,1,0:T(8,128)(2,1)S(1)} %get-tuple-element.20), channel_id=1, source_target_pairs={{0,6},{1,7},{2,0},{3,1},{4,2},{5,3},{6,4},{7,5},{8,14},{9,15},{10,... | collective-permute-start | bytes 393224 | tf_op jit(solution)/shard_map/ppermute | solution.py:613
  38.6 8.7 %collective-permute-start.4 = (bf16[2,64,512]{2,1,0:T(8,128)(2,1)S(1)}, bf16[2,64,512]{2,1,0:T(8,128)(2,1)S(1)}, u32[]{:S(2)}, u32[]{:S(2)}) collective-permute-start(bf16[2,64,512]{2,1,0:T(8,128)(2,1)S(1)} %get-tuple-element.22), channel_id=1, source_target_pairs={{0,2},{1,3},{2,4},{3,5},{4,6},{5,7},{6,0},{7,1},{8,10},{9,11},{10,... | collective-permute-start | bytes 393224 | tf_op jit(solution)/shard_map/ppermute | solution.py:613
  38.6 6.0 %collective-permute-start.5 = (bf16[2,64,512]{2,1,0:T(8,128)(2,1)S(1)}, bf16[2,64,512]{2,1,0:T(8,128)(2,1)S(1)}, u32[]{:S(2)}, u32[]{:S(2)}) collective-permute-start(bf16[2,64,512]{2,1,0:T(8,128)(2,1)S(1)} %get-tuple-element.21), channel_id=1, source_target_pairs={{0,4},{1,5},{2,6},{3,7},{4,0},{5,1},{6,2},{7,3},{8,12},{9,13},{10,... | collective-permute-start | bytes 393224 | tf_op jit(solution)/shard_map/ppermute | solution.py:613
  47.4 2.6 %collective-permute-start.7 = (bf16[4,64,512]{2,1,0:T(8,128)(2,1)S(1)}, bf16[4,64,512]{2,1,0:T(8,128)(2,1)S(1)}, u32[]{:S(2)}, u32[]{:S(2)}) collective-permute-start(bf16[4,64,512]{2,1,0:T(8,128)(2,1)S(1)} %pad_maximum_fusion), channel_id=1, source_target_pairs={{0,1},{1,0},{2,3},{3,2},{4,5},{5,4},{6,7},{7,6},{8,9},{9,8},{10,11... | collective-permute-start | bytes 786440 | tf_op jit(solution)/shard_map/ppermute | solution.py:617

commit v5 on v4

--- a/solution.py
+++ b/solution.py
@@ -80,7 +80,8 @@
 
 
 def prepare_kernel(
-    owner_count, records_hbm, owners_hbm, phased_ref, slots_ref, records_ref, owners_ref, sems
+    owner_count, records_hbm, owners_hbm, phased_hbm, slots_hbm,
+    records_ref, owners_ref, phased_ref, slots_ref, sems,
 ):
     loads = [
         pltpu.make_async_copy(records_hbm, records_ref, sems.at[0]),
@@ -107,6 +108,8 @@
         phases.append(total.astype(BF16))
     for p in range(PH):
         phased_ref[:, p * LANES : (p + 1) * LANES] = phases[p]
+    stores = [pltpu.make_async_copy(phased_ref, phased_hbm, sems.at[2])]
+    stores[0].start()
     high = PH // GROUP
     stacked = jnp.concatenate(
         [jnp.concatenate(phases[h * GROUP : (h + 1) * GROUP], axis=1) for h in range(high)], axis=0
@@ -137,7 +140,14 @@
         & (row // (SLOTS * BS) % high == col // stations)
     )
     select = jnp.where(right, wanted, 0.0).astype(BF16)
-    slots_ref[...] = dot(select, stacked).astype(BF16)
+    parts, size = 4, rows // 4
+    for i in range(parts):
+        at = pl.ds(i * size, size)
+        slots_ref[at, :] = dot(select[i * size : (i + 1) * size], stacked).astype(BF16)
+        stores.append(pltpu.make_async_copy(slots_ref.at[at, :], slots_hbm.at[at, :], sems.at[3 + i]))
+        stores[-1].start()
+    for store in stores:
+        store.wait()
 
 
 def prepare(records, owners, owner_count):
@@ -146,15 +156,17 @@
     return pl.pallas_call(
         lambda *refs: prepare_kernel(owner_count, *refs),
         out_shape=(
-            jax.ShapeDtypeStruct((stations, length), BF16),
-            jax.ShapeDtypeStruct((rows, GROUP * LANES), BF16),
+            pltpu.HBM((stations, length), BF16),
+            pltpu.HBM((rows, GROUP * LANES), BF16),
         ),
         in_specs=[pl.BlockSpec(memory_space=pltpu.HBM)] * 2,
-        out_specs=[pl.BlockSpec(memory_space=pltpu.VMEM)] * 2,
+        out_specs=[pl.BlockSpec(memory_space=pltpu.HBM)] * 2,
         scratch_shapes=[
             pltpu.VMEM(records.shape, records.dtype),
             pltpu.VMEM(owners.shape, owners.dtype),
-            pltpu.SemaphoreType.DMA((2,)),
+            pltpu.VMEM((stations, length), BF16),
+            pltpu.VMEM((rows, GROUP * LANES), BF16),
+            pltpu.SemaphoreType.DMA((7,)),
         ],
         compiler_params=pltpu.CompilerParams(vmem_limit_bytes=16 * MIB),
         cost_estimate=pl.CostEstimate(
@@ -162,6 +174,24 @@
         ),
         name="prepare",
     )(in_hbm(records), in_hbm(owners))
+
+
+def copy_kernel(x_hbm, out_hbm, sem):
+    copy = pltpu.make_async_copy(x_hbm, out_hbm, sem)
+    copy.start()
+    copy.wait()
+
+
+def copied(x):
+    return pl.pallas_call(
+        copy_kernel,
+        out_shape=pltpu.HBM(x.shape, x.dtype),
+        in_specs=[pl.BlockSpec(memory_space=pltpu.HBM)],
+        out_specs=pl.BlockSpec(memory_space=pltpu.HBM),
+        scratch_shapes=[pltpu.SemaphoreType.DMA(())],
+        cost_estimate=pl.CostEstimate(flops=1000 * MIB, bytes_accessed=MIB, transcendentals=0),
+        name="copied",
+    )(in_hbm(x))
 
 
 def add(a, b):
@@ -324,22 +354,20 @@
 
 
 def own_kernel(
-    segs, me_ref, *refs
+    segs, me_ref, near_ref, far_ref, white_ref, phase_ref, x_ref, y_ref, f_ref, sum_ref, trace_ref
 ):
-    pairs, refs = refs[: segs // CORES], refs[segs // CORES :]
-    white_ref, phase_ref, x_ref, y_ref, f_ref, sum_ref, trace_ref = refs
     rows, length = x_ref.shape[1], PH * LANES
     stations = rows // segs
     per_tile = LANES // PH
     me, chips = me_ref[0], segs // CORES
-    for i, ref in enumerate(pairs):
+    for i in range(chips):
         chip = (lax.div(me, CORES) + chips - i) & (chips - 1)
-        for j in range(CORES):
+        for j, ref in enumerate((near_ref, far_ref)):
             core = (me + j) & (CORES - 1)
             at = pl.ds(pl.multiple_of((chip * CORES + core) * stations, stations), stations)
             for p in range(PH):
                 x_ref[p, at, :] = ref[
-                    j * stations : (j + 1) * stations, p * LANES : (p + 1) * LANES
+                    i * stations : (i + 1) * stations, p * LANES : (p + 1) * LANES
                 ]
     scale = whiten(x_ref, y_ref, f_ref, sum_ref, trace_ref, segs)
     def put(p, s, tile):
@@ -446,7 +474,7 @@
         ],
         compiler_params=pltpu.CompilerParams(vmem_limit_bytes=16 * MIB),
         cost_estimate=pl.CostEstimate(
-            flops=2000 * MIB, bytes_accessed=9 * MIB, transcendentals=0
+            flops=1, bytes_accessed=9 * MIB, transcendentals=0
         ),
         name="shift",
     )(phases)
@@ -598,14 +626,15 @@
     across = [(i, i ^ 1) for i in range(segs)]
     phased, slots = prepare(records, owners.T, sources)
     slots = slots.reshape(sources, -1, GROUP * LANES)
-    other = lax.ppermute(phased, "seg", across)
+    phased = copied(phased)
     passing = lax.all_to_all(slots, "sta", 0, 0, tiled=True)
     passing = passing.reshape(segs, -1, GROUP * LANES)
-    pair = jnp.concatenate([phased, other], axis=0)
-    pairs = [pair] + [lax.ppermute(pair, "seg", along_x[k]) for k in range(1, chips)]
-    whitened, phases = own_part(me.reshape(1), pairs, segs)
+    own = [phased] + [lax.ppermute(phased, "seg", along_x[k]) for k in range(1, chips)]
+    own = jnp.concatenate(own, axis=0)
+    other = lax.ppermute(own, "seg", across)
+    whitened, phases = own_part(me.reshape(1), (own, other), segs)
+    passing, phases = lax.optimization_barrier((passing, phases))
     shifted, extra = shift(phases)
-    passing, shifted, extra = lax.optimization_barrier((passing, shifted, extra))
     near = [passing]
     for k in range(1, chips):
         at = ((chip + k) & (chips - 1)) * CORES
@@ -614,7 +643,8 @@
     other_core = 1 - (me & (CORES - 1))
     give = [lax.dynamic_slice_in_dim(passing, chip * CORES + other_core, 1, 0)]
     give += [lax.dynamic_slice_in_dim(block, other_core, 1, 0) for block in near[1:]]
-    far = lax.ppermute(jnp.concatenate(give, axis=0), "seg", across)
+    give, shifted, extra = lax.optimization_barrier((jnp.concatenate(give, axis=0), shifted, extra))
+    far = lax.ppermute(give, "seg", across)
     result = correlate(me.reshape(1), near, far, shifted, extra, segs)
     return whitened, result.reshape(-1, stations, LAGS)
 

time: 63.3 us -> 60.9 us (0.962)
  waiting for transfers between devices: 14.2 us -> 9.73 us
  Pallas kernels: 24.9 us -> 28 us
  starting transfers between devices: 23 us -> 21.1 us
  other arithmetic: 0.04 us -> 0.89 us
    ppermute x3, waiting for transfers between devices: 7.18 us -> 2.71 us  [on_device(): near.append(lax.ppermute(block, 'seg', along_x[k]))]
    pallas_call x0 -> x1, Pallas kernels: none -> 3.1 us  [copied(): pl.pallas_call(copy_kernel, out_shape=pltpu.HBM(x.shape, x.dtype), in_spe...]
    ppermute x3, starting transfers between devices: 3.65 us -> 1.98 us  [on_device(): near.append(lax.ppermute(block, 'seg', along_x[k]))]
    concatenate x1 -> x2, other arithmetic: 0.04 us -> 0.89 us  [the longest x1 0.86 us: on_device(): own = jnp.concatenate(own, axis=0)]
  transfers between devices with their start and end apart: 9 -> 9, of which waited for: 7 -> 6; matrix products, arithmetic and copies ran while one was open for 0% -> 1% of each run, Pallas kernels for 14% -> 20%
where the time goes in v5:
time: 60.9 us; the launch traced here: 60.6 us
  Pallas kernels  28 us (46%)
  starting transfers between devices  21.1 us (35%)
  waiting for transfers between devices  9.73 us (16%)
  other arithmetic  0.89 us (1%)
  between operations  0.87 us (1%)
    pallas_call x1, Pallas kernels, correlate(): pl.pallas_call(lambda *refs: correlate_kernel(segs, *refs), out_shape=jax...  12.9 us
    all_to_all x1, starting transfers between devices, on_device(): passing = lax.all_to_all(slots, 'sta', 0, 0, tiled=True)  12 us
    pallas_call x1, Pallas kernels, shift(): pl.pallas_call(lambda *refs: shift_kernel(stations, *refs), out_shape=(pl...  4.9 us
    ppermute x3, waiting for transfers between devices, on_device(): lax.ppermute(phased, 'seg', along_x[k])  4.7 us
    pallas_call x1, Pallas kernels, own_part(): pl.pallas_call(lambda *refs: own_kernel(segs, *refs), out_shape=(jax.Shap...  4.23 us
    ppermute x3, starting transfers between devices, on_device(): lax.ppermute(phased, 'seg', along_x[k])  3.68 us
    pallas_call x1, Pallas kernels, copied(): pl.pallas_call(copy_kernel, out_shape=pltpu.HBM(x.shape, x.dtype), in_spe...  3.1 us
    pallas_call x1, Pallas kernels, prepare(): pl.pallas_call(lambda *refs: prepare_kernel(owner_count, *refs), out_shap...  2.85 us
  transfers between devices with their start and end apart: 9, of which 6 were waited for; matrix products, arithmetic and copies ran while one was open for 1% of the time, Pallas kernels for 20%

profile of v5, /device:TPU:1, one launch (start us, length us, event | category | flops | bytes accessed | tf_op | source)
XLA Modules:
  0.0 60.6 jit_solution(8326429925070482190)
XLA Ops:
  0.6 2.9 %prepare.1 = (bf16[16,2048]{1,0:T(8,128)(2,1)}, bf16[512,512]{1,0:T(8,128)(2,1)}) custom-call(bf16[16,2048]{1,0:T(8,128)(2,1)} %refs_0_.1, s32[4,8]{1,0:T(4,128)} %bitcast.9), custom_call_target="tpu_custom_call" | custom-call | flops 104857600 | bytes 2097152 | tf_op jit(solution)/shard_map/prepare/pallas_call | solution.py:156
  3.5 12.0 %all-to-all-start = ((bf16[32,16,512]{2,1,0:T(8,128)(2,1)}), bf16[32,16,512]{2,1,0:T(8,128)(2,1)S(1)}, u32[]{:S(2)}, u32[]{:S(2)}) async-start(bf16[32,16,512]{2,1,0:T(8,128)(2,1)} %bitcast.8), calls=%async_computation | async-start | bytes 1048576 | tf_op jit(solution)/shard_map/all_to_all | solution.py:630
  15.5 3.1 %copied.1 = bf16[16,2048]{1,0:T(8,128)(2,1)} custom-call(bf16[16,2048]{1,0:T(8,128)(2,1)} %get-tuple-element.13.x_hbm), custom_call_target="tpu_custom_call" | custom-call | flops 1048576000 | bytes 1048576 | tf_op jit(solution)/shard_map/copied/pallas_call | solution.py:186
  18.6 2.6 %collective-permute-start.2 = (bf16[16,2048]{1,0:T(8,128)(2,1)}, bf16[16,2048]{1,0:T(8,128)(2,1)S(1)}, u32[]{:S(2)}, u32[]{:S(2)}) collective-permute-start(bf16[16,2048]{1,0:T(8,128)(2,1)} %copied.1), channel_id=1, source_target_pairs={{0,6},{1,7},{2,0},{3,1},{4,2},{5,3},{6,4},{7,5},{8,14},{9,15},{10,... | collective-permute-start | bytes 196616 | tf_op jit(solution)/shard_map/ppermute | solution.py:632
  21.2 0.5 collective-permute-start.1
  21.7 0.6 %collective-permute-start = (bf16[16,2048]{1,0:T(8,128)(2,1)}, bf16[16,2048]{1,0:T(8,128)(2,1)S(1)}, u32[]{:S(2)}, u32[]{:S(2)}) collective-permute-start(bf16[16,2048]{1,0:T(8,128)(2,1)} %copied.1), channel_id=1, source_target_pairs={{0,2},{1,3},{2,4},{3,5},{4,6},{5,7},{6,0},{7,1},{8,10},{9,11},{10,... | collective-permute-start | bytes 196616 | tf_op jit(solution)/shard_map/ppermute | solution.py:632
  22.3 0.5 collective-permute-done.2
  22.9 3.5 %collective-permute-done.1 = bf16[16,2048]{1,0:T(8,128)(2,1)S(1)} collective-permute-done((bf16[16,2048]{1,0:T(8,128)(2,1)}, bf16[16,2048]{1,0:T(8,128)(2,1)S(1)}, u32[]{:S(2)}, u32[]{:S(2)}) %collective-permute-start.1) | collective-permute-done | bytes 65568 | tf_op jit(solution)/shard_map/ppermute | solution.py:632
  26.3 0.7 %collective-permute-done = bf16[16,2048]{1,0:T(8,128)(2,1)S(1)} collective-permute-done((bf16[16,2048]{1,0:T(8,128)(2,1)}, bf16[16,2048]{1,0:T(8,128)(2,1)S(1)}, u32[]{:S(2)}, u32[]{:S(2)}) %collective-permute-start) | collective-permute-done | bytes 65568 | tf_op jit(solution)/shard_map/ppermute | solution.py:632
  27.0 0.9 %pad_maximum_fusion.refs_1_ = bf16[64,2048]{1,0:T(8,128)(2,1)S(1)} fusion(bf16[16,2048]{1,0:T(8,128)(2,1)S(1)} %collective-permute-done.2, bf16[16,2048]{1,0:T(8,128)(2,1)S(1)} %collective-permute-done.1, bf16[16,2048]{1,0:T(8,128)(2,1)S(1)} %collective-permute-done, bf16[16,2048]{1,0:T(8,128)(2,1)} %copied.1), kind=kLoop, calls=%fused_computation | loop fusion | flops 1048576 | bytes 524288 | tf_op jit(solution)/shard_map/concatenate | solution.py:633
  27.9 2.2 %collective-permute-start.3 = (bf16[64,2048]{1,0:T(8,128)(2,1)S(1)}, bf16[64,2048]{1,0:T(8,128)(2,1)S(1)}, u32[]{:S(2)}, u32[]{:S(2)}) collective-permute-start(bf16[64,2048]{1,0:T(8,128)(2,1)S(1)} %pad_maximum_fusion.refs_1_), channel_id=1, source_target_pairs={{0,1},{1,0},{2,3},{3,2},{4,5},{5,4},{6,7},{7,6},{8,9},{9,8},{10,11... | collective-permute-start | bytes 786440 | tf_op jit(solution)/shard_map/ppermute | solution.py:634
  30.1 1.2 %collective-permute-done.3.refs_2_ = bf16[64,2048]{1,0:T(8,128)(2,1)S(1)} collective-permute-done((bf16[64,2048]{1,0:T(8,128)(2,1)S(1)}, bf16[64,2048]{1,0:T(8,128)(2,1)S(1)}, u32[]{:S(2)}, u32[]{:S(2)}) %collective-permute-start.3) | collective-permute-done | bytes 262176 | tf_op jit(solution)/shard_map/ppermute | solution.py:634
  31.2 4.2 %own.1 = (bf16[16,2048]{1,0:T(8,128)(2,1)}, f32[4,512,128]{2,1,0:T(8,128)S(1)}) custom-call(s32[1]{0:T(128)} %bitcast.refs_0_, bf16[64,2048]{1,0:T(8,128)(2,1)S(1)} %pad_maximum_fusion.refs_1_, bf16[64,2048]{1,0:T(8,128)(2,1)S(1)} %collective-permute-done.3.refs_2_), custom_call_target="tpu_custom_call" | custom-call | flops 2097152000 | bytes 4194304 | tf_op jit(solution)/shard_map/own/pallas_call | solution.py:395
  35.5 0.0 all-to-all-done
  35.5 0.4 collective-permute-start.6
  35.9 0.9 %collective-permute-start.5 = (bf16[2,64,512]{2,1,0:T(8,128)(2,1)S(1)}, bf16[2,64,512]{2,1,0:T(8,128)(2,1)S(1)}, u32[]{:S(2)}, u32[]{:S(2)}) collective-permute-start(bf16[2,64,512]{2,1,0:T(8,128)(2,1)S(1)} %get-tuple-element.25), channel_id=1, source_target_pairs={{0,4},{1,5},{2,6},{3,7},{4,0},{5,1},{6,2},{7,3},{8,12},{9,13},{10,... | collective-permute-start | bytes 393224 | tf_op jit(solution)/shard_map/ppermute | solution.py:642
  36.7 0.7 %collective-permute-start.4 = (bf16[2,64,512]{2,1,0:T(8,128)(2,1)S(1)}, bf16[2,64,512]{2,1,0:T(8,128)(2,1)S(1)}, u32[]{:S(2)}, u32[]{:S(2)}) collective-permute-start(bf16[2,64,512]{2,1,0:T(8,128)(2,1)S(1)} %get-tuple-element.26), channel_id=1, source_target_pairs={{0,2},{1,3},{2,4},{3,5},{4,6},{5,7},{6,0},{7,1},{8,10},{9,11},{10,... | collective-permute-start | bytes 393224 | tf_op jit(solution)/shard_map/ppermute | solution.py:642
  37.5 4.9 %shift.1 = (bf16[8192,512]{1,0:T(8,128)(2,1)}, bf16[512,512]{1,0:T(8,128)(2,1)}) custom-call(f32[4,512,128]{2,1,0:T(8,128)S(1)} %get-tuple-element.18.refs_0_), custom_call_target="tpu_custom_call" | custom-call | flops 1 | bytes 9437184 | tf_op jit(solution)/shard_map/shift/pallas_call | solution.py:462
  42.4 0.0 collective-permute-done.6.refs_4_
  42.4 0.0 collective-permute-done.5.refs_3_
  42.5 2.7 %collective-permute-done.4.refs_2_ = bf16[2,64,512]{2,1,0:T(8,128)(2,1)S(1)} collective-permute-done((bf16[2,64,512]{2,1,0:T(8,128)(2,1)S(1)}, bf16[2,64,512]{2,1,0:T(8,128)(2,1)S(1)}, u32[]{:S(2)}, u32[]{:S(2)}) %collective-permute-start.4) | collective-permute-done | bytes 131104 | tf_op jit(solution)/shard_map/ppermute | solution.py:642
  45.2 1.2 %collective-permute-start.7 = (bf16[4,64,512]{2,1,0:T(8,128)(2,1)S(1)}, bf16[4,64,512]{2,1,0:T(8,128)(2,1)S(1)}, u32[]{:S(2)}, u32[]{:S(2)}) collective-permute-start(bf16[4,64,512]{2,1,0:T(8,128)(2,1)S(1)} %pad_maximum_fusion.1), channel_id=1, source_target_pairs={{0,1},{1,0},{2,3},{3,2},{4,5},{5,4},{6,7},{7,6},{8,9},{9,8},{10,11... | collective-permute-start | bytes 786440 | tf_op jit(solution)/shard_map/ppermute | solution.py:647
  46.4 1.2 %collective-permute-done.7.refs_5_ = bf16[4,64,512]{2,1,0:T(8,128)(2,1)S(1)} collective-permute-done((bf16[4,64,512]{2,1,0:T(8,128)(2,1)S(1)}, bf16[4,64,512]{2,1,0:T(8,128)(2,1)S(1)}, u32[]{:S(2)}, u32[]{:S(2)}) %collective-permute-start.7) | collective-permute-done | bytes 262176 | tf_op jit(solution)/shard_map/ppermute | solution.py:647
  47.6 12.9 %correlate.1 = bf16[256,512]{1,0:T(8,128)(2,1)} custom-call(s32[1]{0:T(128)} %bitcast.refs_0_, bf16[8,64,512]{2,1,0:T(8,128)(2,1)S(1)} %bitcast.7, bf16[2,64,512]{2,1,0:T(8,128)(2,1)S(1)} %collective-permute-done.4.refs_2_, bf16[2,64,512]{2,1,0:T(8,128)(2,1)S(1)} %collective-permute-done.5.refs_3_, bf16[2,64,512]{2,1,0:T(8,128)(2,1)S(1)} %collective-permute-done.6.refs_4_, ...), custom_call_target="tpu_custom_call" | custom-call | flops 6291456000 | bytes 20971520 | tf_op jit(solution)/shard_map/correlate/pallas_call | solution.py:584
  (6 shorter events, 0.1 us)
Async XLA Ops:
  3.5 32.0 %all-to-all-start = ((bf16[32,16,512]{2,1,0:T(8,128)(2,1)}), bf16[32,16,512]{2,1,0:T(8,128)(2,1)S(1)}, u32[]{:S(2)}, u32[]{:S(2)}) async-start(bf16[32,16,512]{2,1,0:T(8,128)(2,1)} %bitcast.8), calls=%async_computation | async-start | bytes 1048576 | tf_op jit(solution)/shard_map/all_to_all | solution.py:630
  18.6 4.2 %collective-permute-start.2 = (bf16[16,2048]{1,0:T(8,128)(2,1)}, bf16[16,2048]{1,0:T(8,128)(2,1)S(1)}, u32[]{:S(2)}, u32[]{:S(2)}) collective-permute-start(bf16[16,2048]{1,0:T(8,128)(2,1)} %copied.1), channel_id=1, source_target_pairs={{0,6},{1,7},{2,0},{3,1},{4,2},{5,3},{6,4},{7,5},{8,14},{9,15},{10,... | collective-permute-start | bytes 196616 | tf_op jit(solution)/shard_map/ppermute | solution.py:632
  21.2 5.1 %collective-permute-start.1 = (bf16[16,2048]{1,0:T(8,128)(2,1)}, bf16[16,2048]{1,0:T(8,128)(2,1)S(1)}, u32[]{:S(2)}, u32[]{:S(2)}) collective-permute-start(bf16[16,2048]{1,0:T(8,128)(2,1)} %copied.1), channel_id=1, source_target_pairs={{0,4},{1,5},{2,6},{3,7},{4,0},{5,1},{6,2},{7,3},{8,12},{9,13},{10,... | collective-permute-start | bytes 196616 | tf_op jit(solution)/shard_map/ppermute | solution.py:632
  21.7 5.3 %collective-permute-start = (bf16[16,2048]{1,0:T(8,128)(2,1)}, bf16[16,2048]{1,0:T(8,128)(2,1)S(1)}, u32[]{:S(2)}, u32[]{:S(2)}) collective-permute-start(bf16[16,2048]{1,0:T(8,128)(2,1)} %copied.1), channel_id=1, source_target_pairs={{0,2},{1,3},{2,4},{3,5},{4,6},{5,7},{6,0},{7,1},{8,10},{9,11},{10,... | collective-permute-start | bytes 196616 | tf_op jit(solution)/shard_map/ppermute | solution.py:632
  27.9 3.3 %collective-permute-start.3 = (bf16[64,2048]{1,0:T(8,128)(2,1)S(1)}, bf16[64,2048]{1,0:T(8,128)(2,1)S(1)}, u32[]{:S(2)}, u32[]{:S(2)}) collective-permute-start(bf16[64,2048]{1,0:T(8,128)(2,1)S(1)} %pad_maximum_fusion.refs_1_), channel_id=1, source_target_pairs={{0,1},{1,0},{2,3},{3,2},{4,5},{5,4},{6,7},{7,6},{8,9},{9,8},{10,11... | collective-permute-start | bytes 786440 | tf_op jit(solution)/shard_map/ppermute | solution.py:634
  35.5 6.9 %collective-permute-start.6 = (bf16[2,64,512]{2,1,0:T(8,128)(2,1)S(1)}, bf16[2,64,512]{2,1,0:T(8,128)(2,1)S(1)}, u32[]{:S(2)}, u32[]{:S(2)}) collective-permute-start(bf16[2,64,512]{2,1,0:T(8,128)(2,1)S(1)} %get-tuple-element.24), channel_id=1, source_target_pairs={{0,6},{1,7},{2,0},{3,1},{4,2},{5,3},{6,4},{7,5},{8,14},{9,15},{10,... | collective-permute-start | bytes 393224 | tf_op jit(solution)/shard_map/ppermute | solution.py:642
  35.9 6.6 %collective-permute-start.5 = (bf16[2,64,512]{2,1,0:T(8,128)(2,1)S(1)}, bf16[2,64,512]{2,1,0:T(8,128)(2,1)S(1)}, u32[]{:S(2)}, u32[]{:S(2)}) collective-permute-start(bf16[2,64,512]{2,1,0:T(8,128)(2,1)S(1)} %get-tuple-element.25), channel_id=1, source_target_pairs={{0,4},{1,5},{2,6},{3,7},{4,0},{5,1},{6,2},{7,3},{8,12},{9,13},{10,... | collective-permute-start | bytes 393224 | tf_op jit(solution)/shard_map/ppermute | solution.py:642
  36.7 8.4 %collective-permute-start.4 = (bf16[2,64,512]{2,1,0:T(8,128)(2,1)S(1)}, bf16[2,64,512]{2,1,0:T(8,128)(2,1)S(1)}, u32[]{:S(2)}, u32[]{:S(2)}) collective-permute-start(bf16[2,64,512]{2,1,0:T(8,128)(2,1)S(1)} %get-tuple-element.26), channel_id=1, source_target_pairs={{0,2},{1,3},{2,4},{3,5},{4,6},{5,7},{6,0},{7,1},{8,10},{9,11},{10,... | collective-permute-start | bytes 393224 | tf_op jit(solution)/shard_map/ppermute | solution.py:642
  45.2 2.4 %collective-permute-start.7 = (bf16[4,64,512]{2,1,0:T(8,128)(2,1)S(1)}, bf16[4,64,512]{2,1,0:T(8,128)(2,1)S(1)}, u32[]{:S(2)}, u32[]{:S(2)}) collective-permute-start(bf16[4,64,512]{2,1,0:T(8,128)(2,1)S(1)} %pad_maximum_fusion.1), channel_id=1, source_target_pairs={{0,1},{1,0},{2,3},{3,2},{4,5},{5,4},{6,7},{7,6},{8,9},{9,8},{10,11... | collective-permute-start | bytes 786440 | tf_op jit(solution)/shard_map/ppermute | solution.py:647

commit v6 on v5

--- a/solution.py
+++ b/solution.py
@@ -174,24 +174,6 @@
         ),
         name="prepare",
     )(in_hbm(records), in_hbm(owners))
-
-
-def copy_kernel(x_hbm, out_hbm, sem):
-    copy = pltpu.make_async_copy(x_hbm, out_hbm, sem)
-    copy.start()
-    copy.wait()
-
-
-def copied(x):
-    return pl.pallas_call(
-        copy_kernel,
-        out_shape=pltpu.HBM(x.shape, x.dtype),
-        in_specs=[pl.BlockSpec(memory_space=pltpu.HBM)],
-        out_specs=pl.BlockSpec(memory_space=pltpu.HBM),
-        scratch_shapes=[pltpu.SemaphoreType.DMA(())],
-        cost_estimate=pl.CostEstimate(flops=1000 * MIB, bytes_accessed=MIB, transcendentals=0),
-        name="copied",
-    )(in_hbm(x))
 
 
 def add(a, b):
@@ -353,21 +335,21 @@
     ]
 
 
-def own_kernel(
-    segs, me_ref, near_ref, far_ref, white_ref, phase_ref, x_ref, y_ref, f_ref, sum_ref, trace_ref
-):
+def own_kernel(segs, me_ref, *refs):
+    pairs, refs = refs[: segs // CORES], refs[segs // CORES :]
+    white_ref, phase_ref, x_ref, y_ref, f_ref, sum_ref, trace_ref = refs
     rows, length = x_ref.shape[1], PH * LANES
     stations = rows // segs
     per_tile = LANES // PH
     me, chips = me_ref[0], segs // CORES
-    for i in range(chips):
+    for i, ref in enumerate(pairs):
         chip = (lax.div(me, CORES) + chips - i) & (chips - 1)
-        for j, ref in enumerate((near_ref, far_ref)):
+        for j in range(CORES):
             core = (me + j) & (CORES - 1)
             at = pl.ds(pl.multiple_of((chip * CORES + core) * stations, stations), stations)
             for p in range(PH):
                 x_ref[p, at, :] = ref[
-                    i * stations : (i + 1) * stations, p * LANES : (p + 1) * LANES
+                    j * stations : (j + 1) * stations, p * LANES : (p + 1) * LANES
                 ]
     scale = whiten(x_ref, y_ref, f_ref, sum_ref, trace_ref, segs)
     def put(p, s, tile):
@@ -415,8 +397,7 @@
 def shift_kernel(stations, phase_ref, shifted_hbm, extra_hbm, shifted_ref, extra_ref, sems):
     count = LAGS // FINE
     tiles = phase_ref.shape[0]
-    total = tiles * LANES
-    lane = iota((FINE, total), 1)
+    lane = iota((FINE, LANES), 1)
 
     def copies(a):
         to = shifted_hbm.at[pl.ds(pl.multiple_of(a * LAGS, LAGS), LAGS), :]
@@ -427,26 +408,29 @@
         )
 
     def body(a, _):
-        block = jnp.concatenate(
-            [phase_ref[s, pl.ds(a, FINE, stride=stations), :] for s in range(tiles)], axis=1
-        )
+        block = [phase_ref[s, pl.ds(a, FINE, stride=stations), :] for s in range(tiles)]
+        zero = jnp.zeros((FINE, LANES), F32)
         for i in range(-1, count):
             m = i + 1 - count // 2
-            moved = pltpu.roll(block, m % total, 1) if m else block
-            if m > 0:
-                moved = jnp.where(lane >= m, moved, 0.0)
-            elif m < 0:
-                moved = jnp.where(lane < total + m, moved, 0.0)
-            moved = moved.astype(BF16)
-            if i < 0:
-                extra_ref[a] = moved
-            else:
-                shifted_ref[a, i * FINE : (i + 1) * FINE, :] = moved
+            turned = [pltpu.roll(tile, m % LANES, 1) if m else tile for tile in block]
+            for t in range(tiles):
+                if m > 0:
+                    moved = jnp.where(lane >= m, turned[t], turned[t - 1] if t else zero)
+                elif m < 0:
+                    later = turned[t + 1] if t + 1 < tiles else zero
+                    moved = jnp.where(lane < LANES + m, turned[t], later)
+                else:
+                    moved = turned[t]
+                cols = slice(t * LANES, (t + 1) * LANES)
+                if i < 0:
+                    extra_ref[a, :, cols] = moved.astype(BF16)
+                else:
+                    shifted_ref[a, i * FINE : (i + 1) * FINE, cols] = moved.astype(BF16)
         for copy in copies(a):
             copy.start()
         return 0
 
-    lax.fori_loop(0, stations, body, 0)
+    lax.fori_loop(0, stations, body, 0, unroll=4)
 
     def finish(a, _):
         for copy in copies(a):
@@ -626,13 +610,12 @@
     across = [(i, i ^ 1) for i in range(segs)]
     phased, slots = prepare(records, owners.T, sources)
     slots = slots.reshape(sources, -1, GROUP * LANES)
-    phased = copied(phased)
     passing = lax.all_to_all(slots, "sta", 0, 0, tiled=True)
     passing = passing.reshape(segs, -1, GROUP * LANES)
-    own = [phased] + [lax.ppermute(phased, "seg", along_x[k]) for k in range(1, chips)]
-    own = jnp.concatenate(own, axis=0)
-    other = lax.ppermute(own, "seg", across)
-    whitened, phases = own_part(me.reshape(1), (own, other), segs)
+    other = lax.ppermute(phased, "seg", across)
+    pair = jnp.concatenate([phased, other], axis=0)
+    pairs = [pair] + [lax.ppermute(pair, "seg", along_x[k]) for k in range(1, chips)]
+    whitened, phases = own_part(me.reshape(1), pairs, segs)
     passing, phases = lax.optimization_barrier((passing, phases))
     shifted, extra = shift(phases)
     near = [passing]

time: 60.9 us -> 59.9 us (0.984)
  Pallas kernels: 28 us -> 23.9 us
  waiting for transfers between devices: 9.73 us -> 11.3 us
  starting transfers between devices: 21.1 us -> 22.6 us
  local copies, waits for them, and re-layouts: 0.06 us -> 0.91 us
  other arithmetic: 0.89 us -> 0.04 us
    pallas_call x1 -> x0, Pallas kernels: 3.1 us -> none  [copied(): pl.pallas_call(copy_kernel, out_shape=pltpu.HBM(x.shape, x.dtype), in_spe...]
    ppermute x1, starting transfers between devices: 1.2 us -> 4.29 us  [on_device(): far = lax.ppermute(give, 'seg', across)]
    ppermute x4, waiting for transfers between devices: 5.86 us -> 8.87 us  [the longest x3 8.6 us: on_device(): lax.ppermute(pair, 'seg', along_x[k])]
    ppermute x3, waiting for transfers between devices: 2.71 us -> 1.31 us  [on_device(): near.append(lax.ppermute(block, 'seg', along_x[k]))]
    ppermute x4, starting transfers between devices: 5.86 us -> 4.65 us  [the longest x3 3.6 us: on_device(): lax.ppermute(pair, 'seg', along_x[k])]
    pallas_call x1, Pallas kernels: 4.9 us -> 3.94 us  [shift(): pl.pallas_call(lambda *refs: shift_kernel(stations, *refs), out_shape=(pl...]
    concatenate x1 -> x0, other arithmetic: 0.86 us -> none  [on_device(): own = jnp.concatenate(own, axis=0)]
    unnamed x0 -> x1, local copies, waits for them, and re-layouts: none -> 0.84 us
  transfers between devices with their start and end apart: 9 -> 9, of which waited for: 6 -> 6; matrix products, arithmetic and copies ran while one was open for 1% -> 1% of each run, Pallas kernels for 20% -> 14%
where the time goes in v6:
time: 59.9 us; the launch traced here: 59.7 us
  Pallas kernels  23.9 us (40%)
  starting transfers between devices  22.6 us (38%)
  waiting for transfers between devices  11.3 us (19%)
  local copies, waits for them, and re-layouts  0.91 us (2%)
  between operations  0.86 us (1%)
    pallas_call x1, Pallas kernels, correlate(): pl.pallas_call(lambda *refs: correlate_kernel(segs, *refs), out_shape=jax...  12.9 us
    all_to_all x1, starting transfers between devices, on_device(): passing = lax.all_to_all(slots, 'sta', 0, 0, tiled=True)  12 us
    ppermute x3, waiting for transfers between devices, on_device(): lax.ppermute(pair, 'seg', along_x[k])  8.6 us
    ppermute x1, starting transfers between devices, on_device(): far = lax.ppermute(give, 'seg', across)  4.29 us
    pallas_call x1, Pallas kernels, own_part(): pl.pallas_call(lambda *refs: own_kernel(segs, *refs), out_shape=(jax.Shap...  4.23 us
    pallas_call x1, Pallas kernels, shift(): pl.pallas_call(lambda *refs: shift_kernel(stations, *refs), out_shape=(pl...  3.94 us
    ppermute x3, starting transfers between devices, on_device(): lax.ppermute(pair, 'seg', along_x[k])  3.6 us
    pallas_call x1, Pallas kernels, prepare(): pl.pallas_call(lambda *refs: prepare_kernel(owner_count, *refs), out_shap...  2.85 us
  transfers between devices with their start and end apart: 9, of which 6 were waited for; matrix products, arithmetic and copies ran while one was open for 1% of the time, Pallas kernels for 14%

profile of v6, /device:TPU:1, one launch (start us, length us, event | category | flops | bytes accessed | tf_op | source)
XLA Modules:
  0.0 59.7 jit_solution(17582593843332391292)
XLA Ops:
  0.6 2.9 %prepare.1 = (bf16[16,2048]{1,0:T(8,128)(2,1)}, bf16[512,512]{1,0:T(8,128)(2,1)}) custom-call(bf16[16,2048]{1,0:T(8,128)(2,1)} %refs_0_.1, s32[4,8]{1,0:T(4,128)} %bitcast.9), custom_call_target="tpu_custom_call" | custom-call | flops 104857600 | bytes 2097152 | tf_op jit(solution)/shard_map/prepare/pallas_call | solution.py:156
  3.5 12.0 %all-to-all-start = ((bf16[32,16,512]{2,1,0:T(8,128)(2,1)}), bf16[32,16,512]{2,1,0:T(8,128)(2,1)S(1)}, u32[]{:S(2)}, u32[]{:S(2)}) async-start(bf16[32,16,512]{2,1,0:T(8,128)(2,1)} %bitcast.8), calls=%async_computation | async-start | bytes 1048576 | tf_op jit(solution)/shard_map/all_to_all | solution.py:613
  15.5 1.0 %collective-permute-start = (bf16[16,2048]{1,0:T(8,128)(2,1)}, bf16[16,2048]{1,0:T(8,128)(2,1)S(1)}, u32[]{:S(2)}, u32[]{:S(2)}) collective-permute-start(bf16[16,2048]{1,0:T(8,128)(2,1)} %get-tuple-element.13), channel_id=1, source_target_pairs={{0,1},{1,0},{2,3},{3,2},{4,5},{5,4},{6,7},{7,6},{8,9},{9,8},{10,11... | collective-permute-start | bytes 196616 | tf_op jit(solution)/shard_map/ppermute | solution.py:615
  16.6 0.8 %constant_dynamic-update-slice_fusion.1 = bf16[32,2048]{1,0:T(8,128)(2,1)S(1)} fusion(bf16[16,2048]{1,0:T(8,128)(2,1)} %get-tuple-element.13), kind=kLoop, calls=%fused_computation.2 | loop fusion | bytes 131072
  17.4 0.3 collective-permute-done
  17.7 2.5 %collective-permute-start.3 = (bf16[32,2048]{1,0:T(8,128)(2,1)S(1)}, bf16[32,2048]{1,0:T(8,128)(2,1)S(1)}, u32[]{:S(2)}, u32[]{:S(2)}) collective-permute-start(bf16[32,2048]{1,0:T(8,128)(2,1)S(1)} %constant_dynamic-update-slice_fusion.refs_1_), channel_id=1, source_target_pairs={{0,6},{1,7},{2,0},{3,1},{4,2},{5,3},{6,4},{7,5},{8,14},{9,15},{10,... | collective-permute-start | bytes 393224 | tf_op jit(solution)/shard_map/ppermute | solution.py:617
  20.2 0.5 collective-permute-start.2
  20.7 0.6 %collective-permute-start.1 = (bf16[32,2048]{1,0:T(8,128)(2,1)S(1)}, bf16[32,2048]{1,0:T(8,128)(2,1)S(1)}, u32[]{:S(2)}, u32[]{:S(2)}) collective-permute-start(bf16[32,2048]{1,0:T(8,128)(2,1)S(1)} %constant_dynamic-update-slice_fusion.refs_1_), channel_id=1, source_target_pairs={{0,2},{1,3},{2,4},{3,5},{4,6},{5,7},{6,0},{7,1},{8,10},{9,11},{10,... | collective-permute-start | bytes 393224 | tf_op jit(solution)/shard_map/ppermute | solution.py:617
  21.3 4.1 %collective-permute-done.3.refs_4_ = bf16[32,2048]{1,0:T(8,128)(2,1)S(1)} collective-permute-done((bf16[32,2048]{1,0:T(8,128)(2,1)S(1)}, bf16[32,2048]{1,0:T(8,128)(2,1)S(1)}, u32[]{:S(2)}, u32[]{:S(2)}) %collective-permute-start.3) | collective-permute-done | bytes 131104 | tf_op jit(solution)/shard_map/ppermute | solution.py:617
  25.4 0.7 %collective-permute-done.2.refs_3_ = bf16[32,2048]{1,0:T(8,128)(2,1)S(1)} collective-permute-done((bf16[32,2048]{1,0:T(8,128)(2,1)S(1)}, bf16[32,2048]{1,0:T(8,128)(2,1)S(1)}, u32[]{:S(2)}, u32[]{:S(2)}) %collective-permute-start.2) | collective-permute-done | bytes 131104 | tf_op jit(solution)/shard_map/ppermute | solution.py:617
  26.1 3.8 %collective-permute-done.1.refs_2_ = bf16[32,2048]{1,0:T(8,128)(2,1)S(1)} collective-permute-done((bf16[32,2048]{1,0:T(8,128)(2,1)S(1)}, bf16[32,2048]{1,0:T(8,128)(2,1)S(1)}, u32[]{:S(2)}, u32[]{:S(2)}) %collective-permute-start.1) | collective-permute-done | bytes 131104 | tf_op jit(solution)/shard_map/ppermute | solution.py:617
  29.9 4.2 %own.1 = (bf16[16,2048]{1,0:T(8,128)(2,1)}, f32[4,512,128]{2,1,0:T(8,128)S(1)}) custom-call(s32[1]{0:T(128)} %bitcast.refs_0_, bf16[32,2048]{1,0:T(8,128)(2,1)S(1)} %constant_dynamic-update-slice_fusion.refs_1_, bf16[32,2048]{1,0:T(8,128)(2,1)S(1)} %collective-permute-done.1.refs_2_, bf16[32,2048]{1,0:T(8,128)(2,1)S(1)} %collective-permute-done.2.refs_3_, ...), custom_call_target="tpu_custom_call" | custom-call | flops 2097152000 | bytes 4194304 | tf_op jit(solution)/shard_map/own/pallas_call | solution.py:377
  34.1 0.0 all-to-all-done
  34.2 0.2 collective-permute-start.6
  34.4 0.5 collective-permute-start.5
  34.9 0.9 %collective-permute-start.4 = (bf16[2,64,512]{2,1,0:T(8,128)(2,1)S(1)}, bf16[2,64,512]{2,1,0:T(8,128)(2,1)S(1)}, u32[]{:S(2)}, u32[]{:S(2)}) collective-permute-start(bf16[2,64,512]{2,1,0:T(8,128)(2,1)S(1)} %get-tuple-element.26), channel_id=1, source_target_pairs={{0,2},{1,3},{2,4},{3,5},{4,6},{5,7},{6,0},{7,1},{8,10},{9,11},{10,... | collective-permute-start | bytes 393224 | tf_op jit(solution)/shard_map/ppermute | solution.py:625
  35.8 3.9 %shift.1 = (bf16[8192,512]{1,0:T(8,128)(2,1)}, bf16[512,512]{1,0:T(8,128)(2,1)}) custom-call(f32[4,512,128]{2,1,0:T(8,128)S(1)} %get-tuple-element.18.refs_0_), custom_call_target="tpu_custom_call" | custom-call | flops 1 | bytes 9437184 | tf_op jit(solution)/shard_map/shift/pallas_call | solution.py:446
  39.8 0.0 collective-permute-done.6.refs_4_
  39.8 0.0 collective-permute-done.5.refs_3_
  39.8 1.3 %collective-permute-done.4.refs_2_ = bf16[2,64,512]{2,1,0:T(8,128)(2,1)S(1)} collective-permute-done((bf16[2,64,512]{2,1,0:T(8,128)(2,1)S(1)}, bf16[2,64,512]{2,1,0:T(8,128)(2,1)S(1)}, u32[]{:S(2)}, u32[]{:S(2)}) %collective-permute-start.4) | collective-permute-done | bytes 131104 | tf_op jit(solution)/shard_map/ppermute | solution.py:625
  41.2 4.3 %collective-permute-start.7 = (bf16[4,64,512]{2,1,0:T(8,128)(2,1)S(1)}, bf16[4,64,512]{2,1,0:T(8,128)(2,1)S(1)}, u32[]{:S(2)}, u32[]{:S(2)}) collective-permute-start(bf16[4,64,512]{2,1,0:T(8,128)(2,1)S(1)} %pad_maximum_fusion), channel_id=1, source_target_pairs={{0,1},{1,0},{2,3},{3,2},{4,5},{5,4},{6,7},{7,6},{8,9},{9,8},{10,11... | collective-permute-start | bytes 786440 | tf_op jit(solution)/shard_map/ppermute | solution.py:630
  45.5 1.2 %collective-permute-done.7.refs_5_ = bf16[4,64,512]{2,1,0:T(8,128)(2,1)S(1)} collective-permute-done((bf16[4,64,512]{2,1,0:T(8,128)(2,1)S(1)}, bf16[4,64,512]{2,1,0:T(8,128)(2,1)S(1)}, u32[]{:S(2)}, u32[]{:S(2)}) %collective-permute-start.7) | collective-permute-done | bytes 262176 | tf_op jit(solution)/shard_map/ppermute | solution.py:630
  46.6 12.9 %correlate.1 = bf16[256,512]{1,0:T(8,128)(2,1)} custom-call(s32[1]{0:T(128)} %bitcast.refs_0_, bf16[8,64,512]{2,1,0:T(8,128)(2,1)S(1)} %bitcast.7, bf16[2,64,512]{2,1,0:T(8,128)(2,1)S(1)} %collective-permute-done.4.refs_2_, bf16[2,64,512]{2,1,0:T(8,128)(2,1)S(1)} %collective-permute-done.5.refs_3_, bf16[2,64,512]{2,1,0:T(8,128)(2,1)S(1)} %collective-permute-done.6.refs_4_, ...), custom_call_target="tpu_custom_call" | custom-call | flops 6291456000 | bytes 20971520 | tf_op jit(solution)/shard_map/correlate/pallas_call | solution.py:568
  (7 shorter events, 0.1 us)
Async XLA Ops:
  3.5 30.7 %all-to-all-start = ((bf16[32,16,512]{2,1,0:T(8,128)(2,1)}), bf16[32,16,512]{2,1,0:T(8,128)(2,1)S(1)}, u32[]{:S(2)}, u32[]{:S(2)}) async-start(bf16[32,16,512]{2,1,0:T(8,128)(2,1)} %bitcast.8), calls=%async_computation | async-start | bytes 1048576 | tf_op jit(solution)/shard_map/all_to_all | solution.py:613
  15.5 2.2 %collective-permute-start = (bf16[16,2048]{1,0:T(8,128)(2,1)}, bf16[16,2048]{1,0:T(8,128)(2,1)S(1)}, u32[]{:S(2)}, u32[]{:S(2)}) collective-permute-start(bf16[16,2048]{1,0:T(8,128)(2,1)} %get-tuple-element.13), channel_id=1, source_target_pairs={{0,1},{1,0},{2,3},{3,2},{4,5},{5,4},{6,7},{7,6},{8,9},{9,8},{10,11... | collective-permute-start | bytes 196616 | tf_op jit(solution)/shard_map/ppermute | solution.py:615
  17.7 7.7 %collective-permute-start.3 = (bf16[32,2048]{1,0:T(8,128)(2,1)S(1)}, bf16[32,2048]{1,0:T(8,128)(2,1)S(1)}, u32[]{:S(2)}, u32[]{:S(2)}) collective-permute-start(bf16[32,2048]{1,0:T(8,128)(2,1)S(1)} %constant_dynamic-update-slice_fusion.refs_1_), channel_id=1, source_target_pairs={{0,6},{1,7},{2,0},{3,1},{4,2},{5,3},{6,4},{7,5},{8,14},{9,15},{10,... | collective-permute-start | bytes 393224 | tf_op jit(solution)/shard_map/ppermute | solution.py:617
  20.2 5.9 %collective-permute-start.2 = (bf16[32,2048]{1,0:T(8,128)(2,1)S(1)}, bf16[32,2048]{1,0:T(8,128)(2,1)S(1)}, u32[]{:S(2)}, u32[]{:S(2)}) collective-permute-start(bf16[32,2048]{1,0:T(8,128)(2,1)S(1)} %constant_dynamic-update-slice_fusion.refs_1_), channel_id=1, source_target_pairs={{0,4},{1,5},{2,6},{3,7},{4,0},{5,1},{6,2},{7,3},{8,12},{9,13},{10,... | collective-permute-start | bytes 393224 | tf_op jit(solution)/shard_map/ppermute | solution.py:617
  20.7 9.2 %collective-permute-start.1 = (bf16[32,2048]{1,0:T(8,128)(2,1)S(1)}, bf16[32,2048]{1,0:T(8,128)(2,1)S(1)}, u32[]{:S(2)}, u32[]{:S(2)}) collective-permute-start(bf16[32,2048]{1,0:T(8,128)(2,1)S(1)} %constant_dynamic-update-slice_fusion.refs_1_), channel_id=1, source_target_pairs={{0,2},{1,3},{2,4},{3,5},{4,6},{5,7},{6,0},{7,1},{8,10},{9,11},{10,... | collective-permute-start | bytes 393224 | tf_op jit(solution)/shard_map/ppermute | solution.py:617
  34.2 5.6 %collective-permute-start.6 = (bf16[2,64,512]{2,1,0:T(8,128)(2,1)S(1)}, bf16[2,64,512]{2,1,0:T(8,128)(2,1)S(1)}, u32[]{:S(2)}, u32[]{:S(2)}) collective-permute-start(bf16[2,64,512]{2,1,0:T(8,128)(2,1)S(1)} %get-tuple-element.24), channel_id=1, source_target_pairs={{0,6},{1,7},{2,0},{3,1},{4,2},{5,3},{6,4},{7,5},{8,14},{9,15},{10,... | collective-permute-start | bytes 393224 | tf_op jit(solution)/shard_map/ppermute | solution.py:625
  34.4 5.4 %collective-permute-start.5 = (bf16[2,64,512]{2,1,0:T(8,128)(2,1)S(1)}, bf16[2,64,512]{2,1,0:T(8,128)(2,1)S(1)}, u32[]{:S(2)}, u32[]{:S(2)}) collective-permute-start(bf16[2,64,512]{2,1,0:T(8,128)(2,1)S(1)} %get-tuple-element.25), channel_id=1, source_target_pairs={{0,4},{1,5},{2,6},{3,7},{4,0},{5,1},{6,2},{7,3},{8,12},{9,13},{10,... | collective-permute-start | bytes 393224 | tf_op jit(solution)/shard_map/ppermute | solution.py:625
  34.9 6.2 %collective-permute-start.4 = (bf16[2,64,512]{2,1,0:T(8,128)(2,1)S(1)}, bf16[2,64,512]{2,1,0:T(8,128)(2,1)S(1)}, u32[]{:S(2)}, u32[]{:S(2)}) collective-permute-start(bf16[2,64,512]{2,1,0:T(8,128)(2,1)S(1)} %get-tuple-element.26), channel_id=1, source_target_pairs={{0,2},{1,3},{2,4},{3,5},{4,6},{5,7},{6,0},{7,1},{8,10},{9,11},{10,... | collective-permute-start | bytes 393224 | tf_op jit(solution)/shard_map/ppermute | solution.py:625
  41.2 5.5 %collective-permute-start.7 = (bf16[4,64,512]{2,1,0:T(8,128)(2,1)S(1)}, bf16[4,64,512]{2,1,0:T(8,128)(2,1)S(1)}, u32[]{:S(2)}, u32[]{:S(2)}) collective-permute-start(bf16[4,64,512]{2,1,0:T(8,128)(2,1)S(1)} %pad_maximum_fusion), channel_id=1, source_target_pairs={{0,1},{1,0},{2,3},{3,2},{4,5},{5,4},{6,7},{7,6},{8,9},{9,8},{10,11... | collective-permute-start | bytes 786440 | tf_op jit(solution)/shard_map/ppermute | solution.py:630

commit v7 on v6

--- a/solution.py
+++ b/solution.py
@@ -93,7 +93,8 @@
     dests, blocks = owners_ref.shape
     per_tile = LANES // PH
     one_hot = spread()
-    loads[0].wait()
+    for load in loads:
+        load.wait()
     tiles = jnp.concatenate(
         [records_ref[:, t * LANES : (t + 1) * LANES] for t in range(length // LANES)], axis=0
     )
@@ -117,7 +118,6 @@
     rows, width = owner_count * high * SLOTS * BS, high * stations
     k_of, column = iota((blocks, width), 0), iota((blocks, width), 1)
     expand = jnp.where(column % stations // BS == k_of, 1.0, 0.0)
-    loads[1].wait()
     named = lax.dot_general(
         owners_ref[...].astype(F32), expand, (((1,), (0,)), ((), ())), preferred_element_type=F32
     )
@@ -356,8 +356,15 @@
         phase_ref[s, (FINE - 1 - p) * stations : (FINE - p) * stations, :] = tile.astype(F32)
 
     fold(trace_ref, scale, segs, put)
-    mine = pl.ds(pl.multiple_of(me_ref[0] * stations, stations), stations)
-    tiles = [trace_ref[p, mine, :] * scale for p in range(PH)]
+    mine = pl.ds(pl.multiple_of(me * stations, stations), stations)
+    for p in range(PH):
+        white_ref[:, p * LANES : (p + 1) * LANES] = (trace_ref[p, mine, :] * scale).astype(BF16)
+
+
+def order_kernel(phased_ref, white_ref):
+    stations, length = phased_ref.shape
+    per_tile = LANES // PH
+    tiles = [phased_ref[:, p * LANES : (p + 1) * LANES].astype(F32) for p in range(PH)]
     moved = []
     for t in range(length // LANES):
         turn = (LANES - per_tile // 2 * t) % LANES
@@ -369,6 +376,41 @@
     natural = dot_t(jnp.concatenate(moved, axis=0), gather_back()).astype(BF16)
     for t in range(length // LANES):
         white_ref[:, t * LANES : (t + 1) * LANES] = natural[t * stations : (t + 1) * stations]
+
+
+def in_sample_order(phased):
+    return pl.pallas_call(
+        order_kernel,
+        out_shape=jax.ShapeDtypeStruct(phased.shape, BF16),
+        in_specs=[pl.BlockSpec(memory_space=pltpu.VMEM)],
+        out_specs=pl.BlockSpec(memory_space=pltpu.VMEM),
+        compiler_params=pltpu.CompilerParams(vmem_limit_bytes=8 * MIB),
+        cost_estimate=pl.CostEstimate(flops=1000 * MIB, bytes_accessed=MIB, transcendentals=0),
+        name="order",
+    )(phased)
+
+
+def pack_kernel(me_ref, *refs):
+    near, out_ref = refs[:-1], refs[-1]
+    other = 1 - (me_ref[0] & (CORES - 1))
+    chip = lax.div(me_ref[0], CORES)
+    for i, ref in enumerate(near):
+        out_ref[i] = ref[(chip * CORES if i == 0 else 0) + other]
+
+
+def pack(me, near):
+    return pl.pallas_call(
+        pack_kernel,
+        out_shape=jax.ShapeDtypeStruct((len(near), *near[0].shape[1:]), BF16),
+        in_specs=[
+            pl.BlockSpec(memory_space=pltpu.SMEM),
+            *[pl.BlockSpec(memory_space=pltpu.VMEM)] * len(near),
+        ],
+        out_specs=pl.BlockSpec(memory_space=pltpu.VMEM),
+        compiler_params=pltpu.CompilerParams(vmem_limit_bytes=8 * MIB),
+        cost_estimate=pl.CostEstimate(flops=0, bytes_accessed=MIB, transcendentals=0),
+        name="pack",
+    )(me, *near)
 
 
 def own_part(me, pairs, segs):
@@ -615,7 +657,7 @@
     other = lax.ppermute(phased, "seg", across)
     pair = jnp.concatenate([phased, other], axis=0)
     pairs = [pair] + [lax.ppermute(pair, "seg", along_x[k]) for k in range(1, chips)]
-    whitened, phases = own_part(me.reshape(1), pairs, segs)
+    mine, phases = own_part(me.reshape(1), pairs, segs)
     passing, phases = lax.optimization_barrier((passing, phases))
     shifted, extra = shift(phases)
     near = [passing]
@@ -623,11 +665,9 @@
         at = ((chip + k) & (chips - 1)) * CORES
         block = lax.dynamic_slice_in_dim(passing, at, CORES, 0)
         near.append(lax.ppermute(block, "seg", along_x[k]))
-    other_core = 1 - (me & (CORES - 1))
-    give = [lax.dynamic_slice_in_dim(passing, chip * CORES + other_core, 1, 0)]
-    give += [lax.dynamic_slice_in_dim(block, other_core, 1, 0) for block in near[1:]]
-    give, shifted, extra = lax.optimization_barrier((jnp.concatenate(give, axis=0), shifted, extra))
-    far = lax.ppermute(give, "seg", across)
+    near, shifted, extra, mine = lax.optimization_barrier((near, shifted, extra, mine))
+    far = lax.ppermute(pack(me.reshape(1), near), "seg", across)
+    whitened = in_sample_order(mine)
     result = correlate(me.reshape(1), near, far, shifted, extra, segs)
     return whitened, result.reshape(-1, stations, LAGS)
 

time: 59.9 us -> 59.5 us (level)
  waiting for transfers between devices: 11.3 us -> 10.4 us
  starting transfers between devices: 22.6 us -> 23.3 us
    pallas_call x0 -> x2, Pallas kernels: none -> 1.16 us  [the longest x1 1.14 us: in_sample_order(): pl.pallas_call(order_kernel, out_shape=jax.ShapeDtypeStruct(phased.shape,...]
    ppermute x1, waiting for transfers between devices: 1.16 us -> 0.02 us  [on_device(): far = lax.ppermute(pack(me.reshape(1), near), 'seg', across)]
    pallas_call x1, Pallas kernels: 4.23 us -> 3.15 us  [own_part(): pl.pallas_call(lambda *refs: own_kernel(segs, *refs), out_shape=(jax.Shap...]
    ppermute x3, starting transfers between devices: 1.63 us -> 2.41 us  [on_device(): near.append(lax.ppermute(block, 'seg', along_x[k]))]
where the time goes in v7:
time: 59.5 us; the launch traced here: 59.2 us
  Pallas kernels  23.8 us (40%)
  starting transfers between devices  23.3 us (39%)
  waiting for transfers between devices  10.4 us (17%)
  local copies, waits for them, and re-layouts  0.89 us (1%)
  between operations  0.86 us (1%)
    pallas_call x1, Pallas kernels, correlate(): pl.pallas_call(lambda *refs: correlate_kernel(segs, *refs), out_shape=jax...  12.9 us
    all_to_all x1, starting transfers between devices, on_device(): passing = lax.all_to_all(slots, 'sta', 0, 0, tiled=True)  12 us
    ppermute x3, waiting for transfers between devices, on_device(): lax.ppermute(pair, 'seg', along_x[k])  8.62 us
    ppermute x1, starting transfers between devices, on_device(): far = lax.ppermute(pack(me.reshape(1), near), 'seg', across)  4.18 us
    pallas_call x1, Pallas kernels, shift(): pl.pallas_call(lambda *refs: shift_kernel(stations, *refs), out_shape=(pl...  3.94 us
    ppermute x3, starting transfers between devices, on_device(): lax.ppermute(pair, 'seg', along_x[k])  3.59 us
    pallas_call x1, Pallas kernels, own_part(): pl.pallas_call(lambda *refs: own_kernel(segs, *refs), out_shape=(jax.Shap...  3.15 us
    pallas_call x1, Pallas kernels, prepare(): pl.pallas_call(lambda *refs: prepare_kernel(owner_count, *refs), out_shap...  2.62 us
  transfers between devices with their start and end apart: 9, of which 6 were waited for; matrix products, arithmetic and copies ran while one was open for 1% of the time, Pallas kernels for 14%

profile of v7, /device:TPU:1, one launch (start us, length us, event | category | flops | bytes accessed | tf_op | source)
XLA Modules:
  0.0 59.2 jit_solution(4452475931411904996)
XLA Ops:
  0.6 2.6 %prepare.1 = (bf16[16,2048]{1,0:T(8,128)(2,1)}, bf16[512,512]{1,0:T(8,128)(2,1)}) custom-call(bf16[16,2048]{1,0:T(8,128)(2,1)} %refs_0_.1, s32[4,8]{1,0:T(4,128)} %bitcast.9), custom_call_target="tpu_custom_call" | custom-call | flops 104857600 | bytes 2097152 | tf_op jit(solution)/shard_map/prepare/pallas_call | solution.py:156
  3.3 12.0 %all-to-all-start = ((bf16[32,16,512]{2,1,0:T(8,128)(2,1)}), bf16[32,16,512]{2,1,0:T(8,128)(2,1)S(1)}, u32[]{:S(2)}, u32[]{:S(2)}) async-start(bf16[32,16,512]{2,1,0:T(8,128)(2,1)} %bitcast.8), calls=%async_computation | async-start | bytes 1048576 | tf_op jit(solution)/shard_map/all_to_all | solution.py:655
  15.3 1.0 %collective-permute-start = (bf16[16,2048]{1,0:T(8,128)(2,1)}, bf16[16,2048]{1,0:T(8,128)(2,1)S(1)}, u32[]{:S(2)}, u32[]{:S(2)}) collective-permute-start(bf16[16,2048]{1,0:T(8,128)(2,1)} %get-tuple-element.18), channel_id=1, source_target_pairs={{0,1},{1,0},{2,3},{3,2},{4,5},{5,4},{6,7},{7,6},{8,9},{9,8},{10,11... | collective-permute-start | bytes 196616 | tf_op jit(solution)/shard_map/ppermute | solution.py:657
  16.4 0.8 %constant_dynamic-update-slice_fusion.1 = bf16[32,2048]{1,0:T(8,128)(2,1)S(1)} fusion(bf16[16,2048]{1,0:T(8,128)(2,1)} %get-tuple-element.18), kind=kLoop, calls=%fused_computation.1 | loop fusion | bytes 131072
  17.2 0.3 collective-permute-done
  17.5 2.5 %collective-permute-start.3 = (bf16[32,2048]{1,0:T(8,128)(2,1)S(1)}, bf16[32,2048]{1,0:T(8,128)(2,1)S(1)}, u32[]{:S(2)}, u32[]{:S(2)}) collective-permute-start(bf16[32,2048]{1,0:T(8,128)(2,1)S(1)} %constant_dynamic-update-slice_fusion.refs_1_), channel_id=1, source_target_pairs={{0,6},{1,7},{2,0},{3,1},{4,2},{5,3},{6,4},{7,5},{8,14},{9,15},{10,... | collective-permute-start | bytes 393224 | tf_op jit(solution)/shard_map/ppermute | solution.py:659
  20.0 0.5 collective-permute-start.2
  20.5 0.6 %collective-permute-start.1 = (bf16[32,2048]{1,0:T(8,128)(2,1)S(1)}, bf16[32,2048]{1,0:T(8,128)(2,1)S(1)}, u32[]{:S(2)}, u32[]{:S(2)}) collective-permute-start(bf16[32,2048]{1,0:T(8,128)(2,1)S(1)} %constant_dynamic-update-slice_fusion.refs_1_), channel_id=1, source_target_pairs={{0,2},{1,3},{2,4},{3,5},{4,6},{5,7},{6,0},{7,1},{8,10},{9,11},{10,... | collective-permute-start | bytes 393224 | tf_op jit(solution)/shard_map/ppermute | solution.py:659
  21.1 4.1 %collective-permute-done.3.refs_4_ = bf16[32,2048]{1,0:T(8,128)(2,1)S(1)} collective-permute-done((bf16[32,2048]{1,0:T(8,128)(2,1)S(1)}, bf16[32,2048]{1,0:T(8,128)(2,1)S(1)}, u32[]{:S(2)}, u32[]{:S(2)}) %collective-permute-start.3) | collective-permute-done | bytes 131104 | tf_op jit(solution)/shard_map/ppermute | solution.py:659
  25.2 0.7 %collective-permute-done.2.refs_3_ = bf16[32,2048]{1,0:T(8,128)(2,1)S(1)} collective-permute-done((bf16[32,2048]{1,0:T(8,128)(2,1)S(1)}, bf16[32,2048]{1,0:T(8,128)(2,1)S(1)}, u32[]{:S(2)}, u32[]{:S(2)}) %collective-permute-start.2) | collective-permute-done | bytes 131104 | tf_op jit(solution)/shard_map/ppermute | solution.py:659
  25.9 3.8 %collective-permute-done.1.refs_2_ = bf16[32,2048]{1,0:T(8,128)(2,1)S(1)} collective-permute-done((bf16[32,2048]{1,0:T(8,128)(2,1)S(1)}, bf16[32,2048]{1,0:T(8,128)(2,1)S(1)}, u32[]{:S(2)}, u32[]{:S(2)}) %collective-permute-start.1) | collective-permute-done | bytes 131104 | tf_op jit(solution)/shard_map/ppermute | solution.py:659
  29.7 3.1 %own.1 = (bf16[16,2048]{1,0:T(8,128)(2,1)S(1)}, f32[4,512,128]{2,1,0:T(8,128)S(1)}) custom-call(s32[1]{0:T(128)} %bitcast.3.refs_0_.me_ref, bf16[32,2048]{1,0:T(8,128)(2,1)S(1)} %constant_dynamic-update-slice_fusion.refs_1_, bf16[32,2048]{1,0:T(8,128)(2,1)S(1)} %collective-permute-done.1.refs_2_, bf16[32,2048]{1,0:T(8,128)(2,1)S(1)} %collective-permute-done.2.refs_3_, ...), custom_call_target="tpu_custom_call" | custom-call | flops 2097152000 | bytes 4194304 | tf_op jit(solution)/shard_map/own/pallas_call | solution.py:419
  32.8 0.0 all-to-all-done
  32.9 1.2 %collective-permute-start.6 = (bf16[2,64,512]{2,1,0:T(8,128)(2,1)S(1)}, bf16[2,64,512]{2,1,0:T(8,128)(2,1)S(1)}, u32[]{:S(2)}, u32[]{:S(2)}) collective-permute-start(bf16[2,64,512]{2,1,0:T(8,128)(2,1)S(1)} %get-tuple-element.32), channel_id=1, source_target_pairs={{0,6},{1,7},{2,0},{3,1},{4,2},{5,3},{6,4},{7,5},{8,14},{9,15},{10,... | collective-permute-start | bytes 393224 | tf_op jit(solution)/shard_map/ppermute | solution.py:667
  34.1 0.6 %collective-permute-start.5 = (bf16[2,64,512]{2,1,0:T(8,128)(2,1)S(1)}, bf16[2,64,512]{2,1,0:T(8,128)(2,1)S(1)}, u32[]{:S(2)}, u32[]{:S(2)}) collective-permute-start(bf16[2,64,512]{2,1,0:T(8,128)(2,1)S(1)} %get-tuple-element.33), channel_id=1, source_target_pairs={{0,4},{1,5},{2,6},{3,7},{4,0},{5,1},{6,2},{7,3},{8,12},{9,13},{10,... | collective-permute-start | bytes 393224 | tf_op jit(solution)/shard_map/ppermute | solution.py:667
  34.7 0.6 %collective-permute-start.4 = (bf16[2,64,512]{2,1,0:T(8,128)(2,1)S(1)}, bf16[2,64,512]{2,1,0:T(8,128)(2,1)S(1)}, u32[]{:S(2)}, u32[]{:S(2)}) collective-permute-start(bf16[2,64,512]{2,1,0:T(8,128)(2,1)S(1)} %get-tuple-element.34), channel_id=1, source_target_pairs={{0,2},{1,3},{2,4},{3,5},{4,6},{5,7},{6,0},{7,1},{8,10},{9,11},{10,... | collective-permute-start | bytes 393224 | tf_op jit(solution)/shard_map/ppermute | solution.py:667
  35.3 3.9 %shift.1 = (bf16[8192,512]{1,0:T(8,128)(2,1)}, bf16[512,512]{1,0:T(8,128)(2,1)}) custom-call(f32[4,512,128]{2,1,0:T(8,128)S(1)} %get-tuple-element.21.refs_0_), custom_call_target="tpu_custom_call" | custom-call | flops 1 | bytes 9437184 | tf_op jit(solution)/shard_map/shift/pallas_call | solution.py:488
  39.3 0.0 collective-permute-done.6.refs_3_.refs_4_
  39.3 0.2 collective-permute-done.5.refs_2_.refs_3_
  39.5 1.3 %collective-permute-done.4.refs_1_.refs_2_ = bf16[2,64,512]{2,1,0:T(8,128)(2,1)S(1)} collective-permute-done((bf16[2,64,512]{2,1,0:T(8,128)(2,1)S(1)}, bf16[2,64,512]{2,1,0:T(8,128)(2,1)S(1)}, u32[]{:S(2)}, u32[]{:S(2)}) %collective-permute-start.4) | collective-permute-done | bytes 131104 | tf_op jit(solution)/shard_map/ppermute | solution.py:667
  40.8 4.2 %collective-permute-start.7 = (bf16[4,64,512]{2,1,0:T(8,128)(2,1)S(1)}, bf16[4,64,512]{2,1,0:T(8,128)(2,1)S(1)}, u32[]{:S(2)}, u32[]{:S(2)}) collective-permute-start(bf16[4,64,512]{2,1,0:T(8,128)(2,1)S(1)} %pack.1), channel_id=1, source_target_pairs={{0,1},{1,0},{2,3},{3,2},{4,5},{5,4},{6,7},{7,6},{8,9},{9,8},{10,11... | collective-permute-start | bytes 786440 | tf_op jit(solution)/shard_map/ppermute | solution.py:669
  45.0 1.1 %order.1 = bf16[16,2048]{1,0:T(8,128)(2,1)} custom-call(bf16[16,2048]{1,0:T(8,128)(2,1)S(1)} %get-tuple-element.25.phased_ref), custom_call_target="tpu_custom_call" | custom-call | flops 1048576000 | bytes 1048576 | tf_op jit(solution)/shard_map/order/pallas_call | solution.py:382
  46.1 0.0 collective-permute-done.7.refs_5_
  46.2 12.9 %correlate.1 = bf16[256,512]{1,0:T(8,128)(2,1)} custom-call(s32[1]{0:T(128)} %bitcast.3.refs_0_.me_ref, bf16[8,64,512]{2,1,0:T(8,128)(2,1)S(1)} %bitcast.7, bf16[2,64,512]{2,1,0:T(8,128)(2,1)S(1)} %collective-permute-done.4.refs_1_.refs_2_, bf16[2,64,512]{2,1,0:T(8,128)(2,1)S(1)} %collective-permute-done.5.refs_2_.refs_3_, ...), custom_call_target="tpu_custom_call" | custom-call | flops 6291456000 | bytes 20971520 | tf_op jit(solution)/shard_map/correlate/pallas_call | solution.py:610
  (3 shorter events, 0.1 us)
Async XLA Ops:
  3.3 29.6 %all-to-all-start = ((bf16[32,16,512]{2,1,0:T(8,128)(2,1)}), bf16[32,16,512]{2,1,0:T(8,128)(2,1)S(1)}, u32[]{:S(2)}, u32[]{:S(2)}) async-start(bf16[32,16,512]{2,1,0:T(8,128)(2,1)} %bitcast.8), calls=%async_computation | async-start | bytes 1048576 | tf_op jit(solution)/shard_map/all_to_all | solution.py:655
  15.3 2.2 %collective-permute-start = (bf16[16,2048]{1,0:T(8,128)(2,1)}, bf16[16,2048]{1,0:T(8,128)(2,1)S(1)}, u32[]{:S(2)}, u32[]{:S(2)}) collective-permute-start(bf16[16,2048]{1,0:T(8,128)(2,1)} %get-tuple-element.18), channel_id=1, source_target_pairs={{0,1},{1,0},{2,3},{3,2},{4,5},{5,4},{6,7},{7,6},{8,9},{9,8},{10,11... | collective-permute-start | bytes 196616 | tf_op jit(solution)/shard_map/ppermute | solution.py:657
  17.5 7.7 %collective-permute-start.3 = (bf16[32,2048]{1,0:T(8,128)(2,1)S(1)}, bf16[32,2048]{1,0:T(8,128)(2,1)S(1)}, u32[]{:S(2)}, u32[]{:S(2)}) collective-permute-start(bf16[32,2048]{1,0:T(8,128)(2,1)S(1)} %constant_dynamic-update-slice_fusion.refs_1_), channel_id=1, source_target_pairs={{0,6},{1,7},{2,0},{3,1},{4,2},{5,3},{6,4},{7,5},{8,14},{9,15},{10,... | collective-permute-start | bytes 393224 | tf_op jit(solution)/shard_map/ppermute | solution.py:659
  20.0 5.9 %collective-permute-start.2 = (bf16[32,2048]{1,0:T(8,128)(2,1)S(1)}, bf16[32,2048]{1,0:T(8,128)(2,1)S(1)}, u32[]{:S(2)}, u32[]{:S(2)}) collective-permute-start(bf16[32,2048]{1,0:T(8,128)(2,1)S(1)} %constant_dynamic-update-slice_fusion.refs_1_), channel_id=1, source_target_pairs={{0,4},{1,5},{2,6},{3,7},{4,0},{5,1},{6,2},{7,3},{8,12},{9,13},{10,... | collective-permute-start | bytes 393224 | tf_op jit(solution)/shard_map/ppermute | solution.py:659
  20.5 9.2 %collective-permute-start.1 = (bf16[32,2048]{1,0:T(8,128)(2,1)S(1)}, bf16[32,2048]{1,0:T(8,128)(2,1)S(1)}, u32[]{:S(2)}, u32[]{:S(2)}) collective-permute-start(bf16[32,2048]{1,0:T(8,128)(2,1)S(1)} %constant_dynamic-update-slice_fusion.refs_1_), channel_id=1, source_target_pairs={{0,2},{1,3},{2,4},{3,5},{4,6},{5,7},{6,0},{7,1},{8,10},{9,11},{10,... | collective-permute-start | bytes 393224 | tf_op jit(solution)/shard_map/ppermute | solution.py:659
  32.9 6.4 %collective-permute-start.6 = (bf16[2,64,512]{2,1,0:T(8,128)(2,1)S(1)}, bf16[2,64,512]{2,1,0:T(8,128)(2,1)S(1)}, u32[]{:S(2)}, u32[]{:S(2)}) collective-permute-start(bf16[2,64,512]{2,1,0:T(8,128)(2,1)S(1)} %get-tuple-element.32), channel_id=1, source_target_pairs={{0,6},{1,7},{2,0},{3,1},{4,2},{5,3},{6,4},{7,5},{8,14},{9,15},{10,... | collective-permute-start | bytes 393224 | tf_op jit(solution)/shard_map/ppermute | solution.py:667
  34.1 5.4 %collective-permute-start.5 = (bf16[2,64,512]{2,1,0:T(8,128)(2,1)S(1)}, bf16[2,64,512]{2,1,0:T(8,128)(2,1)S(1)}, u32[]{:S(2)}, u32[]{:S(2)}) collective-permute-start(bf16[2,64,512]{2,1,0:T(8,128)(2,1)S(1)} %get-tuple-element.33), channel_id=1, source_target_pairs={{0,4},{1,5},{2,6},{3,7},{4,0},{5,1},{6,2},{7,3},{8,12},{9,13},{10,... | collective-permute-start | bytes 393224 | tf_op jit(solution)/shard_map/ppermute | solution.py:667
  34.7 6.1 %collective-permute-start.4 = (bf16[2,64,512]{2,1,0:T(8,128)(2,1)S(1)}, bf16[2,64,512]{2,1,0:T(8,128)(2,1)S(1)}, u32[]{:S(2)}, u32[]{:S(2)}) collective-permute-start(bf16[2,64,512]{2,1,0:T(8,128)(2,1)S(1)} %get-tuple-element.34), channel_id=1, source_target_pairs={{0,2},{1,3},{2,4},{3,5},{4,6},{5,7},{6,0},{7,1},{8,10},{9,11},{10,... | collective-permute-start | bytes 393224 | tf_op jit(solution)/shard_map/ppermute | solution.py:667
  40.8 5.3 %collective-permute-start.7 = (bf16[4,64,512]{2,1,0:T(8,128)(2,1)S(1)}, bf16[4,64,512]{2,1,0:T(8,128)(2,1)S(1)}, u32[]{:S(2)}, u32[]{:S(2)}) collective-permute-start(bf16[4,64,512]{2,1,0:T(8,128)(2,1)S(1)} %pack.1), channel_id=1, source_target_pairs={{0,1},{1,0},{2,3},{3,2},{4,5},{5,4},{6,7},{7,6},{8,9},{9,8},{10,11... | collective-permute-start | bytes 786440 | tf_op jit(solution)/shard_map/ppermute | solution.py:669

commit v8 on v7

--- a/solution.py
+++ b/solution.py
@@ -15,6 +15,7 @@
 
 PH = 16
 LANES = 128
+STEPS = (0, 2, 1, 3)
 FINE = 32
 CORES = 2
 GROUP = 4
@@ -343,7 +344,7 @@
     per_tile = LANES // PH
     me, chips = me_ref[0], segs // CORES
     for i, ref in enumerate(pairs):
-        chip = (lax.div(me, CORES) + chips - i) & (chips - 1)
+        chip = (lax.div(me, CORES) + chips - STEPS[i]) & (chips - 1)
         for j in range(CORES):
             core = (me + j) & (CORES - 1)
             at = pl.ds(pl.multiple_of((chip * CORES + core) * stations, stations), stations)
@@ -535,7 +536,7 @@
     mine = me & (CORES - 1)
     for s in range(segs):
         i = s // CORES
-        chip = (lax.div(me, CORES) + chips - i) & (chips - 1)
+        chip = (lax.div(me, CORES) + chips - STEPS[i]) & (chips - 1)
         if s % CORES:
             source, seg = far_ref[i], chip * CORES + 1 - mine
         else:
@@ -656,12 +657,12 @@
     passing = passing.reshape(segs, -1, GROUP * LANES)
     other = lax.ppermute(phased, "seg", across)
     pair = jnp.concatenate([phased, other], axis=0)
-    pairs = [pair] + [lax.ppermute(pair, "seg", along_x[k]) for k in range(1, chips)]
+    pairs = [pair] + [lax.ppermute(pair, "seg", along_x[k]) for k in STEPS[1:]]
     mine, phases = own_part(me.reshape(1), pairs, segs)
     passing, phases = lax.optimization_barrier((passing, phases))
     shifted, extra = shift(phases)
     near = [passing]
-    for k in range(1, chips):
+    for k in STEPS[1:]:
         at = ((chip + k) & (chips - 1)) * CORES
         block = lax.dynamic_slice_in_dim(passing, at, CORES, 0)
         near.append(lax.ppermute(block, "seg", along_x[k]))

time: 59.5 us -> 59.2 us (level)
  waiting for transfers between devices: 10.4 us -> 7.63 us
  starting transfers between devices: 23.3 us -> 25.8 us
    ppermute x3, waiting for transfers between devices: 8.62 us -> 5.75 us  [on_device(): pairs = [pair] + [lax.ppermute(pair, 'seg', along_x[k]) for k in STEPS[1:]]]
    ppermute x3, starting transfers between devices: 2.41 us -> 4.32 us  [on_device(): near.append(lax.ppermute(block, 'seg', along_x[k]))]
    all_to_all x1, waiting for transfers between devices: 0.01 us -> 0.97 us  [on_device(): passing = lax.all_to_all(slots, 'sta', 0, 0, tiled=True)]
    ppermute x3, waiting for transfers between devices: 1.51 us -> 0.62 us  [on_device(): near.append(lax.ppermute(block, 'seg', along_x[k]))]
    ppermute x3, starting transfers between devices: 3.59 us -> 4.2 us  [on_device(): pairs = [pair] + [lax.ppermute(pair, 'seg', along_x[k]) for k in STEPS[1:]]]
where the time goes in v8:
time: 59.2 us; the launch traced here: 58.9 us
  starting transfers between devices  25.8 us (44%)
  Pallas kernels  23.8 us (40%)
  waiting for transfers between devices  7.63 us (13%)
  local copies, waits for them, and re-layouts  0.88 us (1%)
  between operations  0.85 us (1%)
    pallas_call x1, Pallas kernels, correlate(): pl.pallas_call(lambda *refs: correlate_kernel(segs, *refs), out_shape=jax...  12.9 us
    all_to_all x1, starting transfers between devices, on_device(): passing = lax.all_to_all(slots, 'sta', 0, 0, tiled=True)  12 us
    ppermute x3, waiting for transfers between devices, on_device(): pairs = [pair] + [lax.ppermute(pair, 'seg', along_x[k]) for k in STEPS[1:]]  5.75 us
    ppermute x3, starting transfers between devices, on_device(): near.append(lax.ppermute(block, 'seg', along_x[k]))  4.32 us
    ppermute x3, starting transfers between devices, on_device(): pairs = [pair] + [lax.ppermute(pair, 'seg', along_x[k]) for k in STEPS[1:]]  4.2 us
    ppermute x1, starting transfers between devices, on_device(): far = lax.ppermute(pack(me.reshape(1), near), 'seg', across)  4.18 us
    pallas_call x1, Pallas kernels, shift(): pl.pallas_call(lambda *refs: shift_kernel(stations, *refs), out_shape=(pl...  3.94 us
    pallas_call x1, Pallas kernels, own_part(): pl.pallas_call(lambda *refs: own_kernel(segs, *refs), out_shape=(jax.Shap...  3.15 us
  transfers between devices with their start and end apart: 9, of which 6 were waited for; matrix products, arithmetic and copies ran while one was open for 1% of the time, Pallas kernels for 14%

profile of v8, /device:TPU:1, one launch (start us, length us, event | category | flops | bytes accessed | tf_op | source)
XLA Modules:
  0.0 58.9 jit_solution(3391174931630809211)
XLA Ops:
  0.6 2.6 %prepare.1 = (bf16[16,2048]{1,0:T(8,128)(2,1)}, bf16[512,512]{1,0:T(8,128)(2,1)}) custom-call(bf16[16,2048]{1,0:T(8,128)(2,1)} %refs_0_.1, s32[4,8]{1,0:T(4,128)} %bitcast.9), custom_call_target="tpu_custom_call" | custom-call | flops 104857600 | bytes 2097152 | tf_op jit(solution)/shard_map/prepare/pallas_call | solution.py:157
  3.3 12.0 %all-to-all-start = ((bf16[32,16,512]{2,1,0:T(8,128)(2,1)}), bf16[32,16,512]{2,1,0:T(8,128)(2,1)S(1)}, u32[]{:S(2)}, u32[]{:S(2)}) async-start(bf16[32,16,512]{2,1,0:T(8,128)(2,1)} %bitcast.8), calls=%async_computation | async-start | bytes 1048576 | tf_op jit(solution)/shard_map/all_to_all | solution.py:656
  15.3 1.0 %collective-permute-start = (bf16[16,2048]{1,0:T(8,128)(2,1)}, bf16[16,2048]{1,0:T(8,128)(2,1)S(1)}, u32[]{:S(2)}, u32[]{:S(2)}) collective-permute-start(bf16[16,2048]{1,0:T(8,128)(2,1)} %get-tuple-element.18), channel_id=1, source_target_pairs={{0,1},{1,0},{2,3},{3,2},{4,5},{5,4},{6,7},{7,6},{8,9},{9,8},{10,11... | collective-permute-start | bytes 196616 | tf_op jit(solution)/shard_map/ppermute | solution.py:658
  16.4 0.8 %constant_dynamic-update-slice_fusion.1 = bf16[32,2048]{1,0:T(8,128)(2,1)S(1)} fusion(bf16[16,2048]{1,0:T(8,128)(2,1)} %get-tuple-element.18), kind=kLoop, calls=%fused_computation.1 | loop fusion | bytes 131072
  17.2 0.3 collective-permute-done
  17.5 2.5 %collective-permute-start.3 = (bf16[32,2048]{1,0:T(8,128)(2,1)S(1)}, bf16[32,2048]{1,0:T(8,128)(2,1)S(1)}, u32[]{:S(2)}, u32[]{:S(2)}) collective-permute-start(bf16[32,2048]{1,0:T(8,128)(2,1)S(1)} %constant_dynamic-update-slice_fusion.refs_1_), channel_id=1, source_target_pairs={{0,6},{1,7},{2,0},{3,1},{4,2},{5,3},{6,4},{7,5},{8,14},{9,15},{10,... | collective-permute-start | bytes 393224 | tf_op jit(solution)/shard_map/ppermute | solution.py:660
  20.0 0.0 collective-permute-start.2
  20.0 1.7 %collective-permute-start.1 = (bf16[32,2048]{1,0:T(8,128)(2,1)S(1)}, bf16[32,2048]{1,0:T(8,128)(2,1)S(1)}, u32[]{:S(2)}, u32[]{:S(2)}) collective-permute-start(bf16[32,2048]{1,0:T(8,128)(2,1)S(1)} %constant_dynamic-update-slice_fusion.refs_1_), channel_id=1, source_target_pairs={{0,4},{1,5},{2,6},{3,7},{4,0},{5,1},{6,2},{7,3},{8,12},{9,13},{10,... | collective-permute-start | bytes 393224 | tf_op jit(solution)/shard_map/ppermute | solution.py:660
  21.7 0.8 %collective-permute-done.3.refs_4_ = bf16[32,2048]{1,0:T(8,128)(2,1)S(1)} collective-permute-done((bf16[32,2048]{1,0:T(8,128)(2,1)S(1)}, bf16[32,2048]{1,0:T(8,128)(2,1)S(1)}, u32[]{:S(2)}, u32[]{:S(2)}) %collective-permute-start.3) | collective-permute-done | bytes 131104 | tf_op jit(solution)/shard_map/ppermute | solution.py:660
  22.5 4.4 %collective-permute-done.2.refs_3_ = bf16[32,2048]{1,0:T(8,128)(2,1)S(1)} collective-permute-done((bf16[32,2048]{1,0:T(8,128)(2,1)S(1)}, bf16[32,2048]{1,0:T(8,128)(2,1)S(1)}, u32[]{:S(2)}, u32[]{:S(2)}) %collective-permute-start.2) | collective-permute-done | bytes 131104 | tf_op jit(solution)/shard_map/ppermute | solution.py:660
  26.9 0.6 collective-permute-done.1.refs_2_
  27.4 3.2 %own.1 = (bf16[16,2048]{1,0:T(8,128)(2,1)S(1)}, f32[4,512,128]{2,1,0:T(8,128)S(1)}) custom-call(s32[1]{0:T(128)} %bitcast.3.refs_0_.me_ref, bf16[32,2048]{1,0:T(8,128)(2,1)S(1)} %constant_dynamic-update-slice_fusion.refs_1_, bf16[32,2048]{1,0:T(8,128)(2,1)S(1)} %collective-permute-done.1.refs_2_, bf16[32,2048]{1,0:T(8,128)(2,1)S(1)} %collective-permute-done.2.refs_3_, ...), custom_call_target="tpu_custom_call" | custom-call | flops 2097152000 | bytes 4194304 | tf_op jit(solution)/shard_map/own/pallas_call | solution.py:420
  30.6 1.0 %all-to-all-done = bf16[32,16,512]{2,1,0:T(8,128)(2,1)S(1)} async-done(((bf16[32,16,512]{2,1,0:T(8,128)(2,1)}), bf16[32,16,512]{2,1,0:T(8,128)(2,1)S(1)}, u32[]{:S(2)}, u32[]{:S(2)}) %all-to-all-start) | async-done | bytes 524320 | tf_op jit(solution)/shard_map/all_to_all | solution.py:656
  31.6 2.5 %collective-permute-start.6 = (bf16[2,64,512]{2,1,0:T(8,128)(2,1)S(1)}, bf16[2,64,512]{2,1,0:T(8,128)(2,1)S(1)}, u32[]{:S(2)}, u32[]{:S(2)}) collective-permute-start(bf16[2,64,512]{2,1,0:T(8,128)(2,1)S(1)} %get-tuple-element.32), channel_id=1, source_target_pairs={{0,6},{1,7},{2,0},{3,1},{4,2},{5,3},{6,4},{7,5},{8,14},{9,15},{10,... | collective-permute-start | bytes 393224 | tf_op jit(solution)/shard_map/ppermute | solution.py:668
  34.1 0.0 collective-permute-start.5
  34.1 1.9 %collective-permute-start.4 = (bf16[2,64,512]{2,1,0:T(8,128)(2,1)S(1)}, bf16[2,64,512]{2,1,0:T(8,128)(2,1)S(1)}, u32[]{:S(2)}, u32[]{:S(2)}) collective-permute-start(bf16[2,64,512]{2,1,0:T(8,128)(2,1)S(1)} %get-tuple-element.34), channel_id=1, source_target_pairs={{0,4},{1,5},{2,6},{3,7},{4,0},{5,1},{6,2},{7,3},{8,12},{9,13},{10,... | collective-permute-start | bytes 393224 | tf_op jit(solution)/shard_map/ppermute | solution.py:668
  35.9 3.9 %shift.1 = (bf16[8192,512]{1,0:T(8,128)(2,1)}, bf16[512,512]{1,0:T(8,128)(2,1)}) custom-call(f32[4,512,128]{2,1,0:T(8,128)S(1)} %get-tuple-element.21.refs_0_), custom_call_target="tpu_custom_call" | custom-call | flops 1 | bytes 9437184 | tf_op jit(solution)/shard_map/shift/pallas_call | solution.py:489
  39.9 0.0 collective-permute-done.6.refs_3_.refs_4_
  39.9 0.6 %collective-permute-done.5.refs_2_.refs_3_ = bf16[2,64,512]{2,1,0:T(8,128)(2,1)S(1)} collective-permute-done((bf16[2,64,512]{2,1,0:T(8,128)(2,1)S(1)}, bf16[2,64,512]{2,1,0:T(8,128)(2,1)S(1)}, u32[]{:S(2)}, u32[]{:S(2)}) %collective-permute-start.5) | collective-permute-done | bytes 131104 | tf_op jit(solution)/shard_map/ppermute | solution.py:668
  40.5 0.0 collective-permute-done.4.refs_1_.refs_2_
  40.5 4.2 %collective-permute-start.7 = (bf16[4,64,512]{2,1,0:T(8,128)(2,1)S(1)}, bf16[4,64,512]{2,1,0:T(8,128)(2,1)S(1)}, u32[]{:S(2)}, u32[]{:S(2)}) collective-permute-start(bf16[4,64,512]{2,1,0:T(8,128)(2,1)S(1)} %pack.1), channel_id=1, source_target_pairs={{0,1},{1,0},{2,3},{3,2},{4,5},{5,4},{6,7},{7,6},{8,9},{9,8},{10,11... | collective-permute-start | bytes 786440 | tf_op jit(solution)/shard_map/ppermute | solution.py:670
  44.7 1.1 %order.1 = bf16[16,2048]{1,0:T(8,128)(2,1)} custom-call(bf16[16,2048]{1,0:T(8,128)(2,1)S(1)} %get-tuple-element.25.phased_ref), custom_call_target="tpu_custom_call" | custom-call | flops 1048576000 | bytes 1048576 | tf_op jit(solution)/shard_map/order/pallas_call | solution.py:383
  45.8 0.0 collective-permute-done.7.refs_5_
  45.9 12.9 %correlate.1 = bf16[256,512]{1,0:T(8,128)(2,1)} custom-call(s32[1]{0:T(128)} %bitcast.3.refs_0_.me_ref, bf16[8,64,512]{2,1,0:T(8,128)(2,1)S(1)} %bitcast.7, bf16[2,64,512]{2,1,0:T(8,128)(2,1)S(1)} %collective-permute-done.4.refs_1_.refs_2_, bf16[2,64,512]{2,1,0:T(8,128)(2,1)S(1)} %collective-permute-done.5.refs_2_.refs_3_, ...), custom_call_target="tpu_custom_call" | custom-call | flops 6291456000 | bytes 20971520 | tf_op jit(solution)/shard_map/correlate/pallas_call | solution.py:611
  (3 shorter events, 0.1 us)
Async XLA Ops:
  3.3 28.3 %all-to-all-start = ((bf16[32,16,512]{2,1,0:T(8,128)(2,1)}), bf16[32,16,512]{2,1,0:T(8,128)(2,1)S(1)}, u32[]{:S(2)}, u32[]{:S(2)}) async-start(bf16[32,16,512]{2,1,0:T(8,128)(2,1)} %bitcast.8), calls=%async_computation | async-start | bytes 1048576 | tf_op jit(solution)/shard_map/all_to_all | solution.py:656
  15.3 2.2 %collective-permute-start = (bf16[16,2048]{1,0:T(8,128)(2,1)}, bf16[16,2048]{1,0:T(8,128)(2,1)S(1)}, u32[]{:S(2)}, u32[]{:S(2)}) collective-permute-start(bf16[16,2048]{1,0:T(8,128)(2,1)} %get-tuple-element.18), channel_id=1, source_target_pairs={{0,1},{1,0},{2,3},{3,2},{4,5},{5,4},{6,7},{7,6},{8,9},{9,8},{10,11... | collective-permute-start | bytes 196616 | tf_op jit(solution)/shard_map/ppermute | solution.py:658
  17.5 5.0 %collective-permute-start.3 = (bf16[32,2048]{1,0:T(8,128)(2,1)S(1)}, bf16[32,2048]{1,0:T(8,128)(2,1)S(1)}, u32[]{:S(2)}, u32[]{:S(2)}) collective-permute-start(bf16[32,2048]{1,0:T(8,128)(2,1)S(1)} %constant_dynamic-update-slice_fusion.refs_1_), channel_id=1, source_target_pairs={{0,6},{1,7},{2,0},{3,1},{4,2},{5,3},{6,4},{7,5},{8,14},{9,15},{10,... | collective-permute-start | bytes 393224 | tf_op jit(solution)/shard_map/ppermute | solution.py:660
  20.0 6.9 %collective-permute-start.2 = (bf16[32,2048]{1,0:T(8,128)(2,1)S(1)}, bf16[32,2048]{1,0:T(8,128)(2,1)S(1)}, u32[]{:S(2)}, u32[]{:S(2)}) collective-permute-start(bf16[32,2048]{1,0:T(8,128)(2,1)S(1)} %constant_dynamic-update-slice_fusion.refs_1_), channel_id=1, source_target_pairs={{0,2},{1,3},{2,4},{3,5},{4,6},{5,7},{6,0},{7,1},{8,10},{9,11},{10,... | collective-permute-start | bytes 393224 | tf_op jit(solution)/shard_map/ppermute | solution.py:660
  20.0 7.5 %collective-permute-start.1 = (bf16[32,2048]{1,0:T(8,128)(2,1)S(1)}, bf16[32,2048]{1,0:T(8,128)(2,1)S(1)}, u32[]{:S(2)}, u32[]{:S(2)}) collective-permute-start(bf16[32,2048]{1,0:T(8,128)(2,1)S(1)} %constant_dynamic-update-slice_fusion.refs_1_), channel_id=1, source_target_pairs={{0,4},{1,5},{2,6},{3,7},{4,0},{5,1},{6,2},{7,3},{8,12},{9,13},{10,... | collective-permute-start | bytes 393224 | tf_op jit(solution)/shard_map/ppermute | solution.py:660
  31.6 8.3 %collective-permute-start.6 = (bf16[2,64,512]{2,1,0:T(8,128)(2,1)S(1)}, bf16[2,64,512]{2,1,0:T(8,128)(2,1)S(1)}, u32[]{:S(2)}, u32[]{:S(2)}) collective-permute-start(bf16[2,64,512]{2,1,0:T(8,128)(2,1)S(1)} %get-tuple-element.32), channel_id=1, source_target_pairs={{0,6},{1,7},{2,0},{3,1},{4,2},{5,3},{6,4},{7,5},{8,14},{9,15},{10,... | collective-permute-start | bytes 393224 | tf_op jit(solution)/shard_map/ppermute | solution.py:668
  34.1 6.4 %collective-permute-start.5 = (bf16[2,64,512]{2,1,0:T(8,128)(2,1)S(1)}, bf16[2,64,512]{2,1,0:T(8,128)(2,1)S(1)}, u32[]{:S(2)}, u32[]{:S(2)}) collective-permute-start(bf16[2,64,512]{2,1,0:T(8,128)(2,1)S(1)} %get-tuple-element.33), channel_id=1, source_target_pairs={{0,2},{1,3},{2,4},{3,5},{4,6},{5,7},{6,0},{7,1},{8,10},{9,11},{10,... | collective-permute-start | bytes 393224 | tf_op jit(solution)/shard_map/ppermute | solution.py:668
  34.1 6.4 %collective-permute-start.4 = (bf16[2,64,512]{2,1,0:T(8,128)(2,1)S(1)}, bf16[2,64,512]{2,1,0:T(8,128)(2,1)S(1)}, u32[]{:S(2)}, u32[]{:S(2)}) collective-permute-start(bf16[2,64,512]{2,1,0:T(8,128)(2,1)S(1)} %get-tuple-element.34), channel_id=1, source_target_pairs={{0,4},{1,5},{2,6},{3,7},{4,0},{5,1},{6,2},{7,3},{8,12},{9,13},{10,... | collective-permute-start | bytes 393224 | tf_op jit(solution)/shard_map/ppermute | solution.py:668
  40.5 5.3 %collective-permute-start.7 = (bf16[4,64,512]{2,1,0:T(8,128)(2,1)S(1)}, bf16[4,64,512]{2,1,0:T(8,128)(2,1)S(1)}, u32[]{:S(2)}, u32[]{:S(2)}) collective-permute-start(bf16[4,64,512]{2,1,0:T(8,128)(2,1)S(1)} %pack.1), channel_id=1, source_target_pairs={{0,1},{1,0},{2,3},{3,2},{4,5},{5,4},{6,7},{7,6},{8,9},{9,8},{10,11... | collective-permute-start | bytes 786440 | tf_op jit(solution)/shard_map/ppermute | solution.py:670

commit v9 on v8

--- a/solution.py
+++ b/solution.py
@@ -15,7 +15,7 @@
 
 PH = 16
 LANES = 128
-STEPS = (0, 2, 1, 3)
+STEPS = (0, 2, 3, 1)
 FINE = 32
 CORES = 2
 GROUP = 4

time: 59.2 us -> 58.5 us (0.988)
  transfers between devices with their start and end apart: 9 -> 9, of which waited for: 6 -> 5; matrix products, arithmetic and copies ran while one was open for 1% -> 1% of each run, Pallas kernels for 14% -> 14%
where the time goes in v9:
time: 58.5 us; the launch traced here: 58.3 us
  starting transfers between devices  25.4 us (43%)
  Pallas kernels  23.8 us (41%)
  waiting for transfers between devices  7.36 us (13%)
  local copies, waits for them, and re-layouts  0.88 us (2%)
  between operations  0.86 us (1%)
    pallas_call x1, Pallas kernels, correlate(): pl.pallas_call(lambda *refs: correlate_kernel(segs, *refs), out_shape=jax...  12.9 us
    all_to_all x1, starting transfers between devices, on_device(): passing = lax.all_to_all(slots, 'sta', 0, 0, tiled=True)  12 us
    ppermute x3, waiting for transfers between devices, on_device(): pairs = [pair] + [lax.ppermute(pair, 'seg', along_x[k]) for k in STEPS[1:]]  5.53 us
    ppermute x3, starting transfers between devices, on_device(): near.append(lax.ppermute(block, 'seg', along_x[k]))  4.32 us
    ppermute x3, starting transfers between devices, on_device(): pairs = [pair] + [lax.ppermute(pair, 'seg', along_x[k]) for k in STEPS[1:]]  4.2 us
    pallas_call x1, Pallas kernels, shift(): pl.pallas_call(lambda *refs: shift_kernel(stations, *refs), out_shape=(pl...  3.94 us
    ppermute x1, starting transfers between devices, on_device(): far = lax.ppermute(pack(me.reshape(1), near), 'seg', across)  3.82 us
    pallas_call x1, Pallas kernels, own_part(): pl.pallas_call(lambda *refs: own_kernel(segs, *refs), out_shape=(jax.Shap...  3.15 us
  transfers between devices with their start and end apart: 9, of which 5 were waited for; matrix products, arithmetic and copies ran while one was open for 1% of the time, Pallas kernels for 14%

profile of v9, /device:TPU:1, one launch (start us, length us, event | category | flops | bytes accessed | tf_op | source)
XLA Modules:
  0.0 58.3 jit_solution(16608295545318990239)
XLA Ops:
  0.6 2.6 %prepare.1 = (bf16[16,2048]{1,0:T(8,128)(2,1)}, bf16[512,512]{1,0:T(8,128)(2,1)}) custom-call(bf16[16,2048]{1,0:T(8,128)(2,1)} %refs_0_.1, s32[4,8]{1,0:T(4,128)} %bitcast.9), custom_call_target="tpu_custom_call" | custom-call | flops 104857600 | bytes 2097152 | tf_op jit(solution)/shard_map/prepare/pallas_call | solution.py:157
  3.3 12.0 %all-to-all-start = ((bf16[32,16,512]{2,1,0:T(8,128)(2,1)}), bf16[32,16,512]{2,1,0:T(8,128)(2,1)S(1)}, u32[]{:S(2)}, u32[]{:S(2)}) async-start(bf16[32,16,512]{2,1,0:T(8,128)(2,1)} %bitcast.8), calls=%async_computation | async-start | bytes 1048576 | tf_op jit(solution)/shard_map/all_to_all | solution.py:656
  15.3 1.0 %collective-permute-start = (bf16[16,2048]{1,0:T(8,128)(2,1)}, bf16[16,2048]{1,0:T(8,128)(2,1)S(1)}, u32[]{:S(2)}, u32[]{:S(2)}) collective-permute-start(bf16[16,2048]{1,0:T(8,128)(2,1)} %get-tuple-element.18), channel_id=1, source_target_pairs={{0,1},{1,0},{2,3},{3,2},{4,5},{5,4},{6,7},{7,6},{8,9},{9,8},{10,11... | collective-permute-start | bytes 196616 | tf_op jit(solution)/shard_map/ppermute | solution.py:658
  16.4 0.8 %constant_dynamic-update-slice_fusion.1 = bf16[32,2048]{1,0:T(8,128)(2,1)S(1)} fusion(bf16[16,2048]{1,0:T(8,128)(2,1)} %get-tuple-element.18), kind=kLoop, calls=%fused_computation.1 | loop fusion | bytes 131072
  17.2 0.3 collective-permute-done
  17.5 1.2 %collective-permute-start.3 = (bf16[32,2048]{1,0:T(8,128)(2,1)S(1)}, bf16[32,2048]{1,0:T(8,128)(2,1)S(1)}, u32[]{:S(2)}, u32[]{:S(2)}) collective-permute-start(bf16[32,2048]{1,0:T(8,128)(2,1)S(1)} %constant_dynamic-update-slice_fusion.refs_1_), channel_id=1, source_target_pairs={{0,2},{1,3},{2,4},{3,5},{4,6},{5,7},{6,0},{7,1},{8,10},{9,11},{10,... | collective-permute-start | bytes 393224 | tf_op jit(solution)/shard_map/ppermute | solution.py:660
  18.7 1.5 %collective-permute-start.2 = (bf16[32,2048]{1,0:T(8,128)(2,1)S(1)}, bf16[32,2048]{1,0:T(8,128)(2,1)S(1)}, u32[]{:S(2)}, u32[]{:S(2)}) collective-permute-start(bf16[32,2048]{1,0:T(8,128)(2,1)S(1)} %constant_dynamic-update-slice_fusion.refs_1_), channel_id=1, source_target_pairs={{0,6},{1,7},{2,0},{3,1},{4,2},{5,3},{6,4},{7,5},{8,14},{9,15},{10,... | collective-permute-start | bytes 393224 | tf_op jit(solution)/shard_map/ppermute | solution.py:660
  20.2 1.5 %collective-permute-start.1 = (bf16[32,2048]{1,0:T(8,128)(2,1)S(1)}, bf16[32,2048]{1,0:T(8,128)(2,1)S(1)}, u32[]{:S(2)}, u32[]{:S(2)}) collective-permute-start(bf16[32,2048]{1,0:T(8,128)(2,1)S(1)} %constant_dynamic-update-slice_fusion.refs_1_), channel_id=1, source_target_pairs={{0,4},{1,5},{2,6},{3,7},{4,0},{5,1},{6,2},{7,3},{8,12},{9,13},{10,... | collective-permute-start | bytes 393224 | tf_op jit(solution)/shard_map/ppermute | solution.py:660
  21.7 1.7 %collective-permute-done.3.refs_4_ = bf16[32,2048]{1,0:T(8,128)(2,1)S(1)} collective-permute-done((bf16[32,2048]{1,0:T(8,128)(2,1)S(1)}, bf16[32,2048]{1,0:T(8,128)(2,1)S(1)}, u32[]{:S(2)}, u32[]{:S(2)}) %collective-permute-start.3) | collective-permute-done | bytes 131104 | tf_op jit(solution)/shard_map/ppermute | solution.py:660
  23.4 0.0 collective-permute-done.2.refs_3_
  23.4 3.8 %collective-permute-done.1.refs_2_ = bf16[32,2048]{1,0:T(8,128)(2,1)S(1)} collective-permute-done((bf16[32,2048]{1,0:T(8,128)(2,1)S(1)}, bf16[32,2048]{1,0:T(8,128)(2,1)S(1)}, u32[]{:S(2)}, u32[]{:S(2)}) %collective-permute-start.1) | collective-permute-done | bytes 131104 | tf_op jit(solution)/shard_map/ppermute | solution.py:660
  27.2 3.2 %own.1 = (bf16[16,2048]{1,0:T(8,128)(2,1)S(1)}, f32[4,512,128]{2,1,0:T(8,128)S(1)}) custom-call(s32[1]{0:T(128)} %bitcast.3.refs_0_.me_ref, bf16[32,2048]{1,0:T(8,128)(2,1)S(1)} %constant_dynamic-update-slice_fusion.refs_1_, bf16[32,2048]{1,0:T(8,128)(2,1)S(1)} %collective-permute-done.1.refs_2_, bf16[32,2048]{1,0:T(8,128)(2,1)S(1)} %collective-permute-done.2.refs_3_, ...), custom_call_target="tpu_custom_call" | custom-call | flops 2097152000 | bytes 4194304 | tf_op jit(solution)/shard_map/own/pallas_call | solution.py:420
  30.4 1.2 %all-to-all-done = bf16[32,16,512]{2,1,0:T(8,128)(2,1)S(1)} async-done(((bf16[32,16,512]{2,1,0:T(8,128)(2,1)}), bf16[32,16,512]{2,1,0:T(8,128)(2,1)S(1)}, u32[]{:S(2)}, u32[]{:S(2)}) %all-to-all-start) | async-done | bytes 524320 | tf_op jit(solution)/shard_map/all_to_all | solution.py:656
  31.6 1.3 %collective-permute-start.6 = (bf16[2,64,512]{2,1,0:T(8,128)(2,1)S(1)}, bf16[2,64,512]{2,1,0:T(8,128)(2,1)S(1)}, u32[]{:S(2)}, u32[]{:S(2)}) collective-permute-start(bf16[2,64,512]{2,1,0:T(8,128)(2,1)S(1)} %get-tuple-element.32), channel_id=1, source_target_pairs={{0,2},{1,3},{2,4},{3,5},{4,6},{5,7},{6,0},{7,1},{8,10},{9,11},{10,... | collective-permute-start | bytes 393224 | tf_op jit(solution)/shard_map/ppermute | solution.py:668
  32.9 1.4 %collective-permute-start.5 = (bf16[2,64,512]{2,1,0:T(8,128)(2,1)S(1)}, bf16[2,64,512]{2,1,0:T(8,128)(2,1)S(1)}, u32[]{:S(2)}, u32[]{:S(2)}) collective-permute-start(bf16[2,64,512]{2,1,0:T(8,128)(2,1)S(1)} %get-tuple-element.33), channel_id=1, source_target_pairs={{0,6},{1,7},{2,0},{3,1},{4,2},{5,3},{6,4},{7,5},{8,14},{9,15},{10,... | collective-permute-start | bytes 393224 | tf_op jit(solution)/shard_map/ppermute | solution.py:668
  34.4 1.6 %collective-permute-start.4 = (bf16[2,64,512]{2,1,0:T(8,128)(2,1)S(1)}, bf16[2,64,512]{2,1,0:T(8,128)(2,1)S(1)}, u32[]{:S(2)}, u32[]{:S(2)}) collective-permute-start(bf16[2,64,512]{2,1,0:T(8,128)(2,1)S(1)} %get-tuple-element.34), channel_id=1, source_target_pairs={{0,4},{1,5},{2,6},{3,7},{4,0},{5,1},{6,2},{7,3},{8,12},{9,13},{10,... | collective-permute-start | bytes 393224 | tf_op jit(solution)/shard_map/ppermute | solution.py:668
  35.9 3.9 %shift.1 = (bf16[8192,512]{1,0:T(8,128)(2,1)}, bf16[512,512]{1,0:T(8,128)(2,1)}) custom-call(f32[4,512,128]{2,1,0:T(8,128)S(1)} %get-tuple-element.21.refs_0_), custom_call_target="tpu_custom_call" | custom-call | flops 1 | bytes 9437184 | tf_op jit(solution)/shard_map/shift/pallas_call | solution.py:489
  39.9 0.0 collective-permute-done.6.refs_3_.refs_4_
  39.9 0.0 collective-permute-done.5.refs_2_.refs_3_
  39.9 0.3 collective-permute-done.4.refs_1_.refs_2_
  40.3 3.8 %collective-permute-start.7 = (bf16[4,64,512]{2,1,0:T(8,128)(2,1)S(1)}, bf16[4,64,512]{2,1,0:T(8,128)(2,1)S(1)}, u32[]{:S(2)}, u32[]{:S(2)}) collective-permute-start(bf16[4,64,512]{2,1,0:T(8,128)(2,1)S(1)} %pack.1), channel_id=1, source_target_pairs={{0,1},{1,0},{2,3},{3,2},{4,5},{5,4},{6,7},{7,6},{8,9},{9,8},{10,11... | collective-permute-start | bytes 786440 | tf_op jit(solution)/shard_map/ppermute | solution.py:670
  44.1 1.1 %order.1 = bf16[16,2048]{1,0:T(8,128)(2,1)} custom-call(bf16[16,2048]{1,0:T(8,128)(2,1)S(1)} %get-tuple-element.25.phased_ref), custom_call_target="tpu_custom_call" | custom-call | flops 1048576000 | bytes 1048576 | tf_op jit(solution)/shard_map/order/pallas_call | solution.py:383
  45.2 0.0 collective-permute-done.7.refs_5_
  45.2 12.9 %correlate.1 = bf16[256,512]{1,0:T(8,128)(2,1)} custom-call(s32[1]{0:T(128)} %bitcast.3.refs_0_.me_ref, bf16[8,64,512]{2,1,0:T(8,128)(2,1)S(1)} %bitcast.7, bf16[2,64,512]{2,1,0:T(8,128)(2,1)S(1)} %collective-permute-done.4.refs_1_.refs_2_, bf16[2,64,512]{2,1,0:T(8,128)(2,1)S(1)} %collective-permute-done.5.refs_2_.refs_3_, ...), custom_call_target="tpu_custom_call" | custom-call | flops 6291456000 | bytes 20971520 | tf_op jit(solution)/shard_map/correlate/pallas_call | solution.py:611
  (3 shorter events, 0.1 us)
Async XLA Ops:
  3.3 28.3 %all-to-all-start = ((bf16[32,16,512]{2,1,0:T(8,128)(2,1)}), bf16[32,16,512]{2,1,0:T(8,128)(2,1)S(1)}, u32[]{:S(2)}, u32[]{:S(2)}) async-start(bf16[32,16,512]{2,1,0:T(8,128)(2,1)} %bitcast.8), calls=%async_computation | async-start | bytes 1048576 | tf_op jit(solution)/shard_map/all_to_all | solution.py:656
  15.3 2.2 %collective-permute-start = (bf16[16,2048]{1,0:T(8,128)(2,1)}, bf16[16,2048]{1,0:T(8,128)(2,1)S(1)}, u32[]{:S(2)}, u32[]{:S(2)}) collective-permute-start(bf16[16,2048]{1,0:T(8,128)(2,1)} %get-tuple-element.18), channel_id=1, source_target_pairs={{0,1},{1,0},{2,3},{3,2},{4,5},{5,4},{6,7},{7,6},{8,9},{9,8},{10,11... | collective-permute-start | bytes 196616 | tf_op jit(solution)/shard_map/ppermute | solution.py:658
  17.5 5.9 %collective-permute-start.3 = (bf16[32,2048]{1,0:T(8,128)(2,1)S(1)}, bf16[32,2048]{1,0:T(8,128)(2,1)S(1)}, u32[]{:S(2)}, u32[]{:S(2)}) collective-permute-start(bf16[32,2048]{1,0:T(8,128)(2,1)S(1)} %constant_dynamic-update-slice_fusion.refs_1_), channel_id=1, source_target_pairs={{0,2},{1,3},{2,4},{3,5},{4,6},{5,7},{6,0},{7,1},{8,10},{9,11},{10,... | collective-permute-start | bytes 393224 | tf_op jit(solution)/shard_map/ppermute | solution.py:660
  18.7 4.7 %collective-permute-start.2 = (bf16[32,2048]{1,0:T(8,128)(2,1)S(1)}, bf16[32,2048]{1,0:T(8,128)(2,1)S(1)}, u32[]{:S(2)}, u32[]{:S(2)}) collective-permute-start(bf16[32,2048]{1,0:T(8,128)(2,1)S(1)} %constant_dynamic-update-slice_fusion.refs_1_), channel_id=1, source_target_pairs={{0,6},{1,7},{2,0},{3,1},{4,2},{5,3},{6,4},{7,5},{8,14},{9,15},{10,... | collective-permute-start | bytes 393224 | tf_op jit(solution)/shard_map/ppermute | solution.py:660
  20.2 7.1 %collective-permute-start.1 = (bf16[32,2048]{1,0:T(8,128)(2,1)S(1)}, bf16[32,2048]{1,0:T(8,128)(2,1)S(1)}, u32[]{:S(2)}, u32[]{:S(2)}) collective-permute-start(bf16[32,2048]{1,0:T(8,128)(2,1)S(1)} %constant_dynamic-update-slice_fusion.refs_1_), channel_id=1, source_target_pairs={{0,4},{1,5},{2,6},{3,7},{4,0},{5,1},{6,2},{7,3},{8,12},{9,13},{10,... | collective-permute-start | bytes 393224 | tf_op jit(solution)/shard_map/ppermute | solution.py:660
  31.6 8.3 %collective-permute-start.6 = (bf16[2,64,512]{2,1,0:T(8,128)(2,1)S(1)}, bf16[2,64,512]{2,1,0:T(8,128)(2,1)S(1)}, u32[]{:S(2)}, u32[]{:S(2)}) collective-permute-start(bf16[2,64,512]{2,1,0:T(8,128)(2,1)S(1)} %get-tuple-element.32), channel_id=1, source_target_pairs={{0,2},{1,3},{2,4},{3,5},{4,6},{5,7},{6,0},{7,1},{8,10},{9,11},{10,... | collective-permute-start | bytes 393224 | tf_op jit(solution)/shard_map/ppermute | solution.py:668
  32.9 7.0 %collective-permute-start.5 = (bf16[2,64,512]{2,1,0:T(8,128)(2,1)S(1)}, bf16[2,64,512]{2,1,0:T(8,128)(2,1)S(1)}, u32[]{:S(2)}, u32[]{:S(2)}) collective-permute-start(bf16[2,64,512]{2,1,0:T(8,128)(2,1)S(1)} %get-tuple-element.33), channel_id=1, source_target_pairs={{0,6},{1,7},{2,0},{3,1},{4,2},{5,3},{6,4},{7,5},{8,14},{9,15},{10,... | collective-permute-start | bytes 393224 | tf_op jit(solution)/shard_map/ppermute | solution.py:668
  34.4 5.9 %collective-permute-start.4 = (bf16[2,64,512]{2,1,0:T(8,128)(2,1)S(1)}, bf16[2,64,512]{2,1,0:T(8,128)(2,1)S(1)}, u32[]{:S(2)}, u32[]{:S(2)}) collective-permute-start(bf16[2,64,512]{2,1,0:T(8,128)(2,1)S(1)} %get-tuple-element.34), channel_id=1, source_target_pairs={{0,4},{1,5},{2,6},{3,7},{4,0},{5,1},{6,2},{7,3},{8,12},{9,13},{10,... | collective-permute-start | bytes 393224 | tf_op jit(solution)/shard_map/ppermute | solution.py:668
  40.3 5.0 %collective-permute-start.7 = (bf16[4,64,512]{2,1,0:T(8,128)(2,1)S(1)}, bf16[4,64,512]{2,1,0:T(8,128)(2,1)S(1)}, u32[]{:S(2)}, u32[]{:S(2)}) collective-permute-start(bf16[4,64,512]{2,1,0:T(8,128)(2,1)S(1)} %pack.1), channel_id=1, source_target_pairs={{0,1},{1,0},{2,3},{3,2},{4,5},{5,4},{6,7},{7,6},{8,9},{9,8},{10,11... | collective-permute-start | bytes 786440 | tf_op jit(solution)/shard_map/ppermute | solution.py:670

commit v10 on v9

--- a/solution.py
+++ b/solution.py
@@ -555,7 +555,8 @@
         phase_ref[p * received : (p + 1) * received, s * LANES : (s + 1) * LANES] = tile
 
     fold(trace_ref, scale, segs, put)
-    copies[0].wait()
+    for copy in copies:
+        copy.wait()
     edge = dot_t(phase_ref[...], extra_ref[...])
     width = stations * FINE
     lag = iota((received, width), 1) % FINE
@@ -570,8 +571,6 @@
     norm = 1.0 / math.sqrt(segs * PH * LANES)
 
     def multiply(a):
-        block = shifted_hbm.at[pl.ds(pl.multiple_of(a * LAGS, LAGS), LAGS), :]
-        pltpu.make_async_copy(block, shifted_ref.at[a], sems.at[a]).wait()
         return dot_t(phase_ref[...], shifted_ref[a])
 
     def combine(a, product_ref):

time: 58.5 us -> 57.2 us (0.978)
  Pallas kernels: 23.8 us -> 22.5 us
    pallas_call x1, Pallas kernels: 12.9 us -> 11.6 us  [correlate(): pl.pallas_call(lambda *refs: correlate_kernel(segs, *refs), out_shape=jax...]
where the time goes in v10:
time: 57.2 us; the launch traced here: 57 us
  starting transfers between devices  25.4 us (44%)
  Pallas kernels  22.5 us (39%)
  waiting for transfers between devices  7.36 us (13%)
  local copies, waits for them, and re-layouts  0.88 us (2%)
  between operations  0.86 us (2%)
    all_to_all x1, starting transfers between devices, on_device(): passing = lax.all_to_all(slots, 'sta', 0, 0, tiled=True)  12 us
    pallas_call x1, Pallas kernels, correlate(): pl.pallas_call(lambda *refs: correlate_kernel(segs, *refs), out_shape=jax...  11.6 us
    ppermute x3, waiting for transfers between devices, on_device(): pairs = [pair] + [lax.ppermute(pair, 'seg', along_x[k]) for k in STEPS[1:]]  5.53 us
    ppermute x3, starting transfers between devices, on_device(): near.append(lax.ppermute(block, 'seg', along_x[k]))  4.32 us
    ppermute x3, starting transfers between devices, on_device(): pairs = [pair] + [lax.ppermute(pair, 'seg', along_x[k]) for k in STEPS[1:]]  4.2 us
    pallas_call x1, Pallas kernels, shift(): pl.pallas_call(lambda *refs: shift_kernel(stations, *refs), out_shape=(pl...  3.94 us
    ppermute x1, starting transfers between devices, on_device(): far = lax.ppermute(pack(me.reshape(1), near), 'seg', across)  3.82 us
    pallas_call x1, Pallas kernels, own_part(): pl.pallas_call(lambda *refs: own_kernel(segs, *refs), out_shape=(jax.Shap...  3.15 us
  transfers between devices with their start and end apart: 9, of which 5 were waited for; matrix products, arithmetic and copies ran while one was open for 1% of the time, Pallas kernels for 14%

profile of v10, /device:TPU:1, one launch (start us, length us, event | category | flops | bytes accessed | tf_op | source)
XLA Modules:
  0.0 57.0 jit_solution(48538608562506249)
XLA Ops:
  0.6 2.6 %prepare.1 = (bf16[16,2048]{1,0:T(8,128)(2,1)}, bf16[512,512]{1,0:T(8,128)(2,1)}) custom-call(bf16[16,2048]{1,0:T(8,128)(2,1)} %refs_0_.1, s32[4,8]{1,0:T(4,128)} %bitcast.9), custom_call_target="tpu_custom_call" | custom-call | flops 104857600 | bytes 2097152 | tf_op jit(solution)/shard_map/prepare/pallas_call | solution.py:157
  3.3 12.0 %all-to-all-start = ((bf16[32,16,512]{2,1,0:T(8,128)(2,1)}), bf16[32,16,512]{2,1,0:T(8,128)(2,1)S(1)}, u32[]{:S(2)}, u32[]{:S(2)}) async-start(bf16[32,16,512]{2,1,0:T(8,128)(2,1)} %bitcast.8), calls=%async_computation | async-start | bytes 1048576 | tf_op jit(solution)/shard_map/all_to_all | solution.py:655
  15.3 1.0 %collective-permute-start = (bf16[16,2048]{1,0:T(8,128)(2,1)}, bf16[16,2048]{1,0:T(8,128)(2,1)S(1)}, u32[]{:S(2)}, u32[]{:S(2)}) collective-permute-start(bf16[16,2048]{1,0:T(8,128)(2,1)} %get-tuple-element.18), channel_id=1, source_target_pairs={{0,1},{1,0},{2,3},{3,2},{4,5},{5,4},{6,7},{7,6},{8,9},{9,8},{10,11... | collective-permute-start | bytes 196616 | tf_op jit(solution)/shard_map/ppermute | solution.py:657
  16.4 0.8 %constant_dynamic-update-slice_fusion.1 = bf16[32,2048]{1,0:T(8,128)(2,1)S(1)} fusion(bf16[16,2048]{1,0:T(8,128)(2,1)} %get-tuple-element.18), kind=kLoop, calls=%fused_computation.1 | loop fusion | bytes 131072
  17.2 0.3 collective-permute-done
  17.5 1.2 %collective-permute-start.3 = (bf16[32,2048]{1,0:T(8,128)(2,1)S(1)}, bf16[32,2048]{1,0:T(8,128)(2,1)S(1)}, u32[]{:S(2)}, u32[]{:S(2)}) collective-permute-start(bf16[32,2048]{1,0:T(8,128)(2,1)S(1)} %constant_dynamic-update-slice_fusion.refs_1_), channel_id=1, source_target_pairs={{0,2},{1,3},{2,4},{3,5},{4,6},{5,7},{6,0},{7,1},{8,10},{9,11},{10,... | collective-permute-start | bytes 393224 | tf_op jit(solution)/shard_map/ppermute | solution.py:659
  18.7 1.5 %collective-permute-start.2 = (bf16[32,2048]{1,0:T(8,128)(2,1)S(1)}, bf16[32,2048]{1,0:T(8,128)(2,1)S(1)}, u32[]{:S(2)}, u32[]{:S(2)}) collective-permute-start(bf16[32,2048]{1,0:T(8,128)(2,1)S(1)} %constant_dynamic-update-slice_fusion.refs_1_), channel_id=1, source_target_pairs={{0,6},{1,7},{2,0},{3,1},{4,2},{5,3},{6,4},{7,5},{8,14},{9,15},{10,... | collective-permute-start | bytes 393224 | tf_op jit(solution)/shard_map/ppermute | solution.py:659
  20.2 1.5 %collective-permute-start.1 = (bf16[32,2048]{1,0:T(8,128)(2,1)S(1)}, bf16[32,2048]{1,0:T(8,128)(2,1)S(1)}, u32[]{:S(2)}, u32[]{:S(2)}) collective-permute-start(bf16[32,2048]{1,0:T(8,128)(2,1)S(1)} %constant_dynamic-update-slice_fusion.refs_1_), channel_id=1, source_target_pairs={{0,4},{1,5},{2,6},{3,7},{4,0},{5,1},{6,2},{7,3},{8,12},{9,13},{10,... | collective-permute-start | bytes 393224 | tf_op jit(solution)/shard_map/ppermute | solution.py:659
  21.7 1.7 %collective-permute-done.3.refs_4_ = bf16[32,2048]{1,0:T(8,128)(2,1)S(1)} collective-permute-done((bf16[32,2048]{1,0:T(8,128)(2,1)S(1)}, bf16[32,2048]{1,0:T(8,128)(2,1)S(1)}, u32[]{:S(2)}, u32[]{:S(2)}) %collective-permute-start.3) | collective-permute-done | bytes 131104 | tf_op jit(solution)/shard_map/ppermute | solution.py:659
  23.4 0.0 collective-permute-done.2.refs_3_
  23.4 3.8 %collective-permute-done.1.refs_2_ = bf16[32,2048]{1,0:T(8,128)(2,1)S(1)} collective-permute-done((bf16[32,2048]{1,0:T(8,128)(2,1)S(1)}, bf16[32,2048]{1,0:T(8,128)(2,1)S(1)}, u32[]{:S(2)}, u32[]{:S(2)}) %collective-permute-start.1) | collective-permute-done | bytes 131104 | tf_op jit(solution)/shard_map/ppermute | solution.py:659
  27.2 3.2 %own.1 = (bf16[16,2048]{1,0:T(8,128)(2,1)S(1)}, f32[4,512,128]{2,1,0:T(8,128)S(1)}) custom-call(s32[1]{0:T(128)} %bitcast.3.refs_0_.me_ref, bf16[32,2048]{1,0:T(8,128)(2,1)S(1)} %constant_dynamic-update-slice_fusion.refs_1_, bf16[32,2048]{1,0:T(8,128)(2,1)S(1)} %collective-permute-done.1.refs_2_, bf16[32,2048]{1,0:T(8,128)(2,1)S(1)} %collective-permute-done.2.refs_3_, ...), custom_call_target="tpu_custom_call" | custom-call | flops 2097152000 | bytes 4194304 | tf_op jit(solution)/shard_map/own/pallas_call | solution.py:420
  30.4 1.2 %all-to-all-done = bf16[32,16,512]{2,1,0:T(8,128)(2,1)S(1)} async-done(((bf16[32,16,512]{2,1,0:T(8,128)(2,1)}), bf16[32,16,512]{2,1,0:T(8,128)(2,1)S(1)}, u32[]{:S(2)}, u32[]{:S(2)}) %all-to-all-start) | async-done | bytes 524320 | tf_op jit(solution)/shard_map/all_to_all | solution.py:655
  31.6 1.3 %collective-permute-start.6 = (bf16[2,64,512]{2,1,0:T(8,128)(2,1)S(1)}, bf16[2,64,512]{2,1,0:T(8,128)(2,1)S(1)}, u32[]{:S(2)}, u32[]{:S(2)}) collective-permute-start(bf16[2,64,512]{2,1,0:T(8,128)(2,1)S(1)} %get-tuple-element.32), channel_id=1, source_target_pairs={{0,2},{1,3},{2,4},{3,5},{4,6},{5,7},{6,0},{7,1},{8,10},{9,11},{10,... | collective-permute-start | bytes 393224 | tf_op jit(solution)/shard_map/ppermute | solution.py:667
  32.9 1.4 %collective-permute-start.5 = (bf16[2,64,512]{2,1,0:T(8,128)(2,1)S(1)}, bf16[2,64,512]{2,1,0:T(8,128)(2,1)S(1)}, u32[]{:S(2)}, u32[]{:S(2)}) collective-permute-start(bf16[2,64,512]{2,1,0:T(8,128)(2,1)S(1)} %get-tuple-element.33), channel_id=1, source_target_pairs={{0,6},{1,7},{2,0},{3,1},{4,2},{5,3},{6,4},{7,5},{8,14},{9,15},{10,... | collective-permute-start | bytes 393224 | tf_op jit(solution)/shard_map/ppermute | solution.py:667
  34.4 1.6 %collective-permute-start.4 = (bf16[2,64,512]{2,1,0:T(8,128)(2,1)S(1)}, bf16[2,64,512]{2,1,0:T(8,128)(2,1)S(1)}, u32[]{:S(2)}, u32[]{:S(2)}) collective-permute-start(bf16[2,64,512]{2,1,0:T(8,128)(2,1)S(1)} %get-tuple-element.34), channel_id=1, source_target_pairs={{0,4},{1,5},{2,6},{3,7},{4,0},{5,1},{6,2},{7,3},{8,12},{9,13},{10,... | collective-permute-start | bytes 393224 | tf_op jit(solution)/shard_map/ppermute | solution.py:667
  35.9 3.9 %shift.1 = (bf16[8192,512]{1,0:T(8,128)(2,1)}, bf16[512,512]{1,0:T(8,128)(2,1)}) custom-call(f32[4,512,128]{2,1,0:T(8,128)S(1)} %get-tuple-element.21.refs_0_), custom_call_target="tpu_custom_call" | custom-call | flops 1 | bytes 9437184 | tf_op jit(solution)/shard_map/shift/pallas_call | solution.py:489
  39.9 0.0 collective-permute-done.6.refs_3_.refs_4_
  39.9 0.0 collective-permute-done.5.refs_2_.refs_3_
  39.9 0.3 collective-permute-done.4.refs_1_.refs_2_
  40.3 3.8 %collective-permute-start.7 = (bf16[4,64,512]{2,1,0:T(8,128)(2,1)S(1)}, bf16[4,64,512]{2,1,0:T(8,128)(2,1)S(1)}, u32[]{:S(2)}, u32[]{:S(2)}) collective-permute-start(bf16[4,64,512]{2,1,0:T(8,128)(2,1)S(1)} %pack.1), channel_id=1, source_target_pairs={{0,1},{1,0},{2,3},{3,2},{4,5},{5,4},{6,7},{7,6},{8,9},{9,8},{10,11... | collective-permute-start | bytes 786440 | tf_op jit(solution)/shard_map/ppermute | solution.py:669
  44.1 1.1 %order.1 = bf16[16,2048]{1,0:T(8,128)(2,1)} custom-call(bf16[16,2048]{1,0:T(8,128)(2,1)S(1)} %get-tuple-element.25.phased_ref), custom_call_target="tpu_custom_call" | custom-call | flops 1048576000 | bytes 1048576 | tf_op jit(solution)/shard_map/order/pallas_call | solution.py:383
  45.2 0.0 collective-permute-done.7.refs_5_
  45.2 11.6 %correlate.1 = bf16[256,512]{1,0:T(8,128)(2,1)} custom-call(s32[1]{0:T(128)} %bitcast.3.refs_0_.me_ref, bf16[8,64,512]{2,1,0:T(8,128)(2,1)S(1)} %bitcast.7, bf16[2,64,512]{2,1,0:T(8,128)(2,1)S(1)} %collective-permute-done.4.refs_1_.refs_2_, bf16[2,64,512]{2,1,0:T(8,128)(2,1)S(1)} %collective-permute-done.5.refs_2_.refs_3_, ...), custom_call_target="tpu_custom_call" | custom-call | flops 6291456000 | bytes 20971520 | tf_op jit(solution)/shard_map/correlate/pallas_call | solution.py:610
  (3 shorter events, 0.0 us)
Async XLA Ops:
  3.3 28.3 %all-to-all-start = ((bf16[32,16,512]{2,1,0:T(8,128)(2,1)}), bf16[32,16,512]{2,1,0:T(8,128)(2,1)S(1)}, u32[]{:S(2)}, u32[]{:S(2)}) async-start(bf16[32,16,512]{2,1,0:T(8,128)(2,1)} %bitcast.8), calls=%async_computation | async-start | bytes 1048576 | tf_op jit(solution)/shard_map/all_to_all | solution.py:655
  15.3 2.2 %collective-permute-start = (bf16[16,2048]{1,0:T(8,128)(2,1)}, bf16[16,2048]{1,0:T(8,128)(2,1)S(1)}, u32[]{:S(2)}, u32[]{:S(2)}) collective-permute-start(bf16[16,2048]{1,0:T(8,128)(2,1)} %get-tuple-element.18), channel_id=1, source_target_pairs={{0,1},{1,0},{2,3},{3,2},{4,5},{5,4},{6,7},{7,6},{8,9},{9,8},{10,11... | collective-permute-start | bytes 196616 | tf_op jit(solution)/shard_map/ppermute | solution.py:657
  17.5 5.9 %collective-permute-start.3 = (bf16[32,2048]{1,0:T(8,128)(2,1)S(1)}, bf16[32,2048]{1,0:T(8,128)(2,1)S(1)}, u32[]{:S(2)}, u32[]{:S(2)}) collective-permute-start(bf16[32,2048]{1,0:T(8,128)(2,1)S(1)} %constant_dynamic-update-slice_fusion.refs_1_), channel_id=1, source_target_pairs={{0,2},{1,3},{2,4},{3,5},{4,6},{5,7},{6,0},{7,1},{8,10},{9,11},{10,... | collective-permute-start | bytes 393224 | tf_op jit(solution)/shard_map/ppermute | solution.py:659
  18.7 4.7 %collective-permute-start.2 = (bf16[32,2048]{1,0:T(8,128)(2,1)S(1)}, bf16[32,2048]{1,0:T(8,128)(2,1)S(1)}, u32[]{:S(2)}, u32[]{:S(2)}) collective-permute-start(bf16[32,2048]{1,0:T(8,128)(2,1)S(1)} %constant_dynamic-update-slice_fusion.refs_1_), channel_id=1, source_target_pairs={{0,6},{1,7},{2,0},{3,1},{4,2},{5,3},{6,4},{7,5},{8,14},{9,15},{10,... | collective-permute-start | bytes 393224 | tf_op jit(solution)/shard_map/ppermute | solution.py:659
  20.2 7.1 %collective-permute-start.1 = (bf16[32,2048]{1,0:T(8,128)(2,1)S(1)}, bf16[32,2048]{1,0:T(8,128)(2,1)S(1)}, u32[]{:S(2)}, u32[]{:S(2)}) collective-permute-start(bf16[32,2048]{1,0:T(8,128)(2,1)S(1)} %constant_dynamic-update-slice_fusion.refs_1_), channel_id=1, source_target_pairs={{0,4},{1,5},{2,6},{3,7},{4,0},{5,1},{6,2},{7,3},{8,12},{9,13},{10,... | collective-permute-start | bytes 393224 | tf_op jit(solution)/shard_map/ppermute | solution.py:659
  31.6 8.3 %collective-permute-start.6 = (bf16[2,64,512]{2,1,0:T(8,128)(2,1)S(1)}, bf16[2,64,512]{2,1,0:T(8,128)(2,1)S(1)}, u32[]{:S(2)}, u32[]{:S(2)}) collective-permute-start(bf16[2,64,512]{2,1,0:T(8,128)(2,1)S(1)} %get-tuple-element.32), channel_id=1, source_target_pairs={{0,2},{1,3},{2,4},{3,5},{4,6},{5,7},{6,0},{7,1},{8,10},{9,11},{10,... | collective-permute-start | bytes 393224 | tf_op jit(solution)/shard_map/ppermute | solution.py:667
  32.9 7.0 %collective-permute-start.5 = (bf16[2,64,512]{2,1,0:T(8,128)(2,1)S(1)}, bf16[2,64,512]{2,1,0:T(8,128)(2,1)S(1)}, u32[]{:S(2)}, u32[]{:S(2)}) collective-permute-start(bf16[2,64,512]{2,1,0:T(8,128)(2,1)S(1)} %get-tuple-element.33), channel_id=1, source_target_pairs={{0,6},{1,7},{2,0},{3,1},{4,2},{5,3},{6,4},{7,5},{8,14},{9,15},{10,... | collective-permute-start | bytes 393224 | tf_op jit(solution)/shard_map/ppermute | solution.py:667
  34.4 5.9 %collective-permute-start.4 = (bf16[2,64,512]{2,1,0:T(8,128)(2,1)S(1)}, bf16[2,64,512]{2,1,0:T(8,128)(2,1)S(1)}, u32[]{:S(2)}, u32[]{:S(2)}) collective-permute-start(bf16[2,64,512]{2,1,0:T(8,128)(2,1)S(1)} %get-tuple-element.34), channel_id=1, source_target_pairs={{0,4},{1,5},{2,6},{3,7},{4,0},{5,1},{6,2},{7,3},{8,12},{9,13},{10,... | collective-permute-start | bytes 393224 | tf_op jit(solution)/shard_map/ppermute | solution.py:667
  40.3 5.0 %collective-permute-start.7 = (bf16[4,64,512]{2,1,0:T(8,128)(2,1)S(1)}, bf16[4,64,512]{2,1,0:T(8,128)(2,1)S(1)}, u32[]{:S(2)}, u32[]{:S(2)}) collective-permute-start(bf16[4,64,512]{2,1,0:T(8,128)(2,1)S(1)} %pack.1), channel_id=1, source_target_pairs={{0,1},{1,0},{2,3},{3,2},{4,5},{5,4},{6,7},{7,6},{8,9},{9,8},{10,11... | collective-permute-start | bytes 786440 | tf_op jit(solution)/shard_map/ppermute | solution.py:669

commit v11 on v10

--- a/solution.py
+++ b/solution.py
@@ -594,7 +594,7 @@
         combine(2 * i + 1, odd_ref)
         return 0
 
-    lax.fori_loop(0, stations // 2 - 1, body, 0)
+    lax.fori_loop(0, stations // 2 - 1, body, 0, unroll=7)
     odd_ref[...] = multiply(stations - 1)
     combine(stations - 2, even_ref)
     combine(stations - 1, odd_ref)

time: 57.2 us -> 55.8 us (0.976)
  Pallas kernels: 22.5 us -> 21 us
    pallas_call x1, Pallas kernels: 11.6 us -> 10.2 us  [correlate(): pl.pallas_call(lambda *refs: correlate_kernel(segs, *refs), out_shape=jax...]
  transfers between devices with their start and end apart: 9 -> 9, of which waited for: 5 -> 5; matrix products, arithmetic and copies ran while one was open for 1% -> 2% of each run, Pallas kernels for 14% -> 15%
where the time goes in v11:
time: 55.8 us; the launch traced here: 55.6 us
  starting transfers between devices  25.4 us (46%)
  Pallas kernels  21 us (38%)
  waiting for transfers between devices  7.36 us (13%)
  local copies, waits for them, and re-layouts  0.88 us (2%)
  between operations  0.86 us (2%)
    all_to_all x1, starting transfers between devices, on_device(): passing = lax.all_to_all(slots, 'sta', 0, 0, tiled=True)  12 us
    pallas_call x1, Pallas kernels, correlate(): pl.pallas_call(lambda *refs: correlate_kernel(segs, *refs), out_shape=jax...  10.2 us
    ppermute x3, waiting for transfers between devices, on_device(): pairs = [pair] + [lax.ppermute(pair, 'seg', along_x[k]) for k in STEPS[1:]]  5.53 us
    ppermute x3, starting transfers between devices, on_device(): near.append(lax.ppermute(block, 'seg', along_x[k]))  4.32 us
    ppermute x3, starting transfers between devices, on_device(): pairs = [pair] + [lax.ppermute(pair, 'seg', along_x[k]) for k in STEPS[1:]]  4.2 us
    pallas_call x1, Pallas kernels, shift(): pl.pallas_call(lambda *refs: shift_kernel(stations, *refs), out_shape=(pl...  3.94 us
    ppermute x1, starting transfers between devices, on_device(): far = lax.ppermute(pack(me.reshape(1), near), 'seg', across)  3.82 us
    pallas_call x1, Pallas kernels, own_part(): pl.pallas_call(lambda *refs: own_kernel(segs, *refs), out_shape=(jax.Shap...  3.15 us
  transfers between devices with their start and end apart: 9, of which 5 were waited for; matrix products, arithmetic and copies ran while one was open for 2% of the time, Pallas kernels for 15%

profile of v11, /device:TPU:1, one launch (start us, length us, event | category | flops | bytes accessed | tf_op | source)
XLA Modules:
  0.0 55.6 jit_solution(4266556095314405423)
XLA Ops:
  0.6 2.6 %prepare.1 = (bf16[16,2048]{1,0:T(8,128)(2,1)}, bf16[512,512]{1,0:T(8,128)(2,1)}) custom-call(bf16[16,2048]{1,0:T(8,128)(2,1)} %refs_0_.1, s32[4,8]{1,0:T(4,128)} %bitcast.9), custom_call_target="tpu_custom_call" | custom-call | flops 104857600 | bytes 2097152 | tf_op jit(solution)/shard_map/prepare/pallas_call | solution.py:157
  3.3 12.0 %all-to-all-start = ((bf16[32,16,512]{2,1,0:T(8,128)(2,1)}), bf16[32,16,512]{2,1,0:T(8,128)(2,1)S(1)}, u32[]{:S(2)}, u32[]{:S(2)}) async-start(bf16[32,16,512]{2,1,0:T(8,128)(2,1)} %bitcast.8), calls=%async_computation | async-start | bytes 1048576 | tf_op jit(solution)/shard_map/all_to_all | solution.py:655
  15.3 1.0 %collective-permute-start = (bf16[16,2048]{1,0:T(8,128)(2,1)}, bf16[16,2048]{1,0:T(8,128)(2,1)S(1)}, u32[]{:S(2)}, u32[]{:S(2)}) collective-permute-start(bf16[16,2048]{1,0:T(8,128)(2,1)} %get-tuple-element.18), channel_id=1, source_target_pairs={{0,1},{1,0},{2,3},{3,2},{4,5},{5,4},{6,7},{7,6},{8,9},{9,8},{10,11... | collective-permute-start | bytes 196616 | tf_op jit(solution)/shard_map/ppermute | solution.py:657
  16.4 0.8 %constant_dynamic-update-slice_fusion.1 = bf16[32,2048]{1,0:T(8,128)(2,1)S(1)} fusion(bf16[16,2048]{1,0:T(8,128)(2,1)} %get-tuple-element.18), kind=kLoop, calls=%fused_computation.1 | loop fusion | bytes 131072
  17.2 0.3 collective-permute-done
  17.5 1.2 %collective-permute-start.3 = (bf16[32,2048]{1,0:T(8,128)(2,1)S(1)}, bf16[32,2048]{1,0:T(8,128)(2,1)S(1)}, u32[]{:S(2)}, u32[]{:S(2)}) collective-permute-start(bf16[32,2048]{1,0:T(8,128)(2,1)S(1)} %constant_dynamic-update-slice_fusion.refs_1_), channel_id=1, source_target_pairs={{0,2},{1,3},{2,4},{3,5},{4,6},{5,7},{6,0},{7,1},{8,10},{9,11},{10,... | collective-permute-start | bytes 393224 | tf_op jit(solution)/shard_map/ppermute | solution.py:659
  18.7 1.5 %collective-permute-start.2 = (bf16[32,2048]{1,0:T(8,128)(2,1)S(1)}, bf16[32,2048]{1,0:T(8,128)(2,1)S(1)}, u32[]{:S(2)}, u32[]{:S(2)}) collective-permute-start(bf16[32,2048]{1,0:T(8,128)(2,1)S(1)} %constant_dynamic-update-slice_fusion.refs_1_), channel_id=1, source_target_pairs={{0,6},{1,7},{2,0},{3,1},{4,2},{5,3},{6,4},{7,5},{8,14},{9,15},{10,... | collective-permute-start | bytes 393224 | tf_op jit(solution)/shard_map/ppermute | solution.py:659
  20.2 1.5 %collective-permute-start.1 = (bf16[32,2048]{1,0:T(8,128)(2,1)S(1)}, bf16[32,2048]{1,0:T(8,128)(2,1)S(1)}, u32[]{:S(2)}, u32[]{:S(2)}) collective-permute-start(bf16[32,2048]{1,0:T(8,128)(2,1)S(1)} %constant_dynamic-update-slice_fusion.refs_1_), channel_id=1, source_target_pairs={{0,4},{1,5},{2,6},{3,7},{4,0},{5,1},{6,2},{7,3},{8,12},{9,13},{10,... | collective-permute-start | bytes 393224 | tf_op jit(solution)/shard_map/ppermute | solution.py:659
  21.7 1.7 %collective-permute-done.3.refs_4_ = bf16[32,2048]{1,0:T(8,128)(2,1)S(1)} collective-permute-done((bf16[32,2048]{1,0:T(8,128)(2,1)S(1)}, bf16[32,2048]{1,0:T(8,128)(2,1)S(1)}, u32[]{:S(2)}, u32[]{:S(2)}) %collective-permute-start.3) | collective-permute-done | bytes 131104 | tf_op jit(solution)/shard_map/ppermute | solution.py:659
  23.4 0.0 collective-permute-done.2.refs_3_
  23.4 3.8 %collective-permute-done.1.refs_2_ = bf16[32,2048]{1,0:T(8,128)(2,1)S(1)} collective-permute-done((bf16[32,2048]{1,0:T(8,128)(2,1)S(1)}, bf16[32,2048]{1,0:T(8,128)(2,1)S(1)}, u32[]{:S(2)}, u32[]{:S(2)}) %collective-permute-start.1) | collective-permute-done | bytes 131104 | tf_op jit(solution)/shard_map/ppermute | solution.py:659
  27.2 3.2 %own.1 = (bf16[16,2048]{1,0:T(8,128)(2,1)S(1)}, f32[4,512,128]{2,1,0:T(8,128)S(1)}) custom-call(s32[1]{0:T(128)} %bitcast.3.refs_0_.me_ref, bf16[32,2048]{1,0:T(8,128)(2,1)S(1)} %constant_dynamic-update-slice_fusion.refs_1_, bf16[32,2048]{1,0:T(8,128)(2,1)S(1)} %collective-permute-done.1.refs_2_, bf16[32,2048]{1,0:T(8,128)(2,1)S(1)} %collective-permute-done.2.refs_3_, ...), custom_call_target="tpu_custom_call" | custom-call | flops 2097152000 | bytes 4194304 | tf_op jit(solution)/shard_map/own/pallas_call | solution.py:420
  30.4 1.2 %all-to-all-done = bf16[32,16,512]{2,1,0:T(8,128)(2,1)S(1)} async-done(((bf16[32,16,512]{2,1,0:T(8,128)(2,1)}), bf16[32,16,512]{2,1,0:T(8,128)(2,1)S(1)}, u32[]{:S(2)}, u32[]{:S(2)}) %all-to-all-start) | async-done | bytes 524320 | tf_op jit(solution)/shard_map/all_to_all | solution.py:655
  31.6 1.3 %collective-permute-start.6 = (bf16[2,64,512]{2,1,0:T(8,128)(2,1)S(1)}, bf16[2,64,512]{2,1,0:T(8,128)(2,1)S(1)}, u32[]{:S(2)}, u32[]{:S(2)}) collective-permute-start(bf16[2,64,512]{2,1,0:T(8,128)(2,1)S(1)} %get-tuple-element.32), channel_id=1, source_target_pairs={{0,2},{1,3},{2,4},{3,5},{4,6},{5,7},{6,0},{7,1},{8,10},{9,11},{10,... | collective-permute-start | bytes 393224 | tf_op jit(solution)/shard_map/ppermute | solution.py:667
  32.9 1.4 %collective-permute-start.5 = (bf16[2,64,512]{2,1,0:T(8,128)(2,1)S(1)}, bf16[2,64,512]{2,1,0:T(8,128)(2,1)S(1)}, u32[]{:S(2)}, u32[]{:S(2)}) collective-permute-start(bf16[2,64,512]{2,1,0:T(8,128)(2,1)S(1)} %get-tuple-element.33), channel_id=1, source_target_pairs={{0,6},{1,7},{2,0},{3,1},{4,2},{5,3},{6,4},{7,5},{8,14},{9,15},{10,... | collective-permute-start | bytes 393224 | tf_op jit(solution)/shard_map/ppermute | solution.py:667
  34.4 1.6 %collective-permute-start.4 = (bf16[2,64,512]{2,1,0:T(8,128)(2,1)S(1)}, bf16[2,64,512]{2,1,0:T(8,128)(2,1)S(1)}, u32[]{:S(2)}, u32[]{:S(2)}) collective-permute-start(bf16[2,64,512]{2,1,0:T(8,128)(2,1)S(1)} %get-tuple-element.34), channel_id=1, source_target_pairs={{0,4},{1,5},{2,6},{3,7},{4,0},{5,1},{6,2},{7,3},{8,12},{9,13},{10,... | collective-permute-start | bytes 393224 | tf_op jit(solution)/shard_map/ppermute | solution.py:667
  35.9 3.9 %shift.1 = (bf16[8192,512]{1,0:T(8,128)(2,1)}, bf16[512,512]{1,0:T(8,128)(2,1)}) custom-call(f32[4,512,128]{2,1,0:T(8,128)S(1)} %get-tuple-element.21.refs_0_), custom_call_target="tpu_custom_call" | custom-call | flops 1 | bytes 9437184 | tf_op jit(solution)/shard_map/shift/pallas_call | solution.py:489
  39.9 0.0 collective-permute-done.6.refs_3_.refs_4_
  39.9 0.0 collective-permute-done.5.refs_2_.refs_3_
  39.9 0.3 collective-permute-done.4.refs_1_.refs_2_
  40.3 3.8 %collective-permute-start.7 = (bf16[4,64,512]{2,1,0:T(8,128)(2,1)S(1)}, bf16[4,64,512]{2,1,0:T(8,128)(2,1)S(1)}, u32[]{:S(2)}, u32[]{:S(2)}) collective-permute-start(bf16[4,64,512]{2,1,0:T(8,128)(2,1)S(1)} %pack.1), channel_id=1, source_target_pairs={{0,1},{1,0},{2,3},{3,2},{4,5},{5,4},{6,7},{7,6},{8,9},{9,8},{10,11... | collective-permute-start | bytes 786440 | tf_op jit(solution)/shard_map/ppermute | solution.py:669
  44.1 1.1 %order.1 = bf16[16,2048]{1,0:T(8,128)(2,1)} custom-call(bf16[16,2048]{1,0:T(8,128)(2,1)S(1)} %get-tuple-element.25.phased_ref), custom_call_target="tpu_custom_call" | custom-call | flops 1048576000 | bytes 1048576 | tf_op jit(solution)/shard_map/order/pallas_call | solution.py:383
  45.2 0.0 collective-permute-done.7.refs_5_
  45.2 10.2 %correlate.1 = bf16[256,512]{1,0:T(8,128)(2,1)} custom-call(s32[1]{0:T(128)} %bitcast.3.refs_0_.me_ref, bf16[8,64,512]{2,1,0:T(8,128)(2,1)S(1)} %bitcast.7, bf16[2,64,512]{2,1,0:T(8,128)(2,1)S(1)} %collective-permute-done.4.refs_1_.refs_2_, bf16[2,64,512]{2,1,0:T(8,128)(2,1)S(1)} %collective-permute-done.5.refs_2_.refs_3_, ...), custom_call_target="tpu_custom_call" | custom-call | flops 6291456000 | bytes 20971520 | tf_op jit(solution)/shard_map/correlate/pallas_call | solution.py:610
  (3 shorter events, 0.1 us)
Async XLA Ops:
  3.3 28.3 %all-to-all-start = ((bf16[32,16,512]{2,1,0:T(8,128)(2,1)}), bf16[32,16,512]{2,1,0:T(8,128)(2,1)S(1)}, u32[]{:S(2)}, u32[]{:S(2)}) async-start(bf16[32,16,512]{2,1,0:T(8,128)(2,1)} %bitcast.8), calls=%async_computation | async-start | bytes 1048576 | tf_op jit(solution)/shard_map/all_to_all | solution.py:655
  15.3 2.2 %collective-permute-start = (bf16[16,2048]{1,0:T(8,128)(2,1)}, bf16[16,2048]{1,0:T(8,128)(2,1)S(1)}, u32[]{:S(2)}, u32[]{:S(2)}) collective-permute-start(bf16[16,2048]{1,0:T(8,128)(2,1)} %get-tuple-element.18), channel_id=1, source_target_pairs={{0,1},{1,0},{2,3},{3,2},{4,5},{5,4},{6,7},{7,6},{8,9},{9,8},{10,11... | collective-permute-start | bytes 196616 | tf_op jit(solution)/shard_map/ppermute | solution.py:657
  17.5 5.9 %collective-permute-start.3 = (bf16[32,2048]{1,0:T(8,128)(2,1)S(1)}, bf16[32,2048]{1,0:T(8,128)(2,1)S(1)}, u32[]{:S(2)}, u32[]{:S(2)}) collective-permute-start(bf16[32,2048]{1,0:T(8,128)(2,1)S(1)} %constant_dynamic-update-slice_fusion.refs_1_), channel_id=1, source_target_pairs={{0,2},{1,3},{2,4},{3,5},{4,6},{5,7},{6,0},{7,1},{8,10},{9,11},{10,... | collective-permute-start | bytes 393224 | tf_op jit(solution)/shard_map/ppermute | solution.py:659
  18.7 4.7 %collective-permute-start.2 = (bf16[32,2048]{1,0:T(8,128)(2,1)S(1)}, bf16[32,2048]{1,0:T(8,128)(2,1)S(1)}, u32[]{:S(2)}, u32[]{:S(2)}) collective-permute-start(bf16[32,2048]{1,0:T(8,128)(2,1)S(1)} %constant_dynamic-update-slice_fusion.refs_1_), channel_id=1, source_target_pairs={{0,6},{1,7},{2,0},{3,1},{4,2},{5,3},{6,4},{7,5},{8,14},{9,15},{10,... | collective-permute-start | bytes 393224 | tf_op jit(solution)/shard_map/ppermute | solution.py:659
  20.2 7.1 %collective-permute-start.1 = (bf16[32,2048]{1,0:T(8,128)(2,1)S(1)}, bf16[32,2048]{1,0:T(8,128)(2,1)S(1)}, u32[]{:S(2)}, u32[]{:S(2)}) collective-permute-start(bf16[32,2048]{1,0:T(8,128)(2,1)S(1)} %constant_dynamic-update-slice_fusion.refs_1_), channel_id=1, source_target_pairs={{0,4},{1,5},{2,6},{3,7},{4,0},{5,1},{6,2},{7,3},{8,12},{9,13},{10,... | collective-permute-start | bytes 393224 | tf_op jit(solution)/shard_map/ppermute | solution.py:659
  31.6 8.3 %collective-permute-start.6 = (bf16[2,64,512]{2,1,0:T(8,128)(2,1)S(1)}, bf16[2,64,512]{2,1,0:T(8,128)(2,1)S(1)}, u32[]{:S(2)}, u32[]{:S(2)}) collective-permute-start(bf16[2,64,512]{2,1,0:T(8,128)(2,1)S(1)} %get-tuple-element.32), channel_id=1, source_target_pairs={{0,2},{1,3},{2,4},{3,5},{4,6},{5,7},{6,0},{7,1},{8,10},{9,11},{10,... | collective-permute-start | bytes 393224 | tf_op jit(solution)/shard_map/ppermute | solution.py:667
  32.9 7.0 %collective-permute-start.5 = (bf16[2,64,512]{2,1,0:T(8,128)(2,1)S(1)}, bf16[2,64,512]{2,1,0:T(8,128)(2,1)S(1)}, u32[]{:S(2)}, u32[]{:S(2)}) collective-permute-start(bf16[2,64,512]{2,1,0:T(8,128)(2,1)S(1)} %get-tuple-element.33), channel_id=1, source_target_pairs={{0,6},{1,7},{2,0},{3,1},{4,2},{5,3},{6,4},{7,5},{8,14},{9,15},{10,... | collective-permute-start | bytes 393224 | tf_op jit(solution)/shard_map/ppermute | solution.py:667
  34.4 5.9 %collective-permute-start.4 = (bf16[2,64,512]{2,1,0:T(8,128)(2,1)S(1)}, bf16[2,64,512]{2,1,0:T(8,128)(2,1)S(1)}, u32[]{:S(2)}, u32[]{:S(2)}) collective-permute-start(bf16[2,64,512]{2,1,0:T(8,128)(2,1)S(1)} %get-tuple-element.34), channel_id=1, source_target_pairs={{0,4},{1,5},{2,6},{3,7},{4,0},{5,1},{6,2},{7,3},{8,12},{9,13},{10,... | collective-permute-start | bytes 393224 | tf_op jit(solution)/shard_map/ppermute | solution.py:667
  40.3 5.0 %collective-permute-start.7 = (bf16[4,64,512]{2,1,0:T(8,128)(2,1)S(1)}, bf16[4,64,512]{2,1,0:T(8,128)(2,1)S(1)}, u32[]{:S(2)}, u32[]{:S(2)}) collective-permute-start(bf16[4,64,512]{2,1,0:T(8,128)(2,1)S(1)} %pack.1), channel_id=1, source_target_pairs={{0,1},{1,0},{2,3},{3,2},{4,5},{5,4},{6,7},{7,6},{8,9},{9,8},{10,11... | collective-permute-start | bytes 786440 | tf_op jit(solution)/shard_map/ppermute | solution.py:669
